TPU v7x, 32 devices: a whole 2x2x4 slice. The times are simulated.
32 devices in a mesh: arc: 4 (over x, core), col: 8 (over z, y).
Axes of the slice: x: 2, y: 2, z: 4, core: 2. Of those that a mesh axis runs over, the one named last changes fastest.
Arguments:
- partials: bfloat16 [2048, 4, 8192], P('arc', None, 'col'), may hold values from -0.0625 to 0.0625
- coef: bfloat16 [2048, 256], P('arc'), may hold values from -0.75 to 0.75
- arc_ids: int32 [2048], replicated, may hold values from 0 to 11, never falling along the last dimension, each value on 1 to 512 neighbouring positions
Outputs:
- normal: float32 [8192, 8192], P('col', 'arc')
Inputs may be any that keep to these rules, and one draw needn't show every extreme that they name: `arc_ids`: arc numbers never fall along the epochs; every arc holds 1 to 512 epochs and one holds exactly 512.
All inputs are finite; a program needn't handle non-finite values.
Results may differ from a plain program's by a relative error of at most 0.0024.
The roundings to bfloat16 on the way count: a program that leaves them out, or rounds other values in their place, can miss the bound.
Values may be sent and summed in bfloat16 or wider, within the bound.
No kernel may reach another device: no remote copies, remote signals or barrier semaphores. Data moves between devices by JAX's collectives and lax.ppermute only.
A program may use at most 128 MiB of HBM per device.

v0:
```python
import jax
import jax.numpy as jnp
from jax import lax
from jax.sharding import PartitionSpec as P

FBLK = 128


def from_behind(value, axis, steps):
    count = lax.axis_size(axis)
    first, last = (max(0, -steps), min(count, count - steps))
    return lax.ppermute(value, axis, [(source, source + steps) for source in range(first, last)])


def body(partials, coef, arc_ids):
    epochs_here, channels, width = partials.shape
    band = coef.shape[1]
    flat_rows = partials.reshape(epochs_here, channels * width)
    upper = from_behind(flat_rows[epochs_here - band :], "arc", 1)
    extended = jnp.concatenate([upper, flat_rows], 0)
    first = lax.axis_index("arc") * epochs_here
    ids_all = jnp.concatenate([jnp.full((band,), -1, jnp.int32), arc_ids])
    ids_ext = lax.dynamic_slice_in_dim(ids_all, first, epochs_here + band, 0)
    span = FBLK + band

    def one_block(block):
        start = block * FBLK
        window = lax.dynamic_slice_in_dim(extended, start, span, 0)
        ids_win = lax.dynamic_slice_in_dim(ids_ext, start, span, 0)
        ids_row = lax.dynamic_slice_in_dim(ids_ext, start + band, FBLK, 0)
        coef_blk = lax.dynamic_slice_in_dim(coef, start, FBLK, 0)
        leading = jnp.concatenate([coef_blk[:, ::-1], jnp.ones((FBLK, 1), coef.dtype)], 1)
        padded = jnp.concatenate([leading, jnp.zeros((FBLK, span - band), coef.dtype)], 1)
        skewed = padded.reshape(-1)[: FBLK * span].reshape(FBLK, span)
        same = ids_row[:, None] == ids_win[None, :]
        weight = jnp.where(same, skewed, jnp.zeros_like(skewed))
        return jnp.dot(weight, window, preferred_element_type=jnp.float32).astype(jnp.bfloat16)

    filtered = lax.map(one_block, jnp.arange(epochs_here // FBLK, dtype=jnp.int32))
    filtered = filtered.reshape(epochs_here * channels, width)
    term = lax.dot_general(
        filtered,
        lax.all_gather(filtered, "col", axis=1, tiled=True),
        (((0,), (0,)), ((), ())),
        preferred_element_type=jnp.float32,
    )
    return lax.psum_scatter(term, "arc", scatter_dimension=1, tiled=True)


def solution(mesh):
    return jax.shard_map(
        body,
        mesh=mesh,
        in_specs=(P("arc", None, "col"), P("arc", None), P()),
        out_specs=P("col", "arc"),
        check_vma=False,
    )
```

profile of v0, /device:TPU:0, one launch (start us, length us, event | category | flops | bytes accessed | tf_op | source)
XLA Modules:
  0.0 1002.2 jit_solution(1720651978206385220)
XLA Ops:
  6.5 1.6 slice-done
  8.1 2.2 copy.4
  10.3 2.5 collective-permute-start
  12.8 6.5 copy.5
  19.3 0.1 pad_dynamic-slice_fusion
  19.4 5.7 pad_maximum_fusion
  25.0 26.7 %while.12 = (s32[]{:T(128)}, bf16[4,128,4096]{2,1,0:T(8,128)(2,1)}, s32[4]{0:T(128)S(1)}, s32[768]{0:T(1024)S(1)}, bf16[512,256]{1,0:T(8,128)(2,1)}, /*index=5*/...) while((s32[]{:T(128)}, bf16[4,128,4096]{2,1,0:T(8,128)(2,1)}, ...), condition=%wide.region_1.2_spmd, body=%wide.region_0.1_spmd.sunk | while | flops 403571456 | bytes 5319234 | solution.py:39
  25.0 0.6 dynamic_slice.46
  26.3 0.1 dynamic_slice.48
  26.4 0.1 pad.3.clone.2
  26.4 0.1 dynamic_slice.47
  26.5 0.8 constant_dynamic-slice_fusion.2
  27.4 0.2 rev.7
  27.6 0.4 reshape.28
  28.0 0.1 reshape.29
  28.1 3.6 fusion.14
  31.7 0.6 dynamic_slice.46
  32.9 0.1 dynamic_slice.48
  33.0 0.1 pad.3.clone.2
  33.1 0.1 dynamic_slice.47
  33.2 0.8 constant_dynamic-slice_fusion.2
  34.0 0.2 rev.7
  34.3 0.4 reshape.28
  34.6 0.1 reshape.29
  34.7 3.7 fusion.14
  38.4 0.6 dynamic_slice.46
  39.6 0.1 dynamic_slice.48
  39.7 0.1 pad.3.clone.2
  39.8 0.1 dynamic_slice.47
  39.9 0.8 constant_dynamic-slice_fusion.2
  40.7 0.2 rev.7
  41.0 0.4 reshape.28
  41.3 0.1 reshape.29
  41.4 3.6 fusion.14
  45.0 0.6 dynamic_slice.46
  46.3 0.1 dynamic_slice.48
  46.4 0.1 pad.3.clone.2
  46.4 0.1 dynamic_slice.47
  46.5 0.8 constant_dynamic-slice_fusion.2
  47.4 0.2 rev.7
  47.6 0.4 reshape.28
  48.0 0.1 reshape.29
  48.1 3.6 fusion.14
  51.7 7.5 reshape.24
  59.2 0.0 reduce-scatter.2.cloned.1.call-start
  59.3 659.0 %all-gather.2.cloned.1.call-done = bf16[2048,8192]{1,0:T(8,128)(2,1)} async-done(((bf16[2048,1024]{1,0:T(8,128)(2,1)}), bf16[2048,8192]{1,0:T(8,128)(2,1)}) %all-gather.2.cloned.1.call-update) | async-done | bytes 33554448 | tf_op jit(solution)/shard_map/all_gather | solution.py:43
  718.3 42.1 %fusion.8 = f32[1024,8192]{1,0:T(8,128)} fusion(bf16[2048,1024]{1,0:T(8,128)(2,1)} %reshape.24, bf16[2048,8192]{1,0:T(8,128)(2,1)} %all-gather.2.cloned.1.call-done), kind=kOutput, calls=%fused_computation.14 | convolution fusion | flops 34359738368 | bytes 71303168 | tf_op jit(solution)/shard_map/dot_general | solution.py:41
  760.4 235.0 %reduce-scatter.2.cloned.1.call-done = f32[1024,2048]{1,0:T(8,128)} async-done(((f32[1024,8192]{1,0:T(8,128)}), f32[1024,2048]{1,0:T(8,128)}) %reduce-scatter.2.cloned.1.call-update) | async-done | bytes 8388624 | tf_op jit(solution)/shard_map/reduce_scatter | solution.py:47
  (25 shorter events, 0.2 us)
Async XLA Ops:
  6.5 1.6 slice-start
  6.5 711.8 %all-gather.2.cloned.1.call-start = ((), (), s32[]{:S(2)}) async-start(), calls=%async_computation.1 | async-start | bytes 37748736 | tf_op jit(solution)/shard_map/all_gather | solution.py:43
  10.3 9.1 collective-permute-start
  12.8 6.5 copy-start
  59.2 936.1 %reduce-scatter.2.cloned.1.call-start = ((), (), s32[]{:S(2)}) async-start(), calls=%async_computation.2 | async-start | bytes 41943040 | tf_op jit(solution)/shard_map/reduce_scatter | solution.py:47
Sparse Core Ops, SparseCore 0:
  59.4 658.9 all-gather.1
  760.6 234.7 reduce-scatter.1
where the time goes:
time: 1000 us
  waiting for transfers between devices  894 us (89%)
  matrix products  56.6 us (6%)
  local copies, waits for them, and re-layouts  27.1 us (3%)
  between operations  13.4 us (1%)
    all_gather x1, waiting for transfers between devices, body(): lax.all_gather(filtered, 'col', axis=1, tiled=True)  659 us
    reduce_scatter x1, waiting for transfers between devices, body(): return lax.psum_scatter(term, 'arc', scatter_dimension=1, tiled=True)  235 us
    dot_general x1, matrix products, body(): lax.dot_general(filtered, lax.all_gather(filtered, 'col', axis=1, tiled=T...  42.1 us
  transfers between devices with their start and end apart: 3, of which 2 were waited for; matrix products, arithmetic and copies ran while one was open for 1% of the time, Pallas kernels for 0%

commit v1 on v0

v1 whole, which is shorter than its diff:
```python
import functools

import jax
import jax.numpy as jnp
from jax import lax
from jax.experimental import pallas as pl
from jax.experimental.pallas import tpu as pltpu
from jax.sharding import PartitionSpec as P

PIECES = 4
AXES = ("arc", "col")
SPOTS = 4


def band_weights(coef, arc_ids, epochs_here):
    band = coef.shape[1]
    span = epochs_here + band
    start = lax.axis_index("arc") * epochs_here
    ids_all = jnp.concatenate([jnp.full((band,), -1, jnp.int32), arc_ids])
    ids_win = lax.dynamic_slice_in_dim(ids_all, start, span, 0)
    ids_row = lax.dynamic_slice_in_dim(arc_ids, start, epochs_here, 0)
    leading = jnp.concatenate([coef[:, ::-1], jnp.ones((epochs_here, 1), coef.dtype)], 1)
    padded = jnp.concatenate([leading, jnp.zeros((epochs_here, span - band), coef.dtype)], 1)
    skewed = padded.reshape(-1)[: epochs_here * span].reshape(epochs_here, span)
    return jnp.where(ids_row[:, None] == ids_win[None, :], skewed, jnp.zeros_like(skewed))


def window_of(partials, band):
    arcs = lax.axis_size("arc")
    behind = lax.ppermute(partials[partials.shape[0] - band :], "arc", [(a, a + 1) for a in range(arcs - 1)])
    return jnp.concatenate([behind, partials], 0)


def gathered_body(partials, coef, arc_ids):
    epochs_here, channels, width = partials.shape
    weight = band_weights(coef, arc_ids, epochs_here)
    window = window_of(partials, coef.shape[1])
    filtered = jnp.einsum("et,tcm->cem", weight, window, preferred_element_type=jnp.float32)
    filtered = filtered.astype(jnp.bfloat16).reshape(channels * epochs_here, width)
    term = lax.dot_general(
        filtered,
        lax.all_gather(filtered, "col", axis=1, tiled=True),
        (((0,), (0,)), ((), ())),
        preferred_element_type=jnp.float32,
    )
    return lax.psum_scatter(term, "arc", scatter_dimension=1, tiled=True)


def product_kernel(spot_ref, mine_left, other_left, *refs):
    sources = 2 * SPOTS - 1
    mine, other, out, acc = refs[:sources], refs[sources : 2 * sources], refs[2 * sources], refs[2 * sources + 1]
    step = pl.program_id(0)
    spot = spot_ref[0]

    @pl.when(step == 0)
    def _():
        acc[...] = jnp.zeros_like(acc)

    def pick(group, plane):
        taken = group[SPOTS - 1 + (0 - plane)][...]
        for z in range(1, SPOTS):
            taken = jnp.where(spot == z, group[SPOTS - 1 + z - plane][...], taken)
        return taken

    for plane in range(SPOTS):
        acc[plane] += jnp.dot(mine_left[...], pick(mine, plane), preferred_element_type=jnp.float32)
        acc[plane] += jnp.dot(other_left[...], pick(other, plane), preferred_element_type=jnp.float32)

    @pl.when(step == pl.num_programs(0) - 1)
    def _():
        out[...] = acc[...].astype(out.dtype)


def products(spot, mine_left, other_left, mine, other):
    rows, depth = mine_left.shape
    part = mine[0].shape[1]
    steps = 4
    left_spec = pl.BlockSpec((rows, depth // steps), lambda i, s: (0, i))
    right_spec = pl.BlockSpec((depth // steps, part), lambda i, s: (i, 0))
    return pl.pallas_call(
        product_kernel,
        out_shape=jax.ShapeDtypeStruct((SPOTS, rows, part), jnp.bfloat16),
        grid_spec=pltpu.PrefetchScalarGridSpec(
            num_scalar_prefetch=1,
            grid=(steps,),
            in_specs=[left_spec] * 2 + [right_spec] * (2 * len(mine)),
            out_specs=pl.BlockSpec((SPOTS, rows, part), lambda i, s: (0, 0, 0)),
            scratch_shapes=[pltpu.VMEM((SPOTS, rows, part), jnp.float32)],
        ),
        compiler_params=pltpu.CompilerParams(vmem_limit_bytes=48 << 20),
        cost_estimate=pl.CostEstimate(
            flops=4 * SPOTS * rows * depth * part,
            bytes_accessed=4 * rows * depth + 28 * depth * part + 2 * SPOTS * rows * part,
            transcendentals=0,
        ),
    )(spot, mine_left, other_left, *mine, *other)


def pairs(arcs, cols, target):
    found = []
    for half in range(arcs // 2):
        for core in range(2):
            for spot in range(cols // 2):
                for side in range(2):
                    place = target(half, core, spot, side)
                    if place is not None:
                        h, k, z, y = place
                        found.append(((2 * half + core) * cols + 2 * spot + side, (2 * h + k) * cols + 2 * z + y))
    return found


def line_body(partials, coef, arc_ids):
    epochs_here, channels, width = partials.shape
    arcs, cols = lax.axis_size("arc"), lax.axis_size("col")
    col = lax.axis_index("col")
    spot, side = col // 2, col % 2
    rows, part = epochs_here * channels, width // PIECES

    def send(value, target):
        return lax.ppermute(value, AXES, pairs(arcs, cols, target))

    weight = band_weights(coef, arc_ids, epochs_here)
    window = window_of(partials, coef.shape[1])
    own = []
    for piece in range(PIECES):
        taken = window[:, :, piece * part : (piece + 1) * part]
        filtered = jnp.einsum("et,tcm->cem", weight, taken, preferred_element_type=jnp.float32)
        own.append(filtered.astype(jnp.bfloat16).reshape(rows, part))
    left = jnp.einsum("et,tcm->mce", weight, window, preferred_element_type=jnp.float32)
    left = left.astype(jnp.bfloat16).reshape(width, rows)

    def hop(value, hops, step):
        def target(h, k, z, y):
            there, origin = z + step, z - step * (hops - 1)
            return (h, k, there, y) if 0 <= there < SPOTS and 0 <= origin < SPOTS else None

        return send(value, target)

    got = {}
    for piece in range(PIECES):
        got[piece, 0, 1] = got[piece, 0, -1] = own[piece]
    for turn in range(PIECES + SPOTS):
        for hops in range(1, SPOTS):
            piece = turn - (hops - 1)
            if 0 <= piece < PIECES:
                for step in (1, -1):
                    got[piece, hops, step] = hop(got[piece, hops - 1, step], hops, step)
    mine_left = send(left, lambda h, k, z, y: (h, k, z, y if k == 0 else 1 - y))
    other_left = send(left, lambda h, k, z, y: (h, 1 - k, z, y if k == 1 else 1 - y))

    near, far = [], []
    for piece in range(PIECES):
        mine = [got[piece, abs(d), 1 if d > 0 else -1] for d in range(1 - SPOTS, SPOTS)]
        other = [send(value, lambda h, k, z, y: (h, 1 - k, z, y)) for value in mine]
        terms = products(spot.reshape(1), mine_left, other_left, mine, other)
        came = lax.all_to_all(terms, "arc", split_axis=0, concat_axis=0, tiled=True)
        sums = came[:2].astype(jnp.float32) + came[2:].astype(jnp.float32)
        near.append(sums[0])
        far.append(send(sums[1].astype(jnp.bfloat16), lambda h, k, z, y: (h, k, z, 1 - y)).astype(jnp.float32))
    even = [jnp.where(side == 0, a, b) for a, b in zip(near, far)]
    odd = [jnp.where(side == 0, b, a) for a, b in zip(near, far)]
    return jnp.concatenate(even + odd, 1)


def solution(mesh):
    fits = mesh.shape["arc"] == SPOTS and mesh.shape["col"] == 2 * SPOTS
    return jax.shard_map(
        line_body if fits else gathered_body,
        mesh=mesh,
        in_specs=(P("arc", None, "col"), P("arc", None), P()),
        out_specs=P("col", "arc"),
        check_vma=False,
    )
```

time: 1000 us -> 495 us (0.49)
  waiting for transfers between devices: 894 us -> 229 us
  starting transfers between devices: 2.52 us -> 145 us
  Pallas kernels: 0 us -> 56.4 us
  matrix products: 56.6 us -> 18.4 us
  between operations: 13.4 us -> 0.65 us
    all_gather x1 -> x0, waiting for transfers between devices: 659 us -> none  [body(): lax.all_gather(filtered, 'col', axis=1, tiled=True)]
    reduce_scatter x1 -> x0, waiting for transfers between devices: 235 us -> none  [body(): return lax.psum_scatter(term, 'arc', scatter_dimension=1, tiled=True)]
    ppermute x1 -> x59, waiting for transfers between devices: 0.01 us -> 188 us  [the longest x58 188 us: send(): return lax.ppermute(value, AXES, pairs(arcs, cols, target))]
    ppermute x1 -> x59, starting transfers between devices: 2.48 us -> 127 us  [the longest x58 123 us: send(): return lax.ppermute(value, AXES, pairs(arcs, cols, target))]
    pallas_call x0 -> x4, Pallas kernels: none -> 56.4 us  [products(): pl.pallas_call(product_kernel, out_shape=jax.ShapeDtypeStruct((SPOTS, row...]
    all_to_all x0 -> x4, waiting for transfers between devices: none -> 41.6 us  [line_body(): came = lax.all_to_all(terms, 'arc', split_axis=0, concat_axis=0, tiled=True)]
    dot_general x5, matrix products: 56.6 us -> 18.4 us  [the longest x4 9.89 us: line_body(): jnp.einsum('et,tcm->cem', weight, taken, preferred_element_type=jnp.float32)]
    all_to_all x0 -> x4, starting transfers between devices: none -> 17.9 us  [line_body(): came = lax.all_to_all(terms, 'arc', split_axis=0, concat_axis=0, tiled=True)]
  transfers between devices with their start and end apart: 3 -> 63, of which waited for: 2 -> 19; matrix products, arithmetic and copies ran while one was open for 1% -> 8% of each run, Pallas kernels for 0% -> 11%
where the time goes in v1:
time: 495 us; the launch traced here: 492 us
  waiting for transfers between devices  229 us (46%)
  starting transfers between devices  145 us (29%)
  Pallas kernels  56.4 us (11%)
  local copies, waits for them, and re-layouts  32 us (6%)
  matrix products  18.4 us (4%)
  other arithmetic  10.1 us (2%)
    ppermute x58, waiting for transfers between devices, send(): return lax.ppermute(value, AXES, pairs(arcs, cols, target))  188 us
    ppermute x58, starting transfers between devices, send(): return lax.ppermute(value, AXES, pairs(arcs, cols, target))  123 us
    pallas_call x4, Pallas kernels, products(): pl.pallas_call(product_kernel, out_shape=jax.ShapeDtypeStruct((SPOTS, row...  56.4 us
    all_to_all x4, waiting for transfers between devices, line_body(): came = lax.all_to_all(terms, 'arc', split_axis=0, concat_axis=0, tiled=True)  41.6 us
    all_to_all x4, starting transfers between devices, line_body(): came = lax.all_to_all(terms, 'arc', split_axis=0, concat_axis=0, tiled=True)  17.9 us
    unnamed x32, local copies, waits for them, and re-layouts  12.9 us
  transfers between devices with their start and end apart: 63, of which 19 were waited for; matrix products, arithmetic and copies ran while one was open for 8% of the time, Pallas kernels for 11%

profile of v1, /device:TPU:0, one launch (start us, length us, event | category | flops | bytes accessed | tf_op | source)
XLA Modules:
  0.0 491.7 jit_solution(15628981753273581244)
XLA Ops:
  1.6 1.9 copy.32
  3.5 3.7 collective-permute-start
  10.5 1.9 constant_dynamic-update-slice_fusion.1
  14.8 2.7 copy-done.8
  21.3 5.9 %collective-permute-start.48 = (bf16[2048,256]{1,0:T(8,128)(2,1)}, bf16[2048,256]{1,0:T(8,128)(2,1)}, u32[]{:S(2)}, u32[]{:S(2)}) collective-permute-start(bf16[2048,256]{1,0:T(8,128)(2,1)} %bitcast.18.refs_3_), channel_id=1, source_target_pairs={{0,2},{1,3},{2,4},{3,5},{4,6},{5,7},{8,10},{9,11},{10,12},{11,13},... | collective-permute-start | bytes 3145736 | tf_op jit(solution)/shard_map/ppermute | solution.py:120
  27.2 19.1 %collective-permute-start.54 = (bf16[2048,256]{1,0:T(8,128)(2,1)}, bf16[2048,256]{1,0:T(8,128)(2,1)}, u32[]{:S(2)}, u32[]{:S(2)}) collective-permute-start(bf16[2048,256]{1,0:T(8,128)(2,1)} %bitcast.18.refs_3_), channel_id=1, source_target_pairs={{0,8},{1,9},{2,10},{3,11},{4,12},{5,13},{6,14},{7,15},{8,0},{9,1},... | collective-permute-start | bytes 3145736 | tf_op jit(solution)/shard_map/ppermute | solution.py:120
  46.3 2.5 fusion.23
  50.7 5.5 %collective-permute-start.34 = (bf16[2048,256]{1,0:T(8,128)(2,1)S(1)}, bf16[2048,256]{1,0:T(8,128)(2,1)}, u32[]{:S(2)}, u32[]{:S(2)}) collective-permute-start(bf16[2048,256]{1,0:T(8,128)(2,1)S(1)} %bitcast.58), channel_id=1, source_target_pairs={{0,2},{1,3},{2,4},{3,5},{4,6},{5,7},{8,10},{9,11},{10,12},{11,13},... | collective-permute-start | bytes 3145736 | tf_op jit(solution)/shard_map/ppermute | solution.py:120
  56.2 2.5 fusion.26
  59.2 3.7 fusion.29
  65.9 5.6 %collective-permute-start.20 = (bf16[2048,256]{1,0:T(8,128)(2,1)S(1)}, bf16[2048,256]{1,0:T(8,128)(2,1)}, u32[]{:S(2)}, u32[]{:S(2)}) collective-permute-start(bf16[2048,256]{1,0:T(8,128)(2,1)S(1)} %bitcast.66), channel_id=1, source_target_pairs={{0,2},{1,3},{2,4},{3,5},{4,6},{5,7},{8,10},{9,11},{10,12},{11,13},... | collective-permute-start | bytes 3145736 | tf_op jit(solution)/shard_map/ppermute | solution.py:120
  71.5 6.0 %collective-permute-done.31.refs_2_ = bf16[2048,256]{1,0:T(8,128)(2,1)} collective-permute-done((bf16[2048,256]{1,0:T(8,128)(2,1)S(1)}, bf16[2048,256]{1,0:T(8,128)(2,1)}, u32[]{:S(2)}, u32[]{:S(2)}) %collective-permute-start.31) | collective-permute-done | bytes 1048608 | tf_op jit(solution)/shard_map/ppermute | solution.py:120
  77.5 2.3 collective-permute-start.26
  79.8 4.9 collective-permute-start.6
  85.9 14.0 %collective-permute-done.17.refs_2_ = bf16[2048,256]{1,0:T(8,128)(2,1)} collective-permute-done((bf16[2048,256]{1,0:T(8,128)(2,1)S(1)}, bf16[2048,256]{1,0:T(8,128)(2,1)}, u32[]{:S(2)}, u32[]{:S(2)}) %collective-permute-start.17) | collective-permute-done | bytes 1048608 | tf_op jit(solution)/shard_map/ppermute | solution.py:120
  99.9 2.3 collective-permute-start.12
  105.2 18.6 %collective-permute-done.6.refs_4_ = bf16[2048,256]{1,0:T(8,128)(2,1)} collective-permute-done((bf16[2048,256]{1,0:T(8,128)(2,1)S(1)}, bf16[2048,256]{1,0:T(8,128)(2,1)}, u32[]{:S(2)}, u32[]{:S(2)}) %collective-permute-start.6) | collective-permute-done | bytes 1048608 | tf_op jit(solution)/shard_map/ppermute | solution.py:120
  126.0 18.8 %collective-permute-done.46.refs_1_ = bf16[2048,256]{1,0:T(8,128)(2,1)} collective-permute-done((bf16[2048,256]{1,0:T(8,128)(2,1)}, bf16[2048,256]{1,0:T(8,128)(2,1)}, u32[]{:S(2)}, u32[]{:S(2)}) %collective-permute-start.46) | collective-permute-done | bytes 1048608 | tf_op jit(solution)/shard_map/ppermute | solution.py:120
  146.5 2.3 collective-permute-start.39
  151.8 15.5 %collective-permute-done.32.refs_1_ = bf16[2048,256]{1,0:T(8,128)(2,1)} collective-permute-done((bf16[2048,256]{1,0:T(8,128)(2,1)}, bf16[2048,256]{1,0:T(8,128)(2,1)}, u32[]{:S(2)}, u32[]{:S(2)}) %collective-permute-start.32) | collective-permute-done | bytes 1048608 | tf_op jit(solution)/shard_map/ppermute | solution.py:120
  167.3 2.3 collective-permute-start.25
  171.3 18.5 %collective-permute-done.18.refs_1_ = bf16[2048,256]{1,0:T(8,128)(2,1)} collective-permute-done((bf16[2048,256]{1,0:T(8,128)(2,1)}, bf16[2048,256]{1,0:T(8,128)(2,1)}, u32[]{:S(2)}, u32[]{:S(2)}) %collective-permute-start.18) | collective-permute-done | bytes 1048608 | tf_op jit(solution)/shard_map/ppermute | solution.py:120
  191.3 8.5 %convolution_convert_fusion = bf16[4,1024,512]{1,2,0:T(8,128)(2,1)} fusion(bf16[768,4,1024]{2,0,1:T(8,128)(2,1)} %copy-done.8, bf16[512,768]{1,0:T(8,128)(2,1)} %copy-done.7, s32[768]{0:T(1024)S(1)} %pad_dynamic-slice_fusion, s32[512]{0:T(512)S(1)} %dynamic_slice.6), kind=kOutput, calls=%fused_computation | convolution fusion | flops 3224109056 | bytes 11277312 | tf_op jit(solution)/shard_map/et,tcm->mce/dot_general | solution.py:129
  199.8 6.4 %copy.30 = bf16[1024,2048]{1,0:T(8,128)(2,1)} copy(bf16[1024,2048]{0,1:T(8,128)(2,1)} %bitcast.69) | data formatting | bytes 8388608 | tf_op jit(solution)/shard_map/reshape | solution.py:130
  207.1 32.9 %collective-permute-start.1 = (bf16[1024,2048]{1,0:T(8,128)(2,1)}, bf16[1024,2048]{1,0:T(8,128)(2,1)}, u32[]{:S(2)}, u32[]{:S(2)}) collective-permute-start(bf16[1024,2048]{1,0:T(8,128)(2,1)} %copy.30), channel_id=1, source_target_pairs={{0,0},{1,1},{2,2},{3,3},{4,4},{5,5},{6,6},{7,7},{8,9},{9,8},{10,11... | collective-permute-start | bytes 12582920 | tf_op jit(solution)/shard_map/ppermute | solution.py:120
  243.5 5.5 %collective-permute-done.13.refs_11_ = bf16[2048,256]{1,0:T(8,128)(2,1)} collective-permute-done((bf16[2048,256]{1,0:T(8,128)(2,1)}, bf16[2048,256]{1,0:T(8,128)(2,1)}, u32[]{:S(2)}, u32[]{:S(2)}) %collective-permute-start.13) | collective-permute-done | bytes 1048608 | tf_op jit(solution)/shard_map/ppermute | solution.py:120
  249.1 18.7 %collective-permute-done.47.refs_0_ = bf16[2048,256]{1,0:T(8,128)(2,1)} collective-permute-done((bf16[2048,256]{1,0:T(8,128)(2,1)}, bf16[2048,256]{1,0:T(8,128)(2,1)}, u32[]{:S(2)}, u32[]{:S(2)}) %collective-permute-start.47) | collective-permute-done | bytes 1048608 | tf_op jit(solution)/shard_map/ppermute | solution.py:120
  272.6 23.5 %collective-permute-done.33.refs_0_ = bf16[2048,256]{1,0:T(8,128)(2,1)} collective-permute-done((bf16[2048,256]{1,0:T(8,128)(2,1)}, bf16[2048,256]{1,0:T(8,128)(2,1)}, u32[]{:S(2)}, u32[]{:S(2)}) %collective-permute-start.33) | collective-permute-done | bytes 1048608 | tf_op jit(solution)/shard_map/ppermute | solution.py:120
  296.0 22.1 %collective-permute-done.19.refs_0_ = bf16[2048,256]{1,0:T(8,128)(2,1)} collective-permute-done((bf16[2048,256]{1,0:T(8,128)(2,1)}, bf16[2048,256]{1,0:T(8,128)(2,1)}, u32[]{:S(2)}, u32[]{:S(2)}) %collective-permute-start.19) | collective-permute-done | bytes 1048608 | tf_op jit(solution)/shard_map/ppermute | solution.py:120
  322.7 14.2 %shard_map.40 = bf16[4,1024,256]{2,1,0:T(8,128)(2,1)} custom-call(s32[1]{0:T(128)} %bitcast.spot_ref, bf16[1024,2048]{1,0:T(8,128)(2,1)} %collective-permute-done.1.mine_left, bf16[1024,2048]{1,0:T(8,128)(2,1)} %collective-permute-done.2.other_left, bf16[2048,256]{1,0:T(8,128)(2,1)} %collective-permute-done.47.refs_0_, ...), custom_call_target="tpu_custom_call" | custom-call | flops 8589934592 | bytes 25165824 | tf_op jit(solution)/shard_map/pallas_call | solution.py:80
  336.9 5.1 %all-to-all-start.3 = ((bf16[4,1024,256]{2,1,0:T(8,128)(2,1)}), bf16[4,1024,256]{2,1,0:T(8,128)(2,1)}, u32[]{:S(2)}, u32[]{:S(2)}) async-start(bf16[4,1024,256]{2,1,0:T(8,128)(2,1)} %shard_map.40), calls=%async_computation.3 | async-start | bytes 4194304 | tf_op jit(solution)/shard_map/all_to_all | solution.py:156
  342.6 5.5 %collective-permute-done.5.refs_0_ = bf16[2048,256]{1,0:T(8,128)(2,1)} collective-permute-done((bf16[2048,256]{1,0:T(8,128)(2,1)}, bf16[2048,256]{1,0:T(8,128)(2,1)}, u32[]{:S(2)}, u32[]{:S(2)}) %collective-permute-start.5) | collective-permute-done | bytes 1048608 | tf_op jit(solution)/shard_map/ppermute | solution.py:120
  350.3 14.0 %shard_map.38 = bf16[4,1024,256]{2,1,0:T(8,128)(2,1)} custom-call(s32[1]{0:T(128)} %bitcast.spot_ref, bf16[1024,2048]{1,0:T(8,128)(2,1)} %collective-permute-done.1.mine_left, bf16[1024,2048]{1,0:T(8,128)(2,1)} %collective-permute-done.2.other_left, bf16[2048,256]{1,0:T(8,128)(2,1)} %collective-permute-done.19.refs_0_, ...), custom_call_target="tpu_custom_call" | custom-call | flops 8589934592 | bytes 25165824 | tf_op jit(solution)/shard_map/pallas_call | solution.py:80
  364.3 4.9 all-to-all-done.3
  369.2 4.7 all-to-all-start.1
  375.1 14.1 %shard_map.37 = bf16[4,1024,256]{2,1,0:T(8,128)(2,1)} custom-call(s32[1]{0:T(128)} %bitcast.spot_ref, bf16[1024,2048]{1,0:T(8,128)(2,1)} %collective-permute-done.1.mine_left, bf16[1024,2048]{1,0:T(8,128)(2,1)} %collective-permute-done.2.other_left, bf16[2048,256]{1,0:T(8,128)(2,1)} %collective-permute-done.5.refs_0_, ...), custom_call_target="tpu_custom_call" | custom-call | flops 8589934592 | bytes 25165824 | tf_op jit(solution)/shard_map/pallas_call | solution.py:80
  389.2 10.2 %all-to-all-done.1 = bf16[4,1024,256]{2,1,0:T(8,128)(2,1)} async-done(((bf16[4,1024,256]{2,1,0:T(8,128)(2,1)}), bf16[4,1024,256]{2,1,0:T(8,128)(2,1)}, u32[]{:S(2)}, u32[]{:S(2)}) %all-to-all-start.1) | async-done | bytes 2097184 | tf_op jit(solution)/shard_map/all_to_all | solution.py:156
  399.4 3.6 all-to-all-start
  403.1 14.1 %shard_map.39 = bf16[4,1024,256]{2,1,0:T(8,128)(2,1)} custom-call(s32[1]{0:T(128)} %bitcast.spot_ref, bf16[1024,2048]{1,0:T(8,128)(2,1)} %collective-permute-done.1.mine_left, bf16[1024,2048]{1,0:T(8,128)(2,1)} %collective-permute-done.2.other_left, bf16[2048,256]{1,0:T(8,128)(2,1)} %collective-permute-done.33.refs_0_, ...), custom_call_target="tpu_custom_call" | custom-call | flops 8589934592 | bytes 25165824 | tf_op jit(solution)/shard_map/pallas_call | solution.py:80
  417.2 11.5 %all-to-all-done = bf16[4,1024,256]{2,1,0:T(8,128)(2,1)S(1)} async-done(((bf16[4,1024,256]{2,1,0:T(8,128)(2,1)}), bf16[4,1024,256]{2,1,0:T(8,128)(2,1)S(1)}, u32[]{:S(2)}, u32[]{:S(2)}) %all-to-all-start) | async-done | bytes 2097184 | tf_op jit(solution)/shard_map/all_to_all | solution.py:156
  430.0 4.5 all-to-all-start.2
  434.5 1.8 convert_add_fusion
  438.6 1.8 convert_add_fusion.2
  445.1 15.1 %all-to-all-done.2 = bf16[4,1024,256]{2,1,0:T(8,128)(2,1)} async-done(((bf16[4,1024,256]{2,1,0:T(8,128)(2,1)}), bf16[4,1024,256]{2,1,0:T(8,128)(2,1)}, u32[]{:S(2)}, u32[]{:S(2)}) %all-to-all-start.2) | async-done | bytes 2097184 | tf_op jit(solution)/shard_map/all_to_all | solution.py:156
  460.2 1.9 convert_add_fusion.1
  463.8 10.8 %collective-permute-done.16 = bf16[1024,256]{1,0:T(8,128)(2,1)} collective-permute-done((bf16[1024,256]{1,0:T(8,128)(2,1)}, bf16[1024,256]{1,0:T(8,128)(2,1)}, u32[]{:S(2)}, u32[]{:S(2)}) %collective-permute-start.16) | collective-permute-done | bytes 524320 | tf_op jit(solution)/shard_map/ppermute | solution.py:120
  476.0 9.3 %collective-permute-done.44 = bf16[1024,256]{1,0:T(8,128)(2,1)S(1)} collective-permute-done((bf16[1024,256]{1,0:T(8,128)(2,1)S(1)}, bf16[1024,256]{1,0:T(8,128)(2,1)S(1)}, u32[]{:S(2)}, u32[]{:S(2)}) %collective-permute-start.44) | collective-permute-done | bytes 524320 | tf_op jit(solution)/shard_map/ppermute | solution.py:120
  487.2 3.4 copy-done.10
  (153 shorter events, 62.5 us)
Async XLA Ops:
  20.0 44.5 %collective-permute-start.45 = (bf16[2048,256]{1,0:T(8,128)(2,1)}, bf16[2048,256]{1,0:T(8,128)(2,1)}, u32[]{:S(2)}, u32[]{:S(2)}) collective-permute-start(bf16[2048,256]{1,0:T(8,128)(2,1)} %bitcast.18.refs_3_), channel_id=1, source_target_pairs={{2,0},{3,1},{4,2},{5,3},{6,4},{7,5},{10,8},{11,9},{12,10},{13,11},... | collective-permute-start | bytes 3145736 | tf_op jit(solution)/shard_map/ppermute | solution.py:120
  21.3 43.3 %collective-permute-start.48 = (bf16[2048,256]{1,0:T(8,128)(2,1)}, bf16[2048,256]{1,0:T(8,128)(2,1)}, u32[]{:S(2)}, u32[]{:S(2)}) collective-permute-start(bf16[2048,256]{1,0:T(8,128)(2,1)} %bitcast.18.refs_3_), channel_id=1, source_target_pairs={{0,2},{1,3},{2,4},{3,5},{4,6},{5,7},{8,10},{9,11},{10,12},{11,13},... | collective-permute-start | bytes 3145736 | tf_op jit(solution)/shard_map/ppermute | solution.py:120
  27.2 38.7 %collective-permute-start.54 = (bf16[2048,256]{1,0:T(8,128)(2,1)}, bf16[2048,256]{1,0:T(8,128)(2,1)}, u32[]{:S(2)}, u32[]{:S(2)}) collective-permute-start(bf16[2048,256]{1,0:T(8,128)(2,1)} %bitcast.18.refs_3_), channel_id=1, source_target_pairs={{0,8},{1,9},{2,10},{3,11},{4,12},{5,13},{6,14},{7,15},{8,0},{9,1},... | collective-permute-start | bytes 3145736 | tf_op jit(solution)/shard_map/ppermute | solution.py:120
  49.4 28.1 %collective-permute-start.31 = (bf16[2048,256]{1,0:T(8,128)(2,1)S(1)}, bf16[2048,256]{1,0:T(8,128)(2,1)}, u32[]{:S(2)}, u32[]{:S(2)}) collective-permute-start(bf16[2048,256]{1,0:T(8,128)(2,1)S(1)} %bitcast.57), channel_id=1, source_target_pairs={{2,0},{3,1},{4,2},{5,3},{6,4},{7,5},{10,8},{11,9},{12,10},{13,11},... | collective-permute-start | bytes 3145736 | tf_op jit(solution)/shard_map/ppermute | solution.py:120
  50.7 29.1 %collective-permute-start.34 = (bf16[2048,256]{1,0:T(8,128)(2,1)S(1)}, bf16[2048,256]{1,0:T(8,128)(2,1)}, u32[]{:S(2)}, u32[]{:S(2)}) collective-permute-start(bf16[2048,256]{1,0:T(8,128)(2,1)S(1)} %bitcast.58), channel_id=1, source_target_pairs={{0,2},{1,3},{2,4},{3,5},{4,6},{5,7},{8,10},{9,11},{10,12},{11,13},... | collective-permute-start | bytes 3145736 | tf_op jit(solution)/shard_map/ppermute | solution.py:120
  64.6 35.3 %collective-permute-start.17 = (bf16[2048,256]{1,0:T(8,128)(2,1)S(1)}, bf16[2048,256]{1,0:T(8,128)(2,1)}, u32[]{:S(2)}, u32[]{:S(2)}) collective-permute-start(bf16[2048,256]{1,0:T(8,128)(2,1)S(1)} %bitcast.65), channel_id=1, source_target_pairs={{2,0},{3,1},{4,2},{5,3},{6,4},{7,5},{10,8},{11,9},{12,10},{13,11},... | collective-permute-start | bytes 3145736 | tf_op jit(solution)/shard_map/ppermute | solution.py:120
  65.9 36.3 %collective-permute-start.20 = (bf16[2048,256]{1,0:T(8,128)(2,1)S(1)}, bf16[2048,256]{1,0:T(8,128)(2,1)}, u32[]{:S(2)}, u32[]{:S(2)}) collective-permute-start(bf16[2048,256]{1,0:T(8,128)(2,1)S(1)} %bitcast.66), channel_id=1, source_target_pairs={{0,2},{1,3},{2,4},{3,5},{4,6},{5,7},{8,10},{9,11},{10,12},{11,13},... | collective-permute-start | bytes 3145736 | tf_op jit(solution)/shard_map/ppermute | solution.py:120
  77.5 26.1 %collective-permute-start.26 = (bf16[2048,256]{1,0:T(8,128)(2,1)S(1)}, bf16[2048,256]{1,0:T(8,128)(2,1)S(1)}, u32[]{:S(2)}, u32[]{:S(2)}) collective-permute-start(bf16[2048,256]{1,0:T(8,128)(2,1)S(1)} %bitcast.67), channel_id=1, source_target_pairs={{0,8},{1,9},{2,10},{3,11},{4,12},{5,13},{6,14},{7,15},{8,0},{9,1},... | collective-permute-start | bytes 3145736 | tf_op jit(solution)/shard_map/ppermute | solution.py:120
  79.8 44.0 %collective-permute-start.6 = (bf16[2048,256]{1,0:T(8,128)(2,1)S(1)}, bf16[2048,256]{1,0:T(8,128)(2,1)}, u32[]{:S(2)}, u32[]{:S(2)}) collective-permute-start(bf16[2048,256]{1,0:T(8,128)(2,1)S(1)} %bitcast.61), channel_id=1, source_target_pairs={{0,2},{1,3},{2,4},{3,5},{4,6},{5,7},{8,10},{9,11},{10,12},{11,13},... | collective-permute-start | bytes 3145736 | tf_op jit(solution)/shard_map/ppermute | solution.py:120
  84.6 40.1 %collective-permute-start.3 = (bf16[2048,256]{1,0:T(8,128)(2,1)S(1)}, bf16[2048,256]{1,0:T(8,128)(2,1)}, u32[]{:S(2)}, u32[]{:S(2)}) collective-permute-start(bf16[2048,256]{1,0:T(8,128)(2,1)S(1)} %bitcast.62), channel_id=1, source_target_pairs={{2,0},{3,1},{4,2},{5,3},{6,4},{7,5},{10,8},{11,9},{12,10},{13,11},... | collective-permute-start | bytes 3145736 | tf_op jit(solution)/shard_map/ppermute | solution.py:120
  102.2 42.6 %collective-permute-start.46 = (bf16[2048,256]{1,0:T(8,128)(2,1)}, bf16[2048,256]{1,0:T(8,128)(2,1)}, u32[]{:S(2)}, u32[]{:S(2)}) collective-permute-start(bf16[2048,256]{1,0:T(8,128)(2,1)} %collective-permute-done.45.refs_2_), channel_id=1, source_target_pairs={{2,0},{3,1},{4,2},{5,3},{10,8},{11,9},{12,10},{13,11},{18,16},{19,... | collective-permute-start | bytes 3145736 | tf_op jit(solution)/shard_map/ppermute | solution.py:120
  103.5 43.0 %collective-permute-start.49 = (bf16[2048,256]{1,0:T(8,128)(2,1)}, bf16[2048,256]{1,0:T(8,128)(2,1)}, u32[]{:S(2)}, u32[]{:S(2)}) collective-permute-start(bf16[2048,256]{1,0:T(8,128)(2,1)} %collective-permute-done.48.refs_4_), channel_id=1, source_target_pairs={{2,4},{3,5},{4,6},{5,7},{10,12},{11,13},{12,14},{13,15},{18,20},{1... | collective-permute-start | bytes 3145736 | tf_op jit(solution)/shard_map/ppermute | solution.py:120
  123.8 25.1 %collective-permute-start.53 = (bf16[2048,256]{1,0:T(8,128)(2,1)}, bf16[2048,256]{1,0:T(8,128)(2,1)}, u32[]{:S(2)}, u32[]{:S(2)}) collective-permute-start(bf16[2048,256]{1,0:T(8,128)(2,1)} %collective-permute-done.45.refs_2_), channel_id=1, source_target_pairs={{0,8},{1,9},{2,10},{3,11},{4,12},{5,13},{6,14},{7,15},{8,0},{9,1},... | collective-permute-start | bytes 3145736 | tf_op jit(solution)/shard_map/ppermute | solution.py:120
  124.7 25.4 %collective-permute-start.55 = (bf16[2048,256]{1,0:T(8,128)(2,1)}, bf16[2048,256]{1,0:T(8,128)(2,1)}, u32[]{:S(2)}, u32[]{:S(2)}) collective-permute-start(bf16[2048,256]{1,0:T(8,128)(2,1)} %collective-permute-done.48.refs_4_), channel_id=1, source_target_pairs={{0,8},{1,9},{2,10},{3,11},{4,12},{5,13},{6,14},{7,15},{8,0},{9,1},... | collective-permute-start | bytes 3145736 | tf_op jit(solution)/shard_map/ppermute | solution.py:120
  124.7 42.6 %collective-permute-start.32 = (bf16[2048,256]{1,0:T(8,128)(2,1)}, bf16[2048,256]{1,0:T(8,128)(2,1)}, u32[]{:S(2)}, u32[]{:S(2)}) collective-permute-start(bf16[2048,256]{1,0:T(8,128)(2,1)} %collective-permute-done.31.refs_2_), channel_id=1, source_target_pairs={{2,0},{3,1},{4,2},{5,3},{10,8},{11,9},{12,10},{13,11},{18,16},{19,... | collective-permute-start | bytes 3145736 | tf_op jit(solution)/shard_map/ppermute | solution.py:120
  148.8 41.0 %collective-permute-start.18 = (bf16[2048,256]{1,0:T(8,128)(2,1)}, bf16[2048,256]{1,0:T(8,128)(2,1)}, u32[]{:S(2)}, u32[]{:S(2)}) collective-permute-start(bf16[2048,256]{1,0:T(8,128)(2,1)} %collective-permute-done.17.refs_2_), channel_id=1, source_target_pairs={{2,0},{3,1},{4,2},{5,3},{10,8},{11,9},{12,10},{13,11},{18,16},{19,... | collective-permute-start | bytes 3145736 | tf_op jit(solution)/shard_map/ppermute | solution.py:120
  150.1 56.1 %collective-permute-start.21 = (bf16[2048,256]{1,0:T(8,128)(2,1)}, bf16[2048,256]{1,0:T(8,128)(2,1)}, u32[]{:S(2)}, u32[]{:S(2)}) collective-permute-start(bf16[2048,256]{1,0:T(8,128)(2,1)} %collective-permute-done.20.refs_4_), channel_id=1, source_target_pairs={{2,4},{3,5},{4,6},{5,7},{10,12},{11,13},{12,14},{13,15},{18,20},{1... | collective-permute-start | bytes 3145736 | tf_op jit(solution)/shard_map/ppermute | solution.py:120
  167.3 39.8 %collective-permute-start.25 = (bf16[2048,256]{1,0:T(8,128)(2,1)}, bf16[2048,256]{1,0:T(8,128)(2,1)}, u32[]{:S(2)}, u32[]{:S(2)}) collective-permute-start(bf16[2048,256]{1,0:T(8,128)(2,1)} %collective-permute-done.17.refs_2_), channel_id=1, source_target_pairs={{0,8},{1,9},{2,10},{3,11},{4,12},{5,13},{6,14},{7,15},{8,0},{9,1},... | collective-permute-start | bytes 3145736 | tf_op jit(solution)/shard_map/ppermute | solution.py:120
  169.6 70.4 %collective-permute-start.27 = (bf16[2048,256]{1,0:T(8,128)(2,1)}, bf16[2048,256]{1,0:T(8,128)(2,1)}, u32[]{:S(2)}, u32[]{:S(2)}) collective-permute-start(bf16[2048,256]{1,0:T(8,128)(2,1)} %collective-permute-done.20.refs_4_), channel_id=1, source_target_pairs={{0,8},{1,9},{2,10},{3,11},{4,12},{5,13},{6,14},{7,15},{8,0},{9,1},... | collective-permute-start | bytes 3145736 | tf_op jit(solution)/shard_map/ppermute | solution.py:120
  169.7 70.4 %collective-permute-start.7 = (bf16[2048,256]{1,0:T(8,128)(2,1)}, bf16[2048,256]{1,0:T(8,128)(2,1)}, u32[]{:S(2)}, u32[]{:S(2)}) collective-permute-start(bf16[2048,256]{1,0:T(8,128)(2,1)} %collective-permute-done.6.refs_4_), channel_id=1, source_target_pairs={{2,4},{3,5},{4,6},{5,7},{10,12},{11,13},{12,14},{13,15},{18,20},{1... | collective-permute-start | bytes 3145736 | tf_op jit(solution)/shard_map/ppermute | solution.py:120
  189.8 50.7 %collective-permute-start.4 = (bf16[2048,256]{1,0:T(8,128)(2,1)}, bf16[2048,256]{1,0:T(8,128)(2,1)}, u32[]{:S(2)}, u32[]{:S(2)}) collective-permute-start(bf16[2048,256]{1,0:T(8,128)(2,1)} %collective-permute-done.3.refs_2_), channel_id=1, source_target_pairs={{2,0},{3,1},{4,2},{5,3},{10,8},{11,9},{12,10},{13,11},{18,16},{19,... | collective-permute-start | bytes 3145736 | tf_op jit(solution)/shard_map/ppermute | solution.py:120
  206.2 35.6 %collective-permute-start.11 = (bf16[2048,256]{1,0:T(8,128)(2,1)}, bf16[2048,256]{1,0:T(8,128)(2,1)}, u32[]{:S(2)}, u32[]{:S(2)}) collective-permute-start(bf16[2048,256]{1,0:T(8,128)(2,1)} %collective-permute-done.3.refs_2_), channel_id=1, source_target_pairs={{0,8},{1,9},{2,10},{3,11},{4,12},{5,13},{6,14},{7,15},{8,0},{9,1},... | collective-permute-start | bytes 3145736 | tf_op jit(solution)/shard_map/ppermute | solution.py:120
  207.1 111.6 %collective-permute-start.1 = (bf16[1024,2048]{1,0:T(8,128)(2,1)}, bf16[1024,2048]{1,0:T(8,128)(2,1)}, u32[]{:S(2)}, u32[]{:S(2)}) collective-permute-start(bf16[1024,2048]{1,0:T(8,128)(2,1)} %copy.30), channel_id=1, source_target_pairs={{0,0},{1,1},{2,2},{3,3},{4,4},{5,5},{6,6},{7,7},{8,9},{9,8},{10,11... | collective-permute-start | bytes 12582920 | tf_op jit(solution)/shard_map/ppermute | solution.py:120
  240.0 80.4 %collective-permute-start.2 = (bf16[1024,2048]{1,0:T(8,128)(2,1)}, bf16[1024,2048]{1,0:T(8,128)(2,1)}, u32[]{:S(2)}, u32[]{:S(2)}) collective-permute-start(bf16[1024,2048]{1,0:T(8,128)(2,1)} %copy.30), channel_id=1, source_target_pairs={{0,9},{1,8},{2,11},{3,10},{4,13},{5,12},{6,15},{7,14},{8,0},{9,1},... | collective-permute-start | bytes 12582920 | tf_op jit(solution)/shard_map/ppermute | solution.py:120
  240.5 27.3 %collective-permute-start.47 = (bf16[2048,256]{1,0:T(8,128)(2,1)}, bf16[2048,256]{1,0:T(8,128)(2,1)}, u32[]{:S(2)}, u32[]{:S(2)}) collective-permute-start(bf16[2048,256]{1,0:T(8,128)(2,1)} %collective-permute-done.46.refs_1_), channel_id=1, source_target_pairs={{2,0},{3,1},{10,8},{11,9},{18,16},{19,17},{26,24},{27,25}} | collective-permute-start | bytes 3145736 | tf_op jit(solution)/shard_map/ppermute | solution.py:120
  241.8 26.0 %collective-permute-start.50 = (bf16[2048,256]{1,0:T(8,128)(2,1)}, bf16[2048,256]{1,0:T(8,128)(2,1)}, u32[]{:S(2)}, u32[]{:S(2)}) collective-permute-start(bf16[2048,256]{1,0:T(8,128)(2,1)} %collective-permute-done.49.refs_5_), channel_id=1, source_target_pairs={{4,6},{5,7},{12,14},{13,15},{20,22},{21,23},{28,30},{29,31}} | collective-permute-start | bytes 3145736 | tf_op jit(solution)/shard_map/ppermute | solution.py:120
  267.9 28.2 %collective-permute-start.33 = (bf16[2048,256]{1,0:T(8,128)(2,1)}, bf16[2048,256]{1,0:T(8,128)(2,1)}, u32[]{:S(2)}, u32[]{:S(2)}) collective-permute-start(bf16[2048,256]{1,0:T(8,128)(2,1)} %collective-permute-done.32.refs_1_), channel_id=1, source_target_pairs={{2,0},{3,1},{10,8},{11,9},{18,16},{19,17},{26,24},{27,25}} | collective-permute-start | bytes 3145736 | tf_op jit(solution)/shard_map/ppermute | solution.py:120
  269.2 48.9 %collective-permute-start.19 = (bf16[2048,256]{1,0:T(8,128)(2,1)}, bf16[2048,256]{1,0:T(8,128)(2,1)}, u32[]{:S(2)}, u32[]{:S(2)}) collective-permute-start(bf16[2048,256]{1,0:T(8,128)(2,1)} %collective-permute-done.18.refs_1_), channel_id=1, source_target_pairs={{2,0},{3,1},{10,8},{11,9},{18,16},{19,17},{26,24},{27,25}} | collective-permute-start | bytes 3145736 | tf_op jit(solution)/shard_map/ppermute | solution.py:120
  270.9 47.3 %collective-permute-start.22 = (bf16[2048,256]{1,0:T(8,128)(2,1)}, bf16[2048,256]{1,0:T(8,128)(2,1)}, u32[]{:S(2)}, u32[]{:S(2)}) collective-permute-start(bf16[2048,256]{1,0:T(8,128)(2,1)} %collective-permute-done.21.refs_5_), channel_id=1, source_target_pairs={{4,6},{5,7},{12,14},{13,15},{20,22},{21,23},{28,30},{29,31}} | collective-permute-start | bytes 3145736 | tf_op jit(solution)/shard_map/ppermute | solution.py:120
  320.4 27.7 %collective-permute-start.5 = (bf16[2048,256]{1,0:T(8,128)(2,1)}, bf16[2048,256]{1,0:T(8,128)(2,1)}, u32[]{:S(2)}, u32[]{:S(2)}) collective-permute-start(bf16[2048,256]{1,0:T(8,128)(2,1)} %collective-permute-done.4.refs_1_), channel_id=1, source_target_pairs={{2,0},{3,1},{10,8},{11,9},{18,16},{19,17},{26,24},{27,25}} | collective-permute-start | bytes 3145736 | tf_op jit(solution)/shard_map/ppermute | solution.py:120
  321.7 28.1 %collective-permute-start.23 = (bf16[2048,256]{1,0:T(8,128)(2,1)}, bf16[2048,256]{1,0:T(8,128)(2,1)}, u32[]{:S(2)}, u32[]{:S(2)}) collective-permute-start(bf16[2048,256]{1,0:T(8,128)(2,1)} %collective-permute-done.19.refs_0_), channel_id=1, source_target_pairs={{0,8},{1,9},{2,10},{3,11},{4,12},{5,13},{6,14},{7,15},{8,0},{9,1},... | collective-permute-start | bytes 3145736 | tf_op jit(solution)/shard_map/ppermute | solution.py:120
  322.6 27.1 %collective-permute-start.29 = (bf16[2048,256]{1,0:T(8,128)(2,1)}, bf16[2048,256]{1,0:T(8,128)(2,1)}, u32[]{:S(2)}, u32[]{:S(2)}) collective-permute-start(bf16[2048,256]{1,0:T(8,128)(2,1)} %collective-permute-done.22.refs_6_), channel_id=1, source_target_pairs={{0,8},{1,9},{2,10},{3,11},{4,12},{5,13},{6,14},{7,15},{8,0},{9,1},... | collective-permute-start | bytes 3145736 | tf_op jit(solution)/shard_map/ppermute | solution.py:120
  336.9 32.2 %all-to-all-start.3 = ((bf16[4,1024,256]{2,1,0:T(8,128)(2,1)}), bf16[4,1024,256]{2,1,0:T(8,128)(2,1)}, u32[]{:S(2)}, u32[]{:S(2)}) async-start(bf16[4,1024,256]{2,1,0:T(8,128)(2,1)} %shard_map.40), calls=%async_computation.3 | async-start | bytes 4194304 | tf_op jit(solution)/shard_map/all_to_all | solution.py:156
  342.0 32.0 %collective-permute-start.10 = (bf16[2048,256]{1,0:T(8,128)(2,1)}, bf16[2048,256]{1,0:T(8,128)(2,1)}, u32[]{:S(2)}, u32[]{:S(2)}) collective-permute-start(bf16[2048,256]{1,0:T(8,128)(2,1)} %collective-permute-done.4.refs_1_), channel_id=1, source_target_pairs={{0,8},{1,9},{2,10},{3,11},{4,12},{5,13},{6,14},{7,15},{8,0},{9,1},... | collective-permute-start | bytes 3145736 | tf_op jit(solution)/shard_map/ppermute | solution.py:120
  342.6 31.9 %collective-permute-start.14 = (bf16[2048,256]{1,0:T(8,128)(2,1)}, bf16[2048,256]{1,0:T(8,128)(2,1)}, u32[]{:S(2)}, u32[]{:S(2)}) collective-permute-start(bf16[2048,256]{1,0:T(8,128)(2,1)} %collective-permute-done.7.refs_5_), channel_id=1, source_target_pairs={{0,8},{1,9},{2,10},{3,11},{4,12},{5,13},{6,14},{7,15},{8,0},{9,1},... | collective-permute-start | bytes 3145736 | tf_op jit(solution)/shard_map/ppermute | solution.py:120
  348.1 25.7 %collective-permute-start.36 = (bf16[2048,256]{1,0:T(8,128)(2,1)}, bf16[2048,256]{1,0:T(8,128)(2,1)}, u32[]{:S(2)}, u32[]{:S(2)}) collective-permute-start(bf16[2048,256]{1,0:T(8,128)(2,1)} %collective-permute-done.35.refs_5_), channel_id=1, source_target_pairs={{4,6},{5,7},{12,14},{13,15},{20,22},{21,23},{28,30},{29,31}} | collective-permute-start | bytes 3145736 | tf_op jit(solution)/shard_map/ppermute | solution.py:120
  349.8 25.2 %collective-permute-start.9 = (bf16[2048,256]{1,0:T(8,128)(2,1)}, bf16[2048,256]{1,0:T(8,128)(2,1)}, u32[]{:S(2)}, u32[]{:S(2)}) collective-permute-start(bf16[2048,256]{1,0:T(8,128)(2,1)} %collective-permute-done.5.refs_0_), channel_id=1, source_target_pairs={{0,8},{1,9},{2,10},{3,11},{4,12},{5,13},{6,14},{7,15},{8,0},{9,1},... | collective-permute-start | bytes 3145736 | tf_op jit(solution)/shard_map/ppermute | solution.py:120
  369.2 30.2 %all-to-all-start.1 = ((bf16[4,1024,256]{2,1,0:T(8,128)(2,1)}), bf16[4,1024,256]{2,1,0:T(8,128)(2,1)}, u32[]{:S(2)}, u32[]{:S(2)}) async-start(bf16[4,1024,256]{2,1,0:T(8,128)(2,1)} %shard_map.38), calls=%async_computation.1 | async-start | bytes 4194304 | tf_op jit(solution)/shard_map/all_to_all | solution.py:156
  373.8 29.2 %collective-permute-start.41 = (bf16[2048,256]{1,0:T(8,128)(2,1)}, bf16[2048,256]{1,0:T(8,128)(2,1)}, u32[]{:S(2)}, u32[]{:S(2)}) collective-permute-start(bf16[2048,256]{1,0:T(8,128)(2,1)} %collective-permute-done.34.refs_4_), channel_id=1, source_target_pairs={{0,8},{1,9},{2,10},{3,11},{4,12},{5,13},{6,14},{7,15},{8,0},{9,1},... | collective-permute-start | bytes 3145736 | tf_op jit(solution)/shard_map/ppermute | solution.py:120
  374.1 28.9 %collective-permute-start.38 = (bf16[2048,256]{1,0:T(8,128)(2,1)}, bf16[2048,256]{1,0:T(8,128)(2,1)}, u32[]{:S(2)}, u32[]{:S(2)}) collective-permute-start(bf16[2048,256]{1,0:T(8,128)(2,1)} %collective-permute-done.32.refs_1_), channel_id=1, source_target_pairs={{0,8},{1,9},{2,10},{3,11},{4,12},{5,13},{6,14},{7,15},{8,0},{9,1},... | collective-permute-start | bytes 3145736 | tf_op jit(solution)/shard_map/ppermute | solution.py:120
  374.4 28.6 %collective-permute-start.42 = (bf16[2048,256]{1,0:T(8,128)(2,1)}, bf16[2048,256]{1,0:T(8,128)(2,1)}, u32[]{:S(2)}, u32[]{:S(2)}) collective-permute-start(bf16[2048,256]{1,0:T(8,128)(2,1)} %collective-permute-done.35.refs_5_), channel_id=1, source_target_pairs={{0,8},{1,9},{2,10},{3,11},{4,12},{5,13},{6,14},{7,15},{8,0},{9,1},... | collective-permute-start | bytes 3145736 | tf_op jit(solution)/shard_map/ppermute | solution.py:120
  374.6 28.4 %collective-permute-start.37 = (bf16[2048,256]{1,0:T(8,128)(2,1)}, bf16[2048,256]{1,0:T(8,128)(2,1)}, u32[]{:S(2)}, u32[]{:S(2)}) collective-permute-start(bf16[2048,256]{1,0:T(8,128)(2,1)} %collective-permute-done.33.refs_0_), channel_id=1, source_target_pairs={{0,8},{1,9},{2,10},{3,11},{4,12},{5,13},{6,14},{7,15},{8,0},{9,1},... | collective-permute-start | bytes 3145736 | tf_op jit(solution)/shard_map/ppermute | solution.py:120
  374.9 28.1 %collective-permute-start.43 = (bf16[2048,256]{1,0:T(8,128)(2,1)}, bf16[2048,256]{1,0:T(8,128)(2,1)}, u32[]{:S(2)}, u32[]{:S(2)}) collective-permute-start(bf16[2048,256]{1,0:T(8,128)(2,1)} %collective-permute-done.36.refs_6_), channel_id=1, source_target_pairs={{0,8},{1,9},{2,10},{3,11},{4,12},{5,13},{6,14},{7,15},{8,0},{9,1},... | collective-permute-start | bytes 3145736 | tf_op jit(solution)/shard_map/ppermute | solution.py:120
  399.4 29.3 %all-to-all-start = ((bf16[4,1024,256]{2,1,0:T(8,128)(2,1)}), bf16[4,1024,256]{2,1,0:T(8,128)(2,1)S(1)}, u32[]{:S(2)}, u32[]{:S(2)}) async-start(bf16[4,1024,256]{2,1,0:T(8,128)(2,1)} %shard_map.37), calls=%async_computation | async-start | bytes 4194304 | tf_op jit(solution)/shard_map/all_to_all | solution.py:156
  430.0 30.2 %all-to-all-start.2 = ((bf16[4,1024,256]{2,1,0:T(8,128)(2,1)}), bf16[4,1024,256]{2,1,0:T(8,128)(2,1)}, u32[]{:S(2)}, u32[]{:S(2)}) async-start(bf16[4,1024,256]{2,1,0:T(8,128)(2,1)} %shard_map.39), calls=%async_computation.2 | async-start | bytes 4194304 | tf_op jit(solution)/shard_map/all_to_all | solution.py:156
  437.1 48.4 %collective-permute-start.58 = (bf16[1024,256]{1,0:T(8,128)(2,1)}, bf16[1024,256]{1,0:T(8,128)(2,1)S(1)}, u32[]{:S(2)}, u32[]{:S(2)}) collective-permute-start(bf16[1024,256]{1,0:T(8,128)(2,1)} %fusion.44), channel_id=1, source_target_pairs={{0,1},{1,0},{2,3},{3,2},{4,5},{5,4},{6,7},{7,6},{8,9},{9,8},{10,11... | collective-permute-start | bytes 1572872 | tf_op jit(solution)/shard_map/ppermute | solution.py:120
  441.4 34.5 %collective-permute-start.30 = (bf16[1024,256]{1,0:T(8,128)(2,1)}, bf16[1024,256]{1,0:T(8,128)(2,1)S(1)}, u32[]{:S(2)}, u32[]{:S(2)}) collective-permute-start(bf16[1024,256]{1,0:T(8,128)(2,1)} %fusion.42), channel_id=1, source_target_pairs={{0,1},{1,0},{2,3},{3,2},{4,5},{5,4},{6,7},{7,6},{8,9},{9,8},{10,11... | collective-permute-start | bytes 1572872 | tf_op jit(solution)/shard_map/ppermute | solution.py:120
  443.7 30.9 %collective-permute-start.16 = (bf16[1024,256]{1,0:T(8,128)(2,1)}, bf16[1024,256]{1,0:T(8,128)(2,1)}, u32[]{:S(2)}, u32[]{:S(2)}) collective-permute-start(bf16[1024,256]{1,0:T(8,128)(2,1)} %fusion.41), channel_id=1, source_target_pairs={{0,1},{1,0},{2,3},{3,2},{4,5},{5,4},{6,7},{7,6},{8,9},{9,8},{10,11... | collective-permute-start | bytes 1572872 | tf_op jit(solution)/shard_map/ppermute | solution.py:120
  (31 other events, 442.4 us)

commit v2 on v1

v2 whole, which is shorter than its diff:
```python
import functools

import jax
import jax.numpy as jnp
from jax import lax
from jax.experimental import pallas as pl
from jax.experimental.pallas import tpu as pltpu
from jax.sharding import PartitionSpec as P

PARTS = (4, 2, 2)
AXES = ("arc", "col")
SPOTS = 4


def band_weights(coef, arc_ids, epochs_here):
    band = coef.shape[1]
    span = epochs_here + band
    start = lax.axis_index("arc") * epochs_here
    ids_all = jnp.concatenate([jnp.full((band,), -1, jnp.int32), arc_ids])
    ids_win = lax.dynamic_slice_in_dim(ids_all, start, span, 0)
    ids_row = lax.dynamic_slice_in_dim(arc_ids, start, epochs_here, 0)
    leading = jnp.concatenate([coef[:, ::-1], jnp.ones((epochs_here, 1), coef.dtype)], 1)
    padded = jnp.concatenate([leading, jnp.zeros((epochs_here, span - band), coef.dtype)], 1)
    skewed = padded.reshape(-1)[: epochs_here * span].reshape(epochs_here, span)
    return jnp.where(ids_row[:, None] == ids_win[None, :], skewed, jnp.zeros_like(skewed))


def window_of(partials, band):
    arcs = lax.axis_size("arc")
    behind = lax.ppermute(partials[partials.shape[0] - band :], "arc", [(a, a + 1) for a in range(arcs - 1)])
    return jnp.concatenate([behind, partials], 0)


def gathered_body(partials, coef, arc_ids):
    epochs_here, channels, width = partials.shape
    weight = band_weights(coef, arc_ids, epochs_here)
    window = window_of(partials, coef.shape[1])
    filtered = jnp.einsum("et,tcm->cem", weight, window, preferred_element_type=jnp.float32)
    filtered = filtered.astype(jnp.bfloat16).reshape(channels * epochs_here, width)
    term = lax.dot_general(
        filtered,
        lax.all_gather(filtered, "col", axis=1, tiled=True),
        (((0,), (0,)), ((), ())),
        preferred_element_type=jnp.float32,
    )
    return lax.psum_scatter(term, "arc", scatter_dimension=1, tiled=True)


def filter_kernel(weight, taken, straight, turned):
    found = jnp.dot(weight[...], taken[0], preferred_element_type=jnp.float32).astype(jnp.bfloat16)
    straight[...] = found
    turned[...] = found.T


def filter_half(weight, taken):
    channels, lags, width = taken.shape
    count = weight.shape[0]
    return pl.pallas_call(
        filter_kernel,
        out_shape=(
            jax.ShapeDtypeStruct((channels * count, width), jnp.bfloat16),
            jax.ShapeDtypeStruct((width, channels * count), jnp.bfloat16),
        ),
        grid=(channels,),
        in_specs=[
            pl.BlockSpec((count, lags), lambda c: (0, 0)),
            pl.BlockSpec((1, lags, width), lambda c: (c, 0, 0)),
        ],
        out_specs=(pl.BlockSpec((count, width), lambda c: (c, 0)), pl.BlockSpec((width, count), lambda c: (0, c))),
        compiler_params=pltpu.CompilerParams(vmem_limit_bytes=40 << 20),
        cost_estimate=pl.CostEstimate(
            flops=2 * count * lags * width * channels,
            bytes_accessed=2 * channels * width * (lags + 2 * count),
            transcendentals=0,
        ),
    )(weight, taken)


def product_kernel(flags, *refs):
    near, far, right, outs = refs[:4], refs[4:8], refs[8:12], refs[12:-2]
    left, arrived = refs[-2:]

    @pl.when(pl.program_id(0) == 0)
    def _():
        for value, group in ((0, near), (1, far)):

            @pl.when(flags[0] == value)
            def _():
                copies = [pltpu.make_async_copy(ref, left.at[i], arrived.at[i]) for i, ref in enumerate(group)]
                for copy in copies:
                    copy.start()
                for copy in copies:
                    copy.wait()

    total = jnp.dot(left[0], right[0][...], preferred_element_type=jnp.float32)
    for i in range(1, 4):
        total += jnp.dot(left[i], right[i][...], preferred_element_type=jnp.float32)
    if len(outs) == 1:
        outs[0][...] = total
    else:
        first, keep, give = outs
        swap = flags[1] == 1
        keep[...] = jnp.where(swap, total, first[...])
        give[...] = jnp.where(swap, first[...], total).astype(give.dtype)


def products(flags, near, far, right, start=0, part=None, first=None):
    rows, depth = near[0].shape
    width = rows
    part = part or width
    tile = min(256, part)

    def spec(height, value):
        shift = start // tile if value.shape[1] == width else 0
        return pl.BlockSpec((height, tile), lambda i, w: (0, shift + i))

    here = pl.BlockSpec((rows, tile), lambda i, w: (0, i))
    whole = jax.ShapeDtypeStruct((rows, part), jnp.float32)
    return pl.pallas_call(
        product_kernel,
        out_shape=whole if first is None else (whole, jax.ShapeDtypeStruct((rows, part), jnp.bfloat16)),
        grid_spec=pltpu.PrefetchScalarGridSpec(
            num_scalar_prefetch=1,
            grid=(part // tile,),
            in_specs=[pl.BlockSpec(memory_space=pl.ANY)] * 8
            + [spec(depth, value) for value in right]
            + ([] if first is None else [spec(rows, first)]),
            out_specs=here if first is None else (here, here),
            scratch_shapes=[pltpu.VMEM((4, rows, depth), near[0].dtype), pltpu.SemaphoreType.DMA((4,))],
        ),
        compiler_params=pltpu.CompilerParams(vmem_limit_bytes=40 << 20),
        cost_estimate=pl.CostEstimate(
            flops=depth * part,
            bytes_accessed=depth * part,
            transcendentals=0,
        ),
    )(flags, *near, *far, *right, *([] if first is None else [first]))


def pairs(arcs, cols, target):
    found = []
    for half in range(arcs // 2):
        for core in range(2):
            for spot in range(cols // 2):
                for side in range(2):
                    place = target(half, core, spot, side)
                    if place is not None:
                        h, k, z, y = place
                        found.append(((2 * half + core) * cols + 2 * spot + side, (2 * h + k) * cols + 2 * z + y))
    return found


def line_body(partials, coef, arc_ids):
    epochs_here, channels, width = partials.shape
    band = coef.shape[1]
    arcs, cols = lax.axis_size("arc"), lax.axis_size("col")
    arc, col = lax.axis_index("arc"), lax.axis_index("col")
    half, core, spot, side = arc // 2, arc % 2, col // 2, col % 2
    cut = epochs_here - band
    unit = width // sum(PARTS)
    edges = [unit * sum(PARTS[:i]) for i in range(len(PARTS) + 1)]
    middle = width // 2

    def send(value, target):
        return lax.ppermute(value, AXES, pairs(arcs, cols, target))

    def hop(value, hops, step):
        def target(h, k, z, y):
            there, origin = z + step, z - step * (hops - 1)
            return (h, k, there, y) if 0 <= there < SPOTS and 0 <= origin < SPOTS else None

        return send(value, target)

    def cores(value):
        return send(value, lambda h, k, z, y: (h, 1 - k, z, y))

    def sides(value):
        return send(value, lambda h, k, z, y: (h, k, z, 1 - y))

    def halves(value):
        return send(value, lambda h, k, z, y: (1 - h, k, z, y))

    v = {}

    def fence():
        v.update(lax.optimization_barrier(dict(v)))

    ours = core == spot % 2
    flag_one = jnp.stack([jnp.where(ours, 0, 1), jnp.where(spot // 2 == half, 0, 1)]).astype(jnp.int32)
    flag_two = jnp.stack([jnp.where(ours, 1, 0), jnp.where(spot % 2 == half, 0, 1)]).astype(jnp.int32)
    low, even_spot = spot < SPOTS // 2, spot % 2 == 0

    weight = band_weights(coef, arc_ids, epochs_here)
    behind = lax.ppermute(partials[cut:], "arc", [(a, a + 1) for a in range(arcs - 1)])
    here = jnp.swapaxes(partials, 0, 1)
    v["late"], v["late_t"] = filter_half(weight[band:, band:], here)
    v["up1l"], v["down1l"] = hop(v["late"], 1, 1), hop(v["late"], 1, -1)
    v["far_l"] = sides(v["late_t"])
    v["late_o"] = cores(v["late"])
    behind, _ = lax.optimization_barrier((behind, v["late_o"]))
    v["early"], v["early_t"] = filter_half(
        weight[:band, : 2 * band], jnp.concatenate([jnp.swapaxes(behind, 0, 1), here[:, :band]], 1)
    )
    fence()
    v["up1e"], v["down1e"] = hop(v["early"], 1, 1), hop(v["early"], 1, -1)
    v["far_e"] = sides(v["early_t"])
    v["late_to"], v["early_o"] = cores(v["late_t"]), cores(v["early"])
    fence()

    def near():
        return [v["late_t"], v["late_to"], v["early_t"], v["early_to"]]

    def far():
        return [v["far_l"], v["far_lo"], v["far_e"], v["far_eo"]]

    v["up2l"], v["down2l"] = hop(v["up1l"], 2, 1), hop(v["down1l"], 2, -1)
    v["up2e"], v["down2e"] = hop(v["up1e"], 2, 1), hop(v["down1e"], 2, -1)
    v["early_to"], v["far_lo"], v["far_eo"] = cores(v["early_t"]), cores(v["far_l"]), cores(v["far_e"])
    v["own_t"] = products(flag_one, near(), far(), [v["late"], v["late_o"], v["early"], v["early_o"]])
    low_now, _ = lax.optimization_barrier((low, v["far_eo"]))
    v["next_l"], v["next_e"] = jnp.where(low_now, v["down1l"], v["up1l"]), jnp.where(low_now, v["down1e"], v["up1e"])
    v["next_lo"], v["next_eo"] = cores(v["next_l"]), cores(v["next_e"])
    v["next_t"] = products(flag_two, near(), far(), [v["next_l"], v["next_lo"], v["next_e"], v["next_eo"]])
    fence()

    def over(start):
        right = [v["over_l"], v["over_lo"], v["over_e"], v["over_eo"]]
        return products(flag_one, near(), far(), right, start, middle, v["own_t"])

    def chosen(up, down, stay_up, stay_down):
        stay = jnp.where(even_spot, stay_down, stay_up)
        return jnp.where((spot == 0) | (spot == SPOTS - 1), jnp.where(spot == 0, down, up), stay)

    def last(n):
        a, b = edges[n], edges[n + 1]
        e = chosen(v[f"up3{n}"], v[f"down3{n}"], v["up1e"][:, a:b], v["down1e"][:, a:b])
        return products(flag_two, near(), far(), [v["last_l"], v["last_lo"], e, cores(e)], a, b - a, v["next_t"])

    def third(n):
        v[f"up3{n}"], v[f"down3{n}"] = hop(v[f"up3{n}"], 3, 1), hop(v[f"down3{n}"], 3, -1)

    v["up3l"], v["down3l"] = hop(v["up2l"], 3, 1), hop(v["down2l"], 3, -1)
    for n in range(len(PARTS)):
        v[f"up3{n}"] = v["up2e"][:, edges[n] : edges[n + 1]]
        v[f"down3{n}"] = v["down2e"][:, edges[n] : edges[n + 1]]
    third(0)
    v["over_l"], v["over_e"] = jnp.where(low, v["down2l"], v["up2l"]), jnp.where(low, v["down2e"], v["up2e"])
    v["over_lo"], v["over_eo"] = cores(v["over_l"]), cores(v["over_e"])
    keep_a, give_a = over(0)
    v["sum_a"] = keep_a + halves(give_a)
    v["keep_b"], give_b = over(middle)
    v["give_b"] = halves(give_b)
    fence()
    third(1)
    v["last_l"] = chosen(v["up3l"], v["down3l"], v["up1l"], v["down1l"])
    v["last_lo"] = cores(v["last_l"])
    v["keep0"], v["give0"] = last(0)
    v["sum_b"] = v["keep_b"] + v["give_b"]
    fence()
    third(2)
    v["keep1"], v["give1"] = last(1)
    v["sum0"] = v["keep0"] + halves(v["give0"])
    one = jnp.concatenate([v["sum_a"], v["sum_b"]], 1)
    v["far_one"] = send(
        one.astype(jnp.bfloat16), lambda h, k, z, y: (h, 1 - k, z, 1 - y) if k != z % 2 else None
    )
    fence()

    def home_two(value):
        return send(value.astype(jnp.bfloat16), lambda h, k, z, y: (h, 1 - k, z, 1 - y) if k == z % 2 else None)

    keep, give = last(2)
    sums = [v["sum0"], v["keep1"] + halves(v["give1"]), keep + halves(give)]
    pieces = []
    for n, two in enumerate(sums):
        span = slice(edges[n], edges[n + 1])
        far_two = home_two(two)
        pieces.append((jnp.where(ours, one[:, span], two), jnp.where(ours, v["far_one"][:, span], far_two).astype(jnp.float32)))
    even = [jnp.where(side == 0, a, b) for a, b in pieces]
    odd = [jnp.where(side == 0, b, a) for a, b in pieces]
    return jnp.concatenate(even + odd, 1)


def solution(mesh):
    fits = mesh.shape["arc"] == SPOTS and mesh.shape["col"] == 2 * SPOTS
    return jax.shard_map(
        line_body if fits else gathered_body,
        mesh=mesh,
        in_specs=(P("arc", None, "col"), P("arc", None), P()),
        out_specs=P("col", "arc"),
        check_vma=False,
    )
```

time: 495 us -> 433 us (0.87)
  the two profiles are of different devices: /device:TPU:0 before, /device:TPU:19 now
where the time goes in v2:
time: 433 us; the launch traced here: 431 us
  waiting for transfers between devices  212 us (49%)
  Pallas kernels  73.4 us (17%)
  starting transfers between devices  68.3 us (16%)
  local copies, waits for them, and re-layouts  42.7 us (10%)
  other arithmetic  34.6 us (8%)
    ppermute x41, waiting for transfers between devices, send(): return lax.ppermute(value, AXES, pairs(arcs, cols, target))  212 us
    pallas_call x7, Pallas kernels, products(): pl.pallas_call(product_kernel, out_shape=whole if first is None else (who...  68.8 us
    ppermute x41, starting transfers between devices, send(): return lax.ppermute(value, AXES, pairs(arcs, cols, target))  66.9 us
    unnamed x100, local copies, waits for them, and re-layouts  30.3 us
  transfers between devices with their start and end apart: 42, of which 16 were waited for; matrix products, arithmetic and copies ran while one was open for 9% of the time, Pallas kernels for 17%

profile of v2, /device:TPU:19, one launch (start us, length us, event | category | flops | bytes accessed | tf_op | source)
XLA Modules:
  0.0 431.4 jit_solution(12445771267523008498)
XLA Ops:
  1.6 2.0 copy.9
  5.0 3.4 copy.10
  12.0 2.2 copy-done.14
  14.2 2.3 shard_map.37
  17.9 2.1 collective-permute-start
  21.3 4.4 %collective-permute-start.4 = (bf16[1024,1024]{1,0:T(8,128)(2,1)S(1)}, bf16[1024,1024]{1,0:T(8,128)(2,1)}, u32[]{:S(2)}, u32[]{:S(2)}) collective-permute-start(bf16[1024,1024]{1,0:T(8,128)(2,1)S(1)} %get-tuple-element.144.refs_8_), channel_id=1, source_target_pairs={{0,2},{1,3},{2,4},{3,5},{4,6},{5,7},{8,10},{9,11},{10,12},{11,13},... | collective-permute-start | bytes 6291464 | tf_op jit(solution)/shard_map/ppermute | solution.py:165
  26.0 2.8 pad_maximum_fusion.taken
  28.8 2.3 shard_map.38
  31.1 36.0 %collective-permute-done = bf16[1024,1024]{1,0:T(8,128)(2,1)} collective-permute-done((bf16[1024,1024]{1,0:T(8,128)(2,1)S(1)}, bf16[1024,1024]{1,0:T(8,128)(2,1)}, u32[]{:S(2)}, u32[]{:S(2)}) %collective-permute-start) | collective-permute-done | bytes 2097184 | tf_op jit(solution)/shard_map/ppermute | solution.py:165
  67.1 3.0 collective-permute-done.4
  74.3 4.6 %collective-permute-start.9 = (bf16[1024,1024]{1,0:T(8,128)(2,1)S(1)}, bf16[1024,1024]{1,0:T(8,128)(2,1)}, u32[]{:S(2)}, u32[]{:S(2)}) collective-permute-start(bf16[1024,1024]{1,0:T(8,128)(2,1)S(1)} %get-tuple-element.139.refs_10_), channel_id=1, source_target_pairs={{0,2},{1,3},{2,4},{3,5},{4,6},{5,7},{8,10},{9,11},{10,12},{11,13},... | collective-permute-start | bytes 6291464 | tf_op jit(solution)/shard_map/ppermute | solution.py:165
  78.9 39.3 %collective-permute-done.5 = bf16[1024,1024]{1,0:T(8,128)(2,1)} collective-permute-done((bf16[1024,1024]{1,0:T(8,128)(2,1)S(1)}, bf16[1024,1024]{1,0:T(8,128)(2,1)}, u32[]{:S(2)}, u32[]{:S(2)}) %collective-permute-start.5) | collective-permute-done | bytes 2097184 | tf_op jit(solution)/shard_map/ppermute | solution.py:165
  118.2 2.8 collective-permute-done.7.refs_6_
  125.3 5.7 %collective-permute-done.13.refs_7_ = bf16[1024,1024]{1,0:T(8,128)(2,1)} collective-permute-done((bf16[1024,1024]{1,0:T(8,128)(2,1)}, bf16[1024,1024]{1,0:T(8,128)(2,1)}, u32[]{:S(2)}, u32[]{:S(2)}) %collective-permute-start.13) | collective-permute-done | bytes 2097184 | tf_op jit(solution)/shard_map/ppermute | solution.py:165
  133.2 3.4 broadcast_select_fusion.2.refs_8_
  137.1 2.6 collective-permute-start.10
  141.0 2.7 collective-permute-start.11
  145.0 3.0 collective-permute-start.17
  149.3 2.1 collective-permute-start.18
  159.6 15.1 %shard_map.40.refs_12_ = f32[1024,1024]{1,0:T(8,128)} custom-call(s32[2]{0:T(128)S(1)} %pad_add_fusion.1.flags, bf16[1024,1024]{1,0:T(8,128)(2,1)S(1)} %get-tuple-element.226.refs_0_, bf16[1024,1024]{1,0:T(8,128)(2,1)S(1)} %copy-done.7, bf16[1024,1024]{1,0:T(8,128)(2,1)S(1)} %copy-done.4, bf16[1024,1024]{1,0:T(8,128)(2,1)S(1)} %copy-done.10, ...), custom_call_target="tpu_custom_call" | custom-call | flops 1048576 | bytes 1048576 | tf_op jit(solution)/shard_map/pallas_call | solution.py:119
  174.7 13.1 %shard_map.39.refs_12_ = f32[1024,1024]{1,0:T(8,128)} custom-call(s32[2]{0:T(128)S(1)} %pad_add_fusion.flags, bf16[1024,1024]{1,0:T(8,128)(2,1)S(1)} %get-tuple-element.226.refs_0_, bf16[1024,1024]{1,0:T(8,128)(2,1)S(1)} %copy-done.7, bf16[1024,1024]{1,0:T(8,128)(2,1)S(1)} %copy-done.4, bf16[1024,1024]{1,0:T(8,128)(2,1)S(1)} %copy-done.10, ...), custom_call_target="tpu_custom_call" | custom-call | flops 1048576 | bytes 1048576 | tf_op jit(solution)/shard_map/pallas_call | solution.py:119
  187.8 40.7 %collective-permute-done.11 = bf16[1024,1024]{1,0:T(8,128)(2,1)} collective-permute-done((bf16[1024,1024]{1,0:T(8,128)(2,1)}, bf16[1024,1024]{1,0:T(8,128)(2,1)}, u32[]{:S(2)}, u32[]{:S(2)}) %collective-permute-start.11) | collective-permute-done | bytes 2097184 | tf_op jit(solution)/shard_map/ppermute | solution.py:165
  228.6 10.4 %collective-permute-done.18 = bf16[1024,1024]{1,0:T(8,128)(2,1)} collective-permute-done((bf16[1024,1024]{1,0:T(8,128)(2,1)}, bf16[1024,1024]{1,0:T(8,128)(2,1)}, u32[]{:S(2)}, u32[]{:S(2)}) %collective-permute-start.18) | collective-permute-done | bytes 2097184 | tf_op jit(solution)/shard_map/ppermute | solution.py:165
  244.7 1.9 collective-permute-start.20
  246.6 2.2 collective-permute-done.22.refs_11_
  250.1 10.6 %shard_map.42 = (f32[1024,512]{1,0:T(8,128)S(1)}, bf16[1024,512]{1,0:T(8,128)(2,1)S(1)}) custom-call(s32[2]{0:T(128)S(1)} %pad_add_fusion.1.flags, bf16[1024,1024]{1,0:T(8,128)(2,1)S(1)} %get-tuple-element.226.refs_0_, bf16[1024,1024]{1,0:T(8,128)(2,1)S(1)} %copy-done.7, bf16[1024,1024]{1,0:T(8,128)(2,1)S(1)} %copy-done.4, ...), custom_call_target="tpu_custom_call" | custom-call | flops 524288 | bytes 524288 | tf_op jit(solution)/shard_map/pallas_call | solution.py:119
  262.2 2.6 collective-permute-start.26
  264.8 2.3 slice.71
  267.0 2.3 slice.74
  270.9 2.2 collective-permute-start.25
  273.2 10.6 %shard_map.41 = (f32[1024,512]{1,0:T(8,128)S(1)}, bf16[1024,512]{1,0:T(8,128)(2,1)S(1)}) custom-call(s32[2]{0:T(128)S(1)} %pad_add_fusion.1.flags, bf16[1024,1024]{1,0:T(8,128)(2,1)S(1)} %get-tuple-element.226.refs_0_, bf16[1024,1024]{1,0:T(8,128)(2,1)S(1)} %copy-done.7, bf16[1024,1024]{1,0:T(8,128)(2,1)S(1)} %copy-done.4, ...), custom_call_target="tpu_custom_call" | custom-call | flops 524288 | bytes 524288 | tf_op jit(solution)/shard_map/pallas_call | solution.py:119
  286.3 2.9 fusion.8
  289.5 39.3 %collective-permute-done.25 = bf16[1024,512]{1,0:T(8,128)(2,1)} collective-permute-done((bf16[1024,512]{1,0:T(8,128)(2,1)}, bf16[1024,512]{1,0:T(8,128)(2,1)}, u32[]{:S(2)}, u32[]{:S(2)}) %collective-permute-start.25) | collective-permute-done | bytes 1048608 | tf_op jit(solution)/shard_map/ppermute | solution.py:165
  328.8 2.6 select_select_fusion.refs_8_
  331.4 3.3 collective-permute-start.28
  334.8 2.2 select_select_fusion.1.refs_10_
  338.6 4.4 %collective-permute-start.30 = (bf16[1024,256]{1,0:T(8,128)(2,1)}, bf16[1024,256]{1,0:T(8,128)(2,1)S(1)}, u32[]{:S(2)}, u32[]{:S(2)}) collective-permute-start(bf16[1024,256]{1,0:T(8,128)(2,1)} %get-tuple-element.197), channel_id=1, source_target_pairs={{4,6},{5,7},{12,14},{13,15},{20,22},{21,23},{28,30},{29,31}} | collective-permute-start | bytes 1572872 | tf_op jit(solution)/shard_map/ppermute | solution.py:165
  346.0 7.7 %shard_map.43 = (f32[1024,512]{1,0:T(8,128)S(1)}, bf16[1024,512]{1,0:T(8,128)(2,1)S(1)}) custom-call(s32[2]{0:T(128)S(1)} %pad_add_fusion.flags, bf16[1024,1024]{1,0:T(8,128)(2,1)S(1)} %get-tuple-element.226.refs_0_, bf16[1024,1024]{1,0:T(8,128)(2,1)S(1)} %copy-done.8, bf16[1024,1024]{1,0:T(8,128)(2,1)S(1)} %copy-done.5, bf16[1024,1024]{1,0:T(8,128)(2,1)S(1)} %copy-done.11, ...), custom_call_target="tpu_custom_call" | custom-call | flops 524288 | bytes 524288 | tf_op jit(solution)/shard_map/pallas_call | solution.py:119
  354.8 6.4 %collective-permute-start.32 = (bf16[1024,1024]{1,0:T(8,128)(2,1)S(1)}, bf16[1024,1024]{1,0:T(8,128)(2,1)S(1)}, u32[]{:S(2)}, u32[]{:S(2)}) collective-permute-start(bf16[1024,1024]{1,0:T(8,128)(2,1)S(1)} %pad_maximum_fusion.1), channel_id=1, source_target_pairs={{2,11},{3,10},{6,15},{7,14},{8,1},{9,0},{12,5},{13,4},{18,27},{19,... | collective-permute-start | bytes 6291464 | tf_op jit(solution)/shard_map/ppermute | solution.py:165
  365.3 5.8 %shard_map.44 = (f32[1024,256]{1,0:T(8,128)S(1)}, bf16[1024,256]{1,0:T(8,128)(2,1)}) custom-call(s32[2]{0:T(128)S(1)} %pad_add_fusion.flags, bf16[1024,1024]{1,0:T(8,128)(2,1)S(1)} %get-tuple-element.226.refs_0_, bf16[1024,1024]{1,0:T(8,128)(2,1)S(1)} %copy-done.8, bf16[1024,1024]{1,0:T(8,128)(2,1)S(1)} %copy-done.5, bf16[1024,1024]{1,0:T(8,128)(2,1)S(1)} %copy-done.11, ...), custom_call_target="tpu_custom_call" | custom-call | flops 262144 | bytes 262144 | tf_op jit(solution)/shard_map/pallas_call | solution.py:119
  371.1 13.9 %collective-permute-done.34 = bf16[1024,512]{1,0:T(8,128)(2,1)S(1)} collective-permute-done((bf16[1024,512]{1,0:T(8,128)(2,1)S(1)}, bf16[1024,512]{1,0:T(8,128)(2,1)S(1)}, u32[]{:S(2)}, u32[]{:S(2)}) %collective-permute-start.34) | collective-permute-done | bytes 1048608 | tf_op jit(solution)/shard_map/ppermute | solution.py:165
  385.4 2.1 select_select_fusion.2.refs_10_
  390.2 5.8 %shard_map.45 = (f32[1024,256]{1,0:T(8,128)S(1)}, bf16[1024,256]{1,0:T(8,128)(2,1)}) custom-call(s32[2]{0:T(128)S(1)} %pad_add_fusion.flags, bf16[1024,1024]{1,0:T(8,128)(2,1)S(1)} %get-tuple-element.226.refs_0_, bf16[1024,1024]{1,0:T(8,128)(2,1)S(1)} %copy-done.8, bf16[1024,1024]{1,0:T(8,128)(2,1)S(1)} %copy-done.5, bf16[1024,1024]{1,0:T(8,128)(2,1)S(1)} %copy-done.11, ...), custom_call_target="tpu_custom_call" | custom-call | flops 262144 | bytes 262144 | tf_op jit(solution)/shard_map/pallas_call | solution.py:119
  398.4 2.6 collective-permute-done.37
  403.5 5.2 %collective-permute-done.40 = bf16[1024,256]{1,0:T(8,128)(2,1)S(1)} collective-permute-done((bf16[1024,256]{1,0:T(8,128)(2,1)}, bf16[1024,256]{1,0:T(8,128)(2,1)S(1)}, u32[]{:S(2)}, u32[]{:S(2)}) %collective-permute-start.40) | collective-permute-done | bytes 524320 | tf_op jit(solution)/shard_map/ppermute | solution.py:165
  410.4 2.8 fusion
  415.2 7.9 %collective-permute-done.41 = bf16[1024,256]{1,0:T(8,128)(2,1)S(1)} collective-permute-done((bf16[1024,256]{1,0:T(8,128)(2,1)S(1)}, bf16[1024,256]{1,0:T(8,128)(2,1)S(1)}, u32[]{:S(2)}, u32[]{:S(2)}) %collective-permute-start.41) | collective-permute-done | bytes 524320 | tf_op jit(solution)/shard_map/ppermute | solution.py:165
  426.7 3.4 copy-done.45
  (189 shorter events, 71.4 us)
Async XLA Ops:
  3.6 22.4 %collective-permute-start.1 = (bf16[256,4,1024]{2,0,1:T(8,128)(2,1)}, bf16[256,4,1024]{2,0,1:T(8,128)(2,1)}, u32[]{:S(2)}, u32[]{:S(2)}) collective-permute-start(bf16[256,4,1024]{2,0,1:T(8,128)(2,1)} %copy.9), channel_id=1, source_target_pairs={{0,8},{8,16},{16,24},{1,9},{9,17},{17,25},{2,10},{10,18},{18,26},{... | collective-permute-start | bytes 6291464 | tf_op jit(solution)/shard_map/ppermute | solution.py:194
  16.5 9.4 %collective-permute-start.2 = (bf16[1024,1024]{1,0:T(8,128)(2,1)S(1)}, bf16[1024,1024]{1,0:T(8,128)(2,1)S(1)}, u32[]{:S(2)}, u32[]{:S(2)}) collective-permute-start(bf16[1024,1024]{1,0:T(8,128)(2,1)S(1)} %get-tuple-element.144.refs_8_), channel_id=1, source_target_pairs={{0,8},{1,9},{2,10},{3,11},{4,12},{5,13},{6,14},{7,15},{8,0},{9,1},... | collective-permute-start | bytes 6291464 | tf_op jit(solution)/shard_map/ppermute | solution.py:165
  17.9 49.2 %collective-permute-start = (bf16[1024,1024]{1,0:T(8,128)(2,1)S(1)}, bf16[1024,1024]{1,0:T(8,128)(2,1)}, u32[]{:S(2)}, u32[]{:S(2)}) collective-permute-start(bf16[1024,1024]{1,0:T(8,128)(2,1)S(1)} %get-tuple-element.144.refs_8_), channel_id=1, source_target_pairs={{2,0},{3,1},{4,2},{5,3},{6,4},{7,5},{10,8},{11,9},{12,10},{13,11},... | collective-permute-start | bytes 6291464 | tf_op jit(solution)/shard_map/ppermute | solution.py:165
  20.0 47.2 %collective-permute-start.3 = (bf16[1024,1024]{1,0:T(8,128)(2,1)S(1)}, bf16[1024,1024]{1,0:T(8,128)(2,1)S(1)}, u32[]{:S(2)}, u32[]{:S(2)}) collective-permute-start(bf16[1024,1024]{1,0:T(8,128)(2,1)S(1)} %get-tuple-element.226.refs_0_), channel_id=1, source_target_pairs={{0,1},{1,0},{2,3},{3,2},{4,5},{5,4},{6,7},{7,6},{8,9},{9,8},{10,11... | collective-permute-start | bytes 6291464 | tf_op jit(solution)/shard_map/ppermute | solution.py:165
  21.3 48.8 %collective-permute-start.4 = (bf16[1024,1024]{1,0:T(8,128)(2,1)S(1)}, bf16[1024,1024]{1,0:T(8,128)(2,1)}, u32[]{:S(2)}, u32[]{:S(2)}) collective-permute-start(bf16[1024,1024]{1,0:T(8,128)(2,1)S(1)} %get-tuple-element.144.refs_8_), channel_id=1, source_target_pairs={{0,2},{1,3},{2,4},{3,5},{4,6},{5,7},{8,10},{9,11},{10,12},{11,13},... | collective-permute-start | bytes 6291464 | tf_op jit(solution)/shard_map/ppermute | solution.py:165
  31.1 92.6 %copy-start.3 = (bf16[1024,1024]{1,0:T(8,128)(2,1)}, bf16[1024,1024]{1,0:T(8,128)(2,1)S(1)}, u32[]{:S(2)}) copy-start(bf16[1024,1024]{1,0:T(8,128)(2,1)S(1)} %get-tuple-element.228.refs_2_) | copy-start | bytes 6291460
  31.1 92.6 %copy-start.23 = (bf16[1024,1024]{1,0:T(8,128)(2,1)}, bf16[1024,1024]{1,0:T(8,128)(2,1)S(1)}, u32[]{:S(2)}) copy-start(bf16[1024,1024]{1,0:T(8,128)(2,1)S(1)} %get-tuple-element.139.refs_10_) | copy-start | bytes 6291460
  67.1 53.9 %copy-start = (bf16[1024,1024]{1,0:T(8,128)(2,1)}, bf16[1024,1024]{1,0:T(8,128)(2,1)S(1)}, u32[]{:S(2)}) copy-start(bf16[1024,1024]{1,0:T(8,128)(2,1)S(1)} %collective-permute-done.3.refs_4_) | copy-start | bytes 6291460
  70.1 48.1 %collective-permute-start.5 = (bf16[1024,1024]{1,0:T(8,128)(2,1)S(1)}, bf16[1024,1024]{1,0:T(8,128)(2,1)}, u32[]{:S(2)}, u32[]{:S(2)}) collective-permute-start(bf16[1024,1024]{1,0:T(8,128)(2,1)S(1)} %get-tuple-element.139.refs_10_), channel_id=1, source_target_pairs={{2,0},{3,1},{4,2},{5,3},{6,4},{7,5},{10,8},{11,9},{12,10},{13,11},... | collective-permute-start | bytes 6291464 | tf_op jit(solution)/shard_map/ppermute | solution.py:165
  72.0 46.2 %collective-permute-start.6 = (bf16[1024,1024]{1,0:T(8,128)(2,1)S(1)}, bf16[1024,1024]{1,0:T(8,128)(2,1)S(1)}, u32[]{:S(2)}, u32[]{:S(2)}) collective-permute-start(bf16[1024,1024]{1,0:T(8,128)(2,1)S(1)} %get-tuple-element.139.refs_10_), channel_id=1, source_target_pairs={{0,8},{1,9},{2,10},{3,11},{4,12},{5,13},{6,14},{7,15},{8,0},{9,1},... | collective-permute-start | bytes 6291464 | tf_op jit(solution)/shard_map/ppermute | solution.py:165
  73.7 47.3 %collective-permute-start.7 = (bf16[1024,1024]{1,0:T(8,128)(2,1)S(1)}, bf16[1024,1024]{1,0:T(8,128)(2,1)}, u32[]{:S(2)}, u32[]{:S(2)}) collective-permute-start(bf16[1024,1024]{1,0:T(8,128)(2,1)S(1)} %get-tuple-element.228.refs_2_), channel_id=1, source_target_pairs={{0,1},{1,0},{2,3},{3,2},{4,5},{5,4},{6,7},{7,6},{8,9},{9,8},{10,11... | collective-permute-start | bytes 6291464 | tf_op jit(solution)/shard_map/ppermute | solution.py:165
  74.0 47.1 %collective-permute-start.8 = (bf16[1024,1024]{1,0:T(8,128)(2,1)S(1)}, bf16[1024,1024]{1,0:T(8,128)(2,1)S(1)}, u32[]{:S(2)}, u32[]{:S(2)}) collective-permute-start(bf16[1024,1024]{1,0:T(8,128)(2,1)S(1)} %get-tuple-element.226.refs_0_), channel_id=1, source_target_pairs={{0,8},{1,9},{2,10},{3,11},{4,12},{5,13},{6,14},{7,15},{8,0},{9,1},... | collective-permute-start | bytes 6291464 | tf_op jit(solution)/shard_map/ppermute | solution.py:165
  74.3 49.4 %collective-permute-start.9 = (bf16[1024,1024]{1,0:T(8,128)(2,1)S(1)}, bf16[1024,1024]{1,0:T(8,128)(2,1)}, u32[]{:S(2)}, u32[]{:S(2)}) collective-permute-start(bf16[1024,1024]{1,0:T(8,128)(2,1)S(1)} %get-tuple-element.139.refs_10_), channel_id=1, source_target_pairs={{0,2},{1,3},{2,4},{3,5},{4,6},{5,7},{8,10},{9,11},{10,12},{11,13},... | collective-permute-start | bytes 6291464 | tf_op jit(solution)/shard_map/ppermute | solution.py:165
  123.7 7.3 %collective-permute-start.13 = (bf16[1024,1024]{1,0:T(8,128)(2,1)}, bf16[1024,1024]{1,0:T(8,128)(2,1)}, u32[]{:S(2)}, u32[]{:S(2)}) collective-permute-start(bf16[1024,1024]{1,0:T(8,128)(2,1)} %collective-permute-done.7.refs_6_), channel_id=1, source_target_pairs={{0,8},{1,9},{2,10},{3,11},{4,12},{5,13},{6,14},{7,15},{8,0},{9,1},... | collective-permute-start | bytes 6291464 | tf_op jit(solution)/shard_map/ppermute | solution.py:165
  124.8 14.9 %collective-permute-start.12 = (bf16[1024,1024]{1,0:T(8,128)(2,1)}, bf16[1024,1024]{1,0:T(8,128)(2,1)S(1)}, u32[]{:S(2)}, u32[]{:S(2)}) collective-permute-start(bf16[1024,1024]{1,0:T(8,128)(2,1)} %copy-done.3), channel_id=1, source_target_pairs={{0,8},{1,9},{2,10},{3,11},{4,12},{5,13},{6,14},{7,15},{8,0},{9,1},... | collective-permute-start | bytes 6291464 | tf_op jit(solution)/shard_map/ppermute | solution.py:165
  124.9 18.8 %collective-permute-start.14 = (bf16[1024,1024]{1,0:T(8,128)(2,1)}, bf16[1024,1024]{1,0:T(8,128)(2,1)S(1)}, u32[]{:S(2)}, u32[]{:S(2)}) collective-permute-start(bf16[1024,1024]{1,0:T(8,128)(2,1)} %copy-done), channel_id=1, source_target_pairs={{0,8},{1,9},{2,10},{3,11},{4,12},{5,13},{6,14},{7,15},{8,0},{9,1},... | collective-permute-start | bytes 6291464 | tf_op jit(solution)/shard_map/ppermute | solution.py:165
  132.8 15.2 %collective-permute-start.15 = (bf16[1024,1024]{1,0:T(8,128)(2,1)S(1)}, bf16[1024,1024]{1,0:T(8,128)(2,1)S(1)}, u32[]{:S(2)}, u32[]{:S(2)}) collective-permute-start(bf16[1024,1024]{1,0:T(8,128)(2,1)S(1)} %broadcast_select_fusion.3.refs_10_), channel_id=1, source_target_pairs={{0,8},{1,9},{2,10},{3,11},{4,12},{5,13},{6,14},{7,15},{8,0},{9,1},... | collective-permute-start | bytes 6291464 | tf_op jit(solution)/shard_map/ppermute | solution.py:165
  136.7 38.0 %collective-permute-start.16 = (bf16[1024,1024]{1,0:T(8,128)(2,1)}, bf16[1024,1024]{1,0:T(8,128)(2,1)}, u32[]{:S(2)}, u32[]{:S(2)}) collective-permute-start(bf16[1024,1024]{1,0:T(8,128)(2,1)} %broadcast_select_fusion.2.refs_8_), channel_id=1, source_target_pairs={{0,8},{1,9},{2,10},{3,11},{4,12},{5,13},{6,14},{7,15},{8,0},{9,1},... | collective-permute-start | bytes 6291464 | tf_op jit(solution)/shard_map/ppermute | solution.py:165
  137.1 50.8 %collective-permute-start.10 = (bf16[1024,1024]{1,0:T(8,128)(2,1)}, bf16[1024,1024]{1,0:T(8,128)(2,1)}, u32[]{:S(2)}, u32[]{:S(2)}) collective-permute-start(bf16[1024,1024]{1,0:T(8,128)(2,1)} %collective-permute-done.5), channel_id=1, source_target_pairs={{2,0},{3,1},{4,2},{5,3},{10,8},{11,9},{12,10},{13,11},{18,16},{19,... | collective-permute-start | bytes 6291464 | tf_op jit(solution)/shard_map/ppermute | solution.py:165
  141.0 87.6 %collective-permute-start.11 = (bf16[1024,1024]{1,0:T(8,128)(2,1)}, bf16[1024,1024]{1,0:T(8,128)(2,1)}, u32[]{:S(2)}, u32[]{:S(2)}) collective-permute-start(bf16[1024,1024]{1,0:T(8,128)(2,1)} %collective-permute-done), channel_id=1, source_target_pairs={{2,0},{3,1},{4,2},{5,3},{10,8},{11,9},{12,10},{13,11},{18,16},{19,... | collective-permute-start | bytes 6291464 | tf_op jit(solution)/shard_map/ppermute | solution.py:165
  145.0 83.6 %collective-permute-start.17 = (bf16[1024,1024]{1,0:T(8,128)(2,1)}, bf16[1024,1024]{1,0:T(8,128)(2,1)}, u32[]{:S(2)}, u32[]{:S(2)}) collective-permute-start(bf16[1024,1024]{1,0:T(8,128)(2,1)} %collective-permute-done.9), channel_id=1, source_target_pairs={{2,4},{3,5},{4,6},{5,7},{10,12},{11,13},{12,14},{13,15},{18,20},{1... | collective-permute-start | bytes 6291464 | tf_op jit(solution)/shard_map/ppermute | solution.py:165
  149.3 89.7 %collective-permute-start.18 = (bf16[1024,1024]{1,0:T(8,128)(2,1)}, bf16[1024,1024]{1,0:T(8,128)(2,1)}, u32[]{:S(2)}, u32[]{:S(2)}) collective-permute-start(bf16[1024,1024]{1,0:T(8,128)(2,1)} %collective-permute-done.4), channel_id=1, source_target_pairs={{2,4},{3,5},{4,6},{5,7},{10,12},{11,13},{12,14},{13,15},{18,20},{1... | collective-permute-start | bytes 6291464 | tf_op jit(solution)/shard_map/ppermute | solution.py:165
  240.8 5.8 %collective-permute-start.21 = (bf16[1024,1024]{1,0:T(8,128)(2,1)S(1)}, bf16[1024,1024]{1,0:T(8,128)(2,1)S(1)}, u32[]{:S(2)}, u32[]{:S(2)}) collective-permute-start(bf16[1024,1024]{1,0:T(8,128)(2,1)S(1)} %broadcast_select_fusion.1.refs_8_), channel_id=1, source_target_pairs={{0,8},{1,9},{2,10},{3,11},{4,12},{5,13},{6,14},{7,15},{8,0},{9,1},... | collective-permute-start | bytes 6291464 | tf_op jit(solution)/shard_map/ppermute | solution.py:165
  243.9 5.0 %collective-permute-start.22 = (bf16[1024,1024]{1,0:T(8,128)(2,1)S(1)}, bf16[1024,1024]{1,0:T(8,128)(2,1)S(1)}, u32[]{:S(2)}, u32[]{:S(2)}) collective-permute-start(bf16[1024,1024]{1,0:T(8,128)(2,1)S(1)} %broadcast_select_fusion.refs_10_), channel_id=1, source_target_pairs={{0,8},{1,9},{2,10},{3,11},{4,12},{5,13},{6,14},{7,15},{8,0},{9,1},... | collective-permute-start | bytes 6291464 | tf_op jit(solution)/shard_map/ppermute | solution.py:165
  244.7 84.1 %collective-permute-start.20 = (bf16[1024,1024]{1,0:T(8,128)(2,1)}, bf16[1024,1024]{1,0:T(8,128)(2,1)}, u32[]{:S(2)}, u32[]{:S(2)}) collective-permute-start(bf16[1024,1024]{1,0:T(8,128)(2,1)} %collective-permute-done.11), channel_id=1, source_target_pairs={{2,0},{3,1},{10,8},{11,9},{18,16},{19,17},{26,24},{27,25}} | collective-permute-start | bytes 6291464 | tf_op jit(solution)/shard_map/ppermute | solution.py:165
  260.7 24.4 %collective-permute-start.24 = (bf16[1024,512]{1,0:T(8,128)(2,1)S(1)}, bf16[1024,512]{1,0:T(8,128)(2,1)S(1)}, u32[]{:S(2)}, u32[]{:S(2)}) collective-permute-start(bf16[1024,512]{1,0:T(8,128)(2,1)S(1)} %get-tuple-element.170), channel_id=1, source_target_pairs={{0,16},{1,17},{2,18},{3,19},{4,20},{5,21},{6,22},{7,23},{8,24},{9,... | collective-permute-start | bytes 3145736 | tf_op jit(solution)/shard_map/ppermute | solution.py:165
  262.2 66.6 %collective-permute-start.26 = (bf16[1024,1024]{1,0:T(8,128)(2,1)}, bf16[1024,1024]{1,0:T(8,128)(2,1)}, u32[]{:S(2)}, u32[]{:S(2)}) collective-permute-start(bf16[1024,1024]{1,0:T(8,128)(2,1)} %collective-permute-done.18), channel_id=1, source_target_pairs={{4,6},{5,7},{12,14},{13,15},{20,22},{21,23},{28,30},{29,31}} | collective-permute-start | bytes 6291464 | tf_op jit(solution)/shard_map/ppermute | solution.py:165
  269.3 20.2 %collective-permute-start.19 = (bf16[1024,512]{1,0:T(8,128)(2,1)}, bf16[1024,512]{1,0:T(8,128)(2,1)}, u32[]{:S(2)}, u32[]{:S(2)}) collective-permute-start(bf16[1024,512]{1,0:T(8,128)(2,1)} %slice.71), channel_id=1, source_target_pairs={{2,0},{3,1},{10,8},{11,9},{18,16},{19,17},{26,24},{27,25}} | collective-permute-start | bytes 3145736 | tf_op jit(solution)/shard_map/ppermute | solution.py:165
  270.9 57.8 %collective-permute-start.25 = (bf16[1024,512]{1,0:T(8,128)(2,1)}, bf16[1024,512]{1,0:T(8,128)(2,1)}, u32[]{:S(2)}, u32[]{:S(2)}) collective-permute-start(bf16[1024,512]{1,0:T(8,128)(2,1)} %slice.74), channel_id=1, source_target_pairs={{4,6},{5,7},{12,14},{13,15},{20,22},{21,23},{28,30},{29,31}} | collective-permute-start | bytes 3145736 | tf_op jit(solution)/shard_map/ppermute | solution.py:165
  286.1 42.7 %collective-permute-start.23 = (bf16[1024,512]{1,0:T(8,128)(2,1)S(1)}, bf16[1024,512]{1,0:T(8,128)(2,1)}, u32[]{:S(2)}, u32[]{:S(2)}) collective-permute-start(bf16[1024,512]{1,0:T(8,128)(2,1)S(1)} %get-tuple-element.166), channel_id=1, source_target_pairs={{0,16},{1,17},{2,18},{3,19},{4,20},{5,21},{6,22},{7,23},{8,24},{9,... | collective-permute-start | bytes 3145736 | tf_op jit(solution)/shard_map/ppermute | solution.py:165
  289.5 64.8 %copy-start.24 = (f32[1024,512]{1,0:T(8,128)}, f32[1024,512]{1,0:T(8,128)S(1)}, u32[]{:S(2)}) copy-start(f32[1024,512]{1,0:T(8,128)S(1)} %convert_add_fusion.2) | copy-start | bytes 6291460
  331.4 13.1 %collective-permute-start.28 = (bf16[1024,1024]{1,0:T(8,128)(2,1)S(1)}, bf16[1024,1024]{1,0:T(8,128)(2,1)S(1)}, u32[]{:S(2)}, u32[]{:S(2)}) collective-permute-start(bf16[1024,1024]{1,0:T(8,128)(2,1)S(1)} %select_select_fusion.refs_8_), channel_id=1, source_target_pairs={{0,8},{1,9},{2,10},{3,11},{4,12},{5,13},{6,14},{7,15},{8,0},{9,1},... | collective-permute-start | bytes 6291464 | tf_op jit(solution)/shard_map/ppermute | solution.py:165
  337.0 7.5 %collective-permute-start.29 = (bf16[1024,512]{1,0:T(8,128)(2,1)S(1)}, bf16[1024,512]{1,0:T(8,128)(2,1)S(1)}, u32[]{:S(2)}, u32[]{:S(2)}) collective-permute-start(bf16[1024,512]{1,0:T(8,128)(2,1)S(1)} %select_select_fusion.1.refs_10_), channel_id=1, source_target_pairs={{0,8},{1,9},{2,10},{3,11},{4,12},{5,13},{6,14},{7,15},{8,0},{9,1},... | collective-permute-start | bytes 3145736 | tf_op jit(solution)/shard_map/ppermute | solution.py:165
  337.7 15.9 %collective-permute-start.27 = (bf16[1024,256]{1,0:T(8,128)(2,1)}, bf16[1024,256]{1,0:T(8,128)(2,1)S(1)}, u32[]{:S(2)}, u32[]{:S(2)}) collective-permute-start(bf16[1024,256]{1,0:T(8,128)(2,1)} %get-tuple-element.176), channel_id=1, source_target_pairs={{2,0},{3,1},{10,8},{11,9},{18,16},{19,17},{26,24},{27,25}} | collective-permute-start | bytes 1572872 | tf_op jit(solution)/shard_map/ppermute | solution.py:165
  338.6 15.6 %collective-permute-start.30 = (bf16[1024,256]{1,0:T(8,128)(2,1)}, bf16[1024,256]{1,0:T(8,128)(2,1)S(1)}, u32[]{:S(2)}, u32[]{:S(2)}) collective-permute-start(bf16[1024,256]{1,0:T(8,128)(2,1)} %get-tuple-element.197), channel_id=1, source_target_pairs={{4,6},{5,7},{12,14},{13,15},{20,22},{21,23},{28,30},{29,31}} | collective-permute-start | bytes 1572872 | tf_op jit(solution)/shard_map/ppermute | solution.py:165
  354.8 30.6 %collective-permute-start.32 = (bf16[1024,1024]{1,0:T(8,128)(2,1)S(1)}, bf16[1024,1024]{1,0:T(8,128)(2,1)S(1)}, u32[]{:S(2)}, u32[]{:S(2)}) collective-permute-start(bf16[1024,1024]{1,0:T(8,128)(2,1)S(1)} %pad_maximum_fusion.1), channel_id=1, source_target_pairs={{2,11},{3,10},{6,15},{7,14},{8,1},{9,0},{12,5},{13,4},{18,27},{19,... | collective-permute-start | bytes 6291464 | tf_op jit(solution)/shard_map/ppermute | solution.py:165
  361.2 23.8 %collective-permute-start.34 = (bf16[1024,512]{1,0:T(8,128)(2,1)S(1)}, bf16[1024,512]{1,0:T(8,128)(2,1)S(1)}, u32[]{:S(2)}, u32[]{:S(2)}) collective-permute-start(bf16[1024,512]{1,0:T(8,128)(2,1)S(1)} %get-tuple-element.210), channel_id=1, source_target_pairs={{0,16},{1,17},{2,18},{3,19},{4,20},{5,21},{6,22},{7,23},{8,24},{9,... | collective-permute-start | bytes 3145736 | tf_op jit(solution)/shard_map/ppermute | solution.py:165
  362.7 2.6 collective-permute-start.33
  362.8 22.6 %collective-permute-start.31 = (bf16[1024,256]{1,0:T(8,128)(2,1)S(1)}, bf16[1024,256]{1,0:T(8,128)(2,1)S(1)}, u32[]{:S(2)}, u32[]{:S(2)}) collective-permute-start(bf16[1024,256]{1,0:T(8,128)(2,1)S(1)} %copy-done.46), channel_id=1, source_target_pairs={{2,0},{3,1},{10,8},{11,9},{18,16},{19,17},{26,24},{27,25}} | collective-permute-start | bytes 1572872 | tf_op jit(solution)/shard_map/ppermute | solution.py:165
  363.5 21.9 %collective-permute-start.35 = (bf16[1024,256]{1,0:T(8,128)(2,1)S(1)}, bf16[1024,256]{1,0:T(8,128)(2,1)S(1)}, u32[]{:S(2)}, u32[]{:S(2)}) collective-permute-start(bf16[1024,256]{1,0:T(8,128)(2,1)S(1)} %get-tuple-element.221), channel_id=1, source_target_pairs={{4,6},{5,7},{12,14},{13,15},{20,22},{21,23},{28,30},{29,31}} | collective-permute-start | bytes 1572872 | tf_op jit(solution)/shard_map/ppermute | solution.py:165
  387.5 2.7 collective-permute-start.39
  387.6 13.4 %collective-permute-start.37 = (bf16[1024,256]{1,0:T(8,128)(2,1)}, bf16[1024,256]{1,0:T(8,128)(2,1)}, u32[]{:S(2)}, u32[]{:S(2)}) collective-permute-start(bf16[1024,256]{1,0:T(8,128)(2,1)} %get-tuple-element.225), channel_id=1, source_target_pairs={{0,16},{1,17},{2,18},{3,19},{4,20},{5,21},{6,22},{7,23},{8,24},{9,... | collective-permute-start | bytes 1572872 | tf_op jit(solution)/shard_map/ppermute | solution.py:165
  388.9 21.5 %collective-permute-start.36 = (bf16[1024,512]{1,0:T(8,128)(2,1)}, bf16[1024,512]{1,0:T(8,128)(2,1)}, u32[]{:S(2)}, u32[]{:S(2)}) collective-permute-start(bf16[1024,512]{1,0:T(8,128)(2,1)} %convert_element_type.37), channel_id=1, source_target_pairs={{0,9},{1,8},{4,13},{5,12},{10,3},{11,2},{14,7},{15,6},{16,25},{17,... | collective-permute-start | bytes 3145736 | tf_op jit(solution)/shard_map/ppermute | solution.py:165
  397.0 11.7 %copy-start.17 = (f32[1024,256]{1,0:T(8,128)S(1)}, f32[1024,256]{1,0:T(8,128)}, u32[]{:S(2)}) copy-start(f32[1024,256]{1,0:T(8,128)} %copy-done.16) | copy-start | bytes 3145732
  397.0 11.7 %collective-permute-start.40 = (bf16[1024,256]{1,0:T(8,128)(2,1)}, bf16[1024,256]{1,0:T(8,128)(2,1)S(1)}, u32[]{:S(2)}, u32[]{:S(2)}) collective-permute-start(bf16[1024,256]{1,0:T(8,128)(2,1)} %get-tuple-element.242), channel_id=1, source_target_pairs={{0,16},{1,17},{2,18},{3,19},{4,20},{5,21},{6,22},{7,23},{8,24},{9,... | collective-permute-start | bytes 1572872 | tf_op jit(solution)/shard_map/ppermute | solution.py:165
  398.4 12.0 %copy-start.25 = (f32[1024,512]{1,0:T(8,128)S(1)}, f32[1024,512]{1,0:T(8,128)}, u32[]{:S(2)}) copy-start(f32[1024,512]{1,0:T(8,128)} %copy-done.24) | copy-start | bytes 6291460
  402.2 11.7 %collective-permute-start.38 = (bf16[1024,256]{1,0:T(8,128)(2,1)S(1)}, bf16[1024,256]{1,0:T(8,128)(2,1)S(1)}, u32[]{:S(2)}, u32[]{:S(2)}) collective-permute-start(bf16[1024,256]{1,0:T(8,128)(2,1)S(1)} %fusion.6), channel_id=1, source_target_pairs={{0,9},{1,8},{4,13},{5,12},{10,3},{11,2},{14,7},{15,6},{16,25},{17,... | collective-permute-start | bytes 1572872 | tf_op jit(solution)/shard_map/ppermute | solution.py:165
  408.8 14.3 %collective-permute-start.41 = (bf16[1024,256]{1,0:T(8,128)(2,1)S(1)}, bf16[1024,256]{1,0:T(8,128)(2,1)S(1)}, u32[]{:S(2)}, u32[]{:S(2)}) collective-permute-start(bf16[1024,256]{1,0:T(8,128)(2,1)S(1)} %fusion.7), channel_id=1, source_target_pairs={{0,9},{1,8},{4,13},{5,12},{10,3},{11,2},{14,7},{15,6},{16,25},{17,... | collective-permute-start | bytes 1572872 | tf_op jit(solution)/shard_map/ppermute | solution.py:165
  (44 other events, 193.1 us)

commit v3 on v2

--- a/solution.py
+++ b/solution.py
@@ -46,15 +46,18 @@
     return lax.psum_scatter(term, "arc", scatter_dimension=1, tiled=True)
 
 
-def filter_kernel(weight, taken, straight, turned):
-    found = jnp.dot(weight[...], taken[0], preferred_element_type=jnp.float32).astype(jnp.bfloat16)
+def filter_kernel(weight, behind, here, straight, turned):
+    band = behind.shape[1]
+    found = jnp.dot(weight[:, :band], behind[0], preferred_element_type=jnp.float32)
+    found += jnp.dot(weight[:, band:], here[0], preferred_element_type=jnp.float32)
+    found = found.astype(jnp.bfloat16)
     straight[...] = found
     turned[...] = found.T
 
 
-def filter_half(weight, taken):
-    channels, lags, width = taken.shape
-    count = weight.shape[0]
+def filter_rows(weight, behind, here):
+    channels, count, width = here.shape
+    band = behind.shape[1]
     return pl.pallas_call(
         filter_kernel,
         out_shape=(
@@ -63,21 +66,22 @@
         ),
         grid=(channels,),
         in_specs=[
-            pl.BlockSpec((count, lags), lambda c: (0, 0)),
-            pl.BlockSpec((1, lags, width), lambda c: (c, 0, 0)),
+            pl.BlockSpec((count, band + count), lambda c: (0, 0)),
+            pl.BlockSpec((1, band, width), lambda c: (c, 0, 0)),
+            pl.BlockSpec((1, count, width), lambda c: (c, 0, 0)),
         ],
         out_specs=(pl.BlockSpec((count, width), lambda c: (c, 0)), pl.BlockSpec((width, count), lambda c: (0, c))),
         compiler_params=pltpu.CompilerParams(vmem_limit_bytes=40 << 20),
         cost_estimate=pl.CostEstimate(
-            flops=2 * count * lags * width * channels,
-            bytes_accessed=2 * channels * width * (lags + 2 * count),
+            flops=2 * count * (band + count) * width * channels,
+            bytes_accessed=2 * channels * width * (band + 3 * count),
             transcendentals=0,
         ),
-    )(weight, taken)
+    )(weight, behind, here)
 
 
 def product_kernel(flags, *refs):
-    near, far, right, outs = refs[:4], refs[4:8], refs[8:12], refs[12:-2]
+    near, far, right, outs = refs[:2], refs[2:4], refs[4:6], refs[6:-2]
     left, arrived = refs[-2:]
 
     @pl.when(pl.program_id(0) == 0)
@@ -93,8 +97,7 @@
                     copy.wait()
 
     total = jnp.dot(left[0], right[0][...], preferred_element_type=jnp.float32)
-    for i in range(1, 4):
-        total += jnp.dot(left[i], right[i][...], preferred_element_type=jnp.float32)
+    total += jnp.dot(left[1], right[1][...], preferred_element_type=jnp.float32)
     if len(outs) == 1:
         outs[0][...] = total
     else:
@@ -122,19 +125,62 @@
         grid_spec=pltpu.PrefetchScalarGridSpec(
             num_scalar_prefetch=1,
             grid=(part // tile,),
-            in_specs=[pl.BlockSpec(memory_space=pl.ANY)] * 8
+            in_specs=[pl.BlockSpec(memory_space=pl.ANY)] * 4
             + [spec(depth, value) for value in right]
             + ([] if first is None else [spec(rows, first)]),
             out_specs=here if first is None else (here, here),
-            scratch_shapes=[pltpu.VMEM((4, rows, depth), near[0].dtype), pltpu.SemaphoreType.DMA((4,))],
+            scratch_shapes=[pltpu.VMEM((2, rows, depth), near[0].dtype), pltpu.SemaphoreType.DMA((2,))],
         ),
         compiler_params=pltpu.CompilerParams(vmem_limit_bytes=40 << 20),
-        cost_estimate=pl.CostEstimate(
-            flops=depth * part,
-            bytes_accessed=depth * part,
-            transcendentals=0,
+        cost_estimate=pl.CostEstimate(flops=depth * part, bytes_accessed=depth * part, transcendentals=0),
+    )(flags, *near, *far, *right, *([] if first is None else [first]))
+
+
+def place_kernel(flags, one, keep, came, far_one, far_two, *refs):
+    out = refs[-1]
+    ours = flags[1] == 1
+
+    @pl.when(pl.program_id(1) == 0)
+    def _():
+        out[...] = jnp.where(ours, one[...], keep[...] + came[...].astype(jnp.float32))
+
+    @pl.when(pl.program_id(1) == 1)
+    def _():
+        out[...] = jnp.where(ours, far_one[...], far_two[...]).astype(jnp.float32)
+
+
+def place(flags, one, keep, came, far_one, far_two, start, held=()):
+    rows, width = one.shape
+    part = keep.shape[1]
+    tile = min(256, part)
+    first, count = start // tile, width // tile
+
+    def wide(n, i, w):
+        return 0, first + n
+
+    def narrow(n, i, w):
+        return 0, n
+
+    return pl.pallas_call(
+        place_kernel,
+        out_shape=jax.ShapeDtypeStruct((rows, 2 * width), jnp.float32),
+        grid_spec=pltpu.PrefetchScalarGridSpec(
+            num_scalar_prefetch=1,
+            grid=(part // tile, 2),
+            in_specs=[
+                pl.BlockSpec((rows, tile), wide),
+                pl.BlockSpec((rows, tile), narrow),
+                pl.BlockSpec((rows, tile), narrow),
+                pl.BlockSpec((rows, tile), wide),
+                pl.BlockSpec((rows, tile), narrow),
+            ]
+            + [pl.BlockSpec(memory_space=pl.ANY)] * len(held),
+            out_specs=pl.BlockSpec((rows, tile), lambda n, i, w: (0, (w[0] + i) % 2 * count + first + n)),
         ),
-    )(flags, *near, *far, *right, *([] if first is None else [first]))
+        input_output_aliases={6: 0} if held else {},
+        compiler_params=pltpu.CompilerParams(vmem_limit_bytes=40 << 20),
+        cost_estimate=pl.CostEstimate(flops=rows * part, bytes_accessed=22 * rows * part, transcendentals=0),
+    )(flags, one, keep, came, far_one, far_two, *held)
 
 
 def pairs(arcs, cols, target):
@@ -191,76 +237,56 @@
     low, even_spot = spot < SPOTS // 2, spot % 2 == 0
 
     weight = band_weights(coef, arc_ids, epochs_here)
-    behind = lax.ppermute(partials[cut:], "arc", [(a, a + 1) for a in range(arcs - 1)])
-    here = jnp.swapaxes(partials, 0, 1)
-    v["late"], v["late_t"] = filter_half(weight[band:, band:], here)
-    v["up1l"], v["down1l"] = hop(v["late"], 1, 1), hop(v["late"], 1, -1)
-    v["far_l"] = sides(v["late_t"])
-    v["late_o"] = cores(v["late"])
-    behind, _ = lax.optimization_barrier((behind, v["late_o"]))
-    v["early"], v["early_t"] = filter_half(
-        weight[:band, : 2 * band], jnp.concatenate([jnp.swapaxes(behind, 0, 1), here[:, :band]], 1)
-    )
-    fence()
-    v["up1e"], v["down1e"] = hop(v["early"], 1, 1), hop(v["early"], 1, -1)
-    v["far_e"] = sides(v["early_t"])
-    v["late_to"], v["early_o"] = cores(v["late_t"]), cores(v["early"])
-    fence()
-
-    def near():
-        return [v["late_t"], v["late_to"], v["early_t"], v["early_to"]]
-
-    def far():
-        return [v["far_l"], v["far_lo"], v["far_e"], v["far_eo"]]
-
-    v["up2l"], v["down2l"] = hop(v["up1l"], 2, 1), hop(v["down1l"], 2, -1)
-    v["up2e"], v["down2e"] = hop(v["up1e"], 2, 1), hop(v["down1e"], 2, -1)
-    v["early_to"], v["far_lo"], v["far_eo"] = cores(v["early_t"]), cores(v["far_l"]), cores(v["far_e"])
-    v["own_t"] = products(flag_one, near(), far(), [v["late"], v["late_o"], v["early"], v["early_o"]])
-    low_now, _ = lax.optimization_barrier((low, v["far_eo"]))
-    v["next_l"], v["next_e"] = jnp.where(low_now, v["down1l"], v["up1l"]), jnp.where(low_now, v["down1e"], v["up1e"])
-    v["next_lo"], v["next_eo"] = cores(v["next_l"]), cores(v["next_e"])
-    v["next_t"] = products(flag_two, near(), far(), [v["next_l"], v["next_lo"], v["next_e"], v["next_eo"]])
+    behind = lax.ppermute(jnp.swapaxes(partials[cut:], 0, 1), "arc", [(a, a + 1) for a in range(arcs - 1)])
+    v["own"], v["own_t"] = filter_rows(weight, behind, jnp.swapaxes(partials, 0, 1))
+    v["up1"], v["down1"] = hop(v["own"], 1, 1), hop(v["own"], 1, -1)
+    v["far_t"] = sides(v["own_t"])
+    v["own_o"], v["own_to"] = cores(v["own"]), cores(v["own_t"])
+    fence()
+
+    def product(flags, *rest):
+        return products(flags, [v["own_t"], v["own_to"]], [v["far_t"], v["far_to"]], *rest)
+
+    v["up2"], v["down2"] = hop(v["up1"], 2, 1), hop(v["down1"], 2, -1)
+    v["far_to"] = cores(v["far_t"])
+    v["sum_own"] = product(flag_one, [v["own"], v["own_o"]])
+    v["next"] = jnp.where(low, v["down1"], v["up1"])
+    v["next_o"] = cores(v["next"])
+    v["sum_next"] = product(flag_two, [v["next"], v["next_o"]])
     fence()
 
     def over(start):
-        right = [v["over_l"], v["over_lo"], v["over_e"], v["over_eo"]]
-        return products(flag_one, near(), far(), right, start, middle, v["own_t"])
-
-    def chosen(up, down, stay_up, stay_down):
-        stay = jnp.where(even_spot, stay_down, stay_up)
-        return jnp.where((spot == 0) | (spot == SPOTS - 1), jnp.where(spot == 0, down, up), stay)
+        return product(flag_one, [v["over"], v["over_o"]], start, middle, v["sum_own"])
+
+    def third(n):
+        v[f"up3{n}"], v[f"down3{n}"] = hop(v[f"up3{n}"], 3, 1), hop(v[f"down3{n}"], 3, -1)
 
     def last(n):
         a, b = edges[n], edges[n + 1]
-        e = chosen(v[f"up3{n}"], v[f"down3{n}"], v["up1e"][:, a:b], v["down1e"][:, a:b])
-        return products(flag_two, near(), far(), [v["last_l"], v["last_lo"], e, cores(e)], a, b - a, v["next_t"])
-
-    def third(n):
-        v[f"up3{n}"], v[f"down3{n}"] = hop(v[f"up3{n}"], 3, 1), hop(v[f"down3{n}"], 3, -1)
-
-    v["up3l"], v["down3l"] = hop(v["up2l"], 3, 1), hop(v["down2l"], 3, -1)
+        stay = jnp.where(even_spot, v["down1"][:, a:b], v["up1"][:, a:b])
+        came = jnp.where(spot == 0, v[f"down3{n}"], v[f"up3{n}"])
+        block = jnp.where((spot == 0) | (spot == SPOTS - 1), came, stay)
+        return product(flag_two, [block, cores(block)], a, b - a, v["sum_next"])
+
     for n in range(len(PARTS)):
-        v[f"up3{n}"] = v["up2e"][:, edges[n] : edges[n + 1]]
-        v[f"down3{n}"] = v["down2e"][:, edges[n] : edges[n + 1]]
+        v[f"up3{n}"] = v["up2"][:, edges[n] : edges[n + 1]]
+        v[f"down3{n}"] = v["down2"][:, edges[n] : edges[n + 1]]
     third(0)
-    v["over_l"], v["over_e"] = jnp.where(low, v["down2l"], v["up2l"]), jnp.where(low, v["down2e"], v["up2e"])
-    v["over_lo"], v["over_eo"] = cores(v["over_l"]), cores(v["over_e"])
+    v["over"] = jnp.where(low, v["down2"], v["up2"])
+    v["over_o"] = cores(v["over"])
     keep_a, give_a = over(0)
     v["sum_a"] = keep_a + halves(give_a)
-    v["keep_b"], give_b = over(middle)
-    v["give_b"] = halves(give_b)
+    v["keep_b"], v["give_b"] = over(middle)
     fence()
     third(1)
-    v["last_l"] = chosen(v["up3l"], v["down3l"], v["up1l"], v["down1l"])
-    v["last_lo"] = cores(v["last_l"])
     v["keep0"], v["give0"] = last(0)
-    v["sum_b"] = v["keep_b"] + v["give_b"]
+    v["give_b"] = halves(v["give_b"])
     fence()
     third(2)
     v["keep1"], v["give1"] = last(1)
-    v["sum0"] = v["keep0"] + halves(v["give0"])
-    one = jnp.concatenate([v["sum_a"], v["sum_b"]], 1)
+    v["give0"] = halves(v["give0"])
+    one = jnp.concatenate([v["sum_a"], v["keep_b"] + v["give_b"]], 1)
+    v["one"] = one
     v["far_one"] = send(
         one.astype(jnp.bfloat16), lambda h, k, z, y: (h, 1 - k, z, 1 - y) if k != z % 2 else None
     )
@@ -269,16 +295,16 @@
     def home_two(value):
         return send(value.astype(jnp.bfloat16), lambda h, k, z, y: (h, 1 - k, z, 1 - y) if k == z % 2 else None)
 
+    flags = jnp.stack([side, jnp.where(ours, 1, 0)]).astype(jnp.int32)
+    ends = [(v["keep0"], v["give0"]), (v["keep1"], halves(v["give1"]))]
+    far_two = [home_two(ends[0][0] + ends[0][1])]
     keep, give = last(2)
-    sums = [v["sum0"], v["keep1"] + halves(v["give1"]), keep + halves(give)]
-    pieces = []
-    for n, two in enumerate(sums):
-        span = slice(edges[n], edges[n + 1])
-        far_two = home_two(two)
-        pieces.append((jnp.where(ours, one[:, span], two), jnp.where(ours, v["far_one"][:, span], far_two).astype(jnp.float32)))
-    even = [jnp.where(side == 0, a, b) for a, b in pieces]
-    odd = [jnp.where(side == 0, b, a) for a, b in pieces]
-    return jnp.concatenate(even + odd, 1)
+    ends.append((keep, halves(give)))
+    far_two += [home_two(keep + came) for keep, came in ends[1:]]
+    out = ()
+    for start, (keep, came), far in zip(edges, ends, far_two):
+        out = (place(flags, v["one"], keep, came, v["far_one"], far, start, out),)
+    return out[0]
 
 
 def solution(mesh):

time: 433 us -> 420 us (0.970)
  the two profiles are of different devices: /device:TPU:19 before, /device:TPU:0 now
where the time goes in v3:
time: 420 us; the launch traced here: 419 us
  waiting for transfers between devices  199 us (47%)
  Pallas kernels  99 us (24%)
  starting transfers between devices  65.3 us (16%)
  local copies, waits for them, and re-layouts  32.8 us (8%)
  other arithmetic  22.7 us (5%)
    ppermute x28, waiting for transfers between devices, send(): return lax.ppermute(value, AXES, pairs(arcs, cols, target))  199 us
    pallas_call x7, Pallas kernels, products(): pl.pallas_call(product_kernel, out_shape=whole if first is None else (who...  79.1 us
    ppermute x28, starting transfers between devices, send(): return lax.ppermute(value, AXES, pairs(arcs, cols, target))  62.8 us
    unnamed x39, local copies, waits for them, and re-layouts  13.8 us
    pallas_call x3, Pallas kernels, place(): pl.pallas_call(place_kernel, out_shape=jax.ShapeDtypeStruct((rows, 2 * wi...  12.1 us
  transfers between devices with their start and end apart: 29, of which 12 were waited for; matrix products, arithmetic and copies ran while one was open for 6% of the time, Pallas kernels for 21%

profile of v3, /device:TPU:0, one launch (start us, length us, event | category | flops | bytes accessed | tf_op | source)
XLA Modules:
  0.0 419.1 jit_solution(16868179058723005759)
XLA Ops:
  0.0 3.6 copy.12
  6.2 2.5 collective-permute-start
  9.8 2.2 reshape.8
  16.3 7.7 %shard_map.37 = (bf16[2048,1024]{1,0:T(8,128)(2,1)}, bf16[1024,2048]{1,0:T(8,128)(2,1)}) custom-call(bf16[512,768]{1,0:T(8,128)(2,1)S(1)} %compare_select_fusion.weight, bf16[4,256,1024]{2,1,0:T(8,128)(2,1)S(1)} %collective-permute-done.behind, bf16[4,512,1024]{2,1,0:T(8,128)(2,1)} %bitcast.11), custom_call_target="tpu_custom_call" | custom-call | flops 3221225472 | bytes 14680064 | tf_op jit(solution)/shard_map/pallas_call | solution.py:61
  24.0 18.2 %collective-permute-start.4 = (bf16[1024,2048]{1,0:T(8,128)(2,1)}, bf16[1024,2048]{1,0:T(8,128)(2,1)}, u32[]{:S(2)}, u32[]{:S(2)}) collective-permute-start(bf16[1024,2048]{1,0:T(8,128)(2,1)} %get-tuple-element.141.refs_0_), channel_id=1, source_target_pairs={{0,8},{1,9},{2,10},{3,11},{4,12},{5,13},{6,14},{7,15},{8,0},{9,1},... | collective-permute-start | bytes 12582920 | tf_op jit(solution)/shard_map/ppermute | solution.py:211
  43.7 5.5 %collective-permute-start.5 = (bf16[2048,1024]{1,0:T(8,128)(2,1)}, bf16[2048,1024]{1,0:T(8,128)(2,1)}, u32[]{:S(2)}, u32[]{:S(2)}) collective-permute-start(bf16[2048,1024]{1,0:T(8,128)(2,1)} %get-tuple-element.86.refs_4_), channel_id=1, source_target_pairs={{0,2},{1,3},{2,4},{3,5},{4,6},{5,7},{8,10},{9,11},{10,12},{11,13},... | collective-permute-start | bytes 12582920 | tf_op jit(solution)/shard_map/ppermute | solution.py:211
  50.4 84.5 %collective-permute-done.2.refs_2_ = bf16[1024,2048]{1,0:T(8,128)(2,1)} collective-permute-done((bf16[1024,2048]{1,0:T(8,128)(2,1)}, bf16[1024,2048]{1,0:T(8,128)(2,1)}, u32[]{:S(2)}, u32[]{:S(2)}) %collective-permute-start.2) | collective-permute-done | bytes 4194336 | tf_op jit(solution)/shard_map/ppermute | solution.py:211
  134.9 2.2 collective-permute-done.5
  137.2 7.1 %collective-permute-done.1 = bf16[2048,1024]{1,0:T(8,128)(2,1)} collective-permute-done((bf16[2048,1024]{1,0:T(8,128)(2,1)}, bf16[2048,1024]{1,0:T(8,128)(2,1)}, u32[]{:S(2)}, u32[]{:S(2)}) %collective-permute-start.1) | collective-permute-done | bytes 4194336 | tf_op jit(solution)/shard_map/ppermute | solution.py:211
  144.3 4.6 %broadcast_select_fusion.1.refs_4_ = bf16[2048,1024]{1,0:T(8,128)(2,1)} fusion(bf16[2048,1024]{1,0:T(8,128)(2,1)} %collective-permute-done.1, bf16[2048,1024]{1,0:T(8,128)(2,1)} %collective-permute-done.5, pred[]{:T(512)S(6)} %lt.29), kind=kLoop, calls=%fused_computation.2 | loop fusion | flops 2097152 | bytes 12582913 | tf_op jit(solution)/shard_map/jit(_where)/select_n | solution.py:253
  150.7 2.8 collective-permute-start.9
  153.6 2.8 collective-permute-done.8.refs_5_
  156.4 6.0 %collective-permute-done.7.refs_3_ = bf16[1024,2048]{1,0:T(8,128)(2,1)} collective-permute-done((bf16[1024,2048]{1,0:T(8,128)(2,1)}, bf16[1024,2048]{1,0:T(8,128)(2,1)}, u32[]{:S(2)}, u32[]{:S(2)}) %collective-permute-start.7) | collective-permute-done | bytes 4194336 | tf_op jit(solution)/shard_map/ppermute | solution.py:211
  162.4 15.3 %shard_map.38.refs_6_ = f32[1024,1024]{1,0:T(8,128)S(1)} custom-call(s32[2]{0:T(128)S(1)} %pad_add_fusion.1.flags, bf16[1024,2048]{1,0:T(8,128)(2,1)} %get-tuple-element.141.refs_0_, bf16[1024,2048]{1,0:T(8,128)(2,1)} %collective-permute-done.4.refs_1_, bf16[1024,2048]{1,0:T(8,128)(2,1)} %collective-permute-done.2.refs_2_, ...), custom_call_target="tpu_custom_call" | custom-call | flops 2097152 | bytes 2097152 | tf_op jit(solution)/shard_map/pallas_call | solution.py:122
  177.8 2.1 copy-done
  179.9 15.3 %shard_map.39.refs_6_ = f32[1024,1024]{1,0:T(8,128)S(1)} custom-call(s32[2]{0:T(128)S(1)} %pad_add_fusion.2.flags, bf16[1024,2048]{1,0:T(8,128)(2,1)} %get-tuple-element.141.refs_0_, bf16[1024,2048]{1,0:T(8,128)(2,1)} %collective-permute-done.4.refs_1_, bf16[1024,2048]{1,0:T(8,128)(2,1)} %collective-permute-done.2.refs_2_, ...), custom_call_target="tpu_custom_call" | custom-call | flops 2097152 | bytes 2097152 | tf_op jit(solution)/shard_map/pallas_call | solution.py:122
  195.2 48.9 %collective-permute-done.6 = bf16[2048,1024]{1,0:T(8,128)(2,1)} collective-permute-done((bf16[2048,1024]{1,0:T(8,128)(2,1)}, bf16[2048,1024]{1,0:T(8,128)(2,1)}, u32[]{:S(2)}, u32[]{:S(2)}) %collective-permute-start.6) | collective-permute-done | bytes 4194336 | tf_op jit(solution)/shard_map/ppermute | solution.py:211
  244.1 2.6 broadcast_select_fusion.refs_4_
  246.9 4.5 %slice.44 = bf16[2048,512]{1,0:T(8,128)(2,1)} slice(bf16[2048,1024]{1,0:T(8,128)(2,1)} %collective-permute-done.6), slice={[0:2048], [0:512]} | slice | bytes 4194304 | tf_op jit(solution)/shard_map/slice | solution.py:273
  251.3 3.1 slice.47
  254.4 2.0 collective-permute-start.13
  257.9 2.0 copy-done.15
  259.9 11.8 %shard_map.41 = (f32[1024,512]{1,0:T(8,128)S(1)}, bf16[1024,512]{1,0:T(8,128)(2,1)}) custom-call(s32[2]{0:T(128)S(1)} %pad_add_fusion.2.flags, bf16[1024,2048]{1,0:T(8,128)(2,1)} %get-tuple-element.141.refs_0_, bf16[1024,2048]{1,0:T(8,128)(2,1)} %collective-permute-done.4.refs_1_, bf16[1024,2048]{1,0:T(8,128)(2,1)} %collective-permute-done.2.refs_2_, ...), custom_call_target="tpu_custom_call" | custom-call | flops 1048576 | bytes 1048576 | tf_op jit(solution)/shard_map/pallas_call | solution.py:122
  271.8 2.3 collective-permute-start.12
  274.1 3.9 fusion.1
  278.0 11.1 %shard_map.40 = (f32[1024,512]{1,0:T(8,128)S(1)}, bf16[1024,512]{1,0:T(8,128)(2,1)S(1)}) custom-call(s32[2]{0:T(128)S(1)} %pad_add_fusion.2.flags, bf16[1024,2048]{1,0:T(8,128)(2,1)} %get-tuple-element.141.refs_0_, bf16[1024,2048]{1,0:T(8,128)(2,1)} %collective-permute-done.4.refs_1_, bf16[1024,2048]{1,0:T(8,128)(2,1)} %collective-permute-done.2.refs_2_, ...), custom_call_target="tpu_custom_call" | custom-call | flops 1048576 | bytes 1048576 | tf_op jit(solution)/shard_map/pallas_call | solution.py:122
  289.1 7.5 %collective-permute-done.12 = bf16[1024,512]{1,0:T(8,128)(2,1)S(1)} collective-permute-done((bf16[1024,512]{1,0:T(8,128)(2,1)}, bf16[1024,512]{1,0:T(8,128)(2,1)S(1)}, u32[]{:S(2)}, u32[]{:S(2)}) %collective-permute-start.12) | collective-permute-done | bytes 1048608 | tf_op jit(solution)/shard_map/ppermute | solution.py:211
  297.0 8.6 %collective-permute-done.10 = bf16[2048,512]{1,0:T(8,128)(2,1)} collective-permute-done((bf16[2048,512]{1,0:T(8,128)(2,1)}, bf16[2048,512]{1,0:T(8,128)(2,1)}, u32[]{:S(2)}, u32[]{:S(2)}) %collective-permute-start.10) | collective-permute-done | bytes 2097184 | tf_op jit(solution)/shard_map/ppermute | solution.py:211
  305.6 3.2 select_select_fusion.refs_4_
  310.2 2.3 collective-permute-start.16
  313.3 10.4 %shard_map.42 = (f32[1024,512]{1,0:T(8,128)S(1)}, bf16[1024,512]{1,0:T(8,128)(2,1)S(1)}) custom-call(s32[2]{0:T(128)S(1)} %pad_add_fusion.1.flags, bf16[1024,2048]{1,0:T(8,128)(2,1)} %get-tuple-element.141.refs_0_, bf16[1024,2048]{1,0:T(8,128)(2,1)} %collective-permute-done.4.refs_1_, bf16[1024,2048]{1,0:T(8,128)(2,1)} %collective-permute-done.2.refs_2_, ...), custom_call_target="tpu_custom_call" | custom-call | flops 1048576 | bytes 1048576 | tf_op jit(solution)/shard_map/pallas_call | solution.py:122
  323.7 12.9 %collective-permute-done.14 = bf16[2048,256]{1,0:T(8,128)(2,1)S(1)} collective-permute-done((bf16[2048,256]{1,0:T(8,128)(2,1)}, bf16[2048,256]{1,0:T(8,128)(2,1)S(1)}, u32[]{:S(2)}, u32[]{:S(2)}) %collective-permute-start.14) | collective-permute-done | bytes 1048608 | tf_op jit(solution)/shard_map/ppermute | solution.py:211
  343.0 2.3 collective-permute-start.20
  346.3 2.4 pad_maximum_fusion.one
  348.7 7.6 %shard_map.43 = (f32[1024,256]{1,0:T(8,128)S(1)}, bf16[1024,256]{1,0:T(8,128)(2,1)S(1)}) custom-call(s32[2]{0:T(128)S(1)} %pad_add_fusion.1.flags, bf16[1024,2048]{1,0:T(8,128)(2,1)} %get-tuple-element.141.refs_0_, bf16[1024,2048]{1,0:T(8,128)(2,1)} %collective-permute-done.4.refs_1_, bf16[1024,2048]{1,0:T(8,128)(2,1)} %collective-permute-done.2.refs_2_, ...), custom_call_target="tpu_custom_call" | custom-call | flops 524288 | bytes 524288 | tf_op jit(solution)/shard_map/pallas_call | solution.py:122
  356.3 12.6 %collective-permute-done.18 = bf16[2048,256]{1,0:T(8,128)(2,1)S(1)} collective-permute-done((bf16[2048,256]{1,0:T(8,128)(2,1)}, bf16[2048,256]{1,0:T(8,128)(2,1)S(1)}, u32[]{:S(2)}, u32[]{:S(2)}) %collective-permute-start.18) | collective-permute-done | bytes 1048608 | tf_op jit(solution)/shard_map/ppermute | solution.py:211
  368.9 2.1 select_select_fusion.1.refs_4_
  371.1 2.3 collective-permute-start.26
  373.8 7.6 %shard_map.44 = (f32[1024,256]{1,0:T(8,128)S(1)}, bf16[1024,256]{1,0:T(8,128)(2,1)S(1)}) custom-call(s32[2]{0:T(128)S(1)} %pad_add_fusion.1.flags, bf16[1024,2048]{1,0:T(8,128)(2,1)} %get-tuple-element.141.refs_0_, bf16[1024,2048]{1,0:T(8,128)(2,1)} %collective-permute-done.4.refs_1_, bf16[1024,2048]{1,0:T(8,128)(2,1)} %collective-permute-done.2.refs_2_, ...), custom_call_target="tpu_custom_call" | custom-call | flops 524288 | bytes 524288 | tf_op jit(solution)/shard_map/pallas_call | solution.py:122
  381.4 2.3 collective-permute-start.24
  385.0 3.9 collective-permute-start.28
  389.9 2.1 collective-permute-start.27
  392.0 5.2 %collective-permute-done.24.came = bf16[1024,256]{1,0:T(8,128)(2,1)S(1)} collective-permute-done((bf16[1024,256]{1,0:T(8,128)(2,1)S(1)}, bf16[1024,256]{1,0:T(8,128)(2,1)S(1)}, u32[]{:S(2)}, u32[]{:S(2)}) %collective-permute-start.24) | collective-permute-done | bytes 524320 | tf_op jit(solution)/shard_map/ppermute | solution.py:211
  398.2 3.7 collective-permute-start.25
  402.0 2.2 copy-done.1
  407.0 5.6 %shard_map.45.refs_0_ = f32[1024,2048]{1,0:T(8,128)} custom-call(s32[2]{0:T(128)S(1)} %pad_add_fusion.flags, f32[1024,1024]{1,0:T(8,128)S(1)} %copy-done.1, f32[1024,512]{1,0:T(8,128)S(1)} %copy-done.5, bf16[1024,512]{1,0:T(8,128)(2,1)S(1)} %copy-done.9, bf16[1024,1024]{1,0:T(8,128)(2,1)S(1)} %collective-permute-done.19.far_one, ...), custom_call_target="tpu_custom_call" | custom-call | flops 524288 | bytes 11534336 | tf_op jit(solution)/shard_map/pallas_call | solution.py:164
  412.6 3.3 shard_map.46.refs_0_
  415.9 3.3 shard_map.47
  (91 shorter events, 30.6 us)
Async XLA Ops:
  3.6 2.6 copy-start.16
  3.6 5.2 %copy-start.17 = (bf16[512,256]{1,0:T(8,128)(2,1)S(1)}, bf16[512,256]{1,0:T(8,128)(2,1)}, u32[]{:S(2)}) copy-start(bf16[512,256]{1,0:T(8,128)(2,1)} %param.4) | copy-start | bytes 786436
  6.2 10.1 %collective-permute-start = (bf16[4,256,1024]{2,1,0:T(8,128)(2,1)}, bf16[4,256,1024]{2,1,0:T(8,128)(2,1)S(1)}, u32[]{:S(2)}, u32[]{:S(2)}) collective-permute-start(bf16[4,256,1024]{2,1,0:T(8,128)(2,1)} %slice_bitcast_fusion), channel_id=1, source_target_pairs={{0,8},{8,16},{16,24},{1,9},{9,17},{17,25},{2,10},{10,18},{18,26},{... | collective-permute-start | bytes 6291464 | tf_op jit(solution)/shard_map/ppermute | solution.py:240
  9.8 5.0 %copy-start.18 = (s32[2048]{0:T(1024)S(1)}, s32[2048]{0:T(1024)}, u32[]{:S(2)}) copy-start(s32[2048]{0:T(1024)} %param.5) | copy-start | bytes 24580
  12.0 1.1 slice-start
  24.0 26.4 %collective-permute-start.4 = (bf16[1024,2048]{1,0:T(8,128)(2,1)}, bf16[1024,2048]{1,0:T(8,128)(2,1)}, u32[]{:S(2)}, u32[]{:S(2)}) collective-permute-start(bf16[1024,2048]{1,0:T(8,128)(2,1)} %get-tuple-element.141.refs_0_), channel_id=1, source_target_pairs={{0,8},{1,9},{2,10},{3,11},{4,12},{5,13},{6,14},{7,15},{8,0},{9,1},... | collective-permute-start | bytes 12582920 | tf_op jit(solution)/shard_map/ppermute | solution.py:211
  42.1 92.8 %collective-permute-start.2 = (bf16[1024,2048]{1,0:T(8,128)(2,1)}, bf16[1024,2048]{1,0:T(8,128)(2,1)}, u32[]{:S(2)}, u32[]{:S(2)}) collective-permute-start(bf16[1024,2048]{1,0:T(8,128)(2,1)} %get-tuple-element.141.refs_0_), channel_id=1, source_target_pairs={{0,1},{1,0},{2,3},{3,2},{4,5},{5,4},{6,7},{7,6},{8,9},{9,8},{10,11... | collective-permute-start | bytes 12582920 | tf_op jit(solution)/shard_map/ppermute | solution.py:211
  43.7 93.5 %collective-permute-start.5 = (bf16[2048,1024]{1,0:T(8,128)(2,1)}, bf16[2048,1024]{1,0:T(8,128)(2,1)}, u32[]{:S(2)}, u32[]{:S(2)}) collective-permute-start(bf16[2048,1024]{1,0:T(8,128)(2,1)} %get-tuple-element.86.refs_4_), channel_id=1, source_target_pairs={{0,2},{1,3},{2,4},{3,5},{4,6},{5,7},{8,10},{9,11},{10,12},{11,13},... | collective-permute-start | bytes 12582920 | tf_op jit(solution)/shard_map/ppermute | solution.py:211
  49.1 88.0 %collective-permute-start.3 = (bf16[2048,1024]{1,0:T(8,128)(2,1)}, bf16[2048,1024]{1,0:T(8,128)(2,1)}, u32[]{:S(2)}, u32[]{:S(2)}) collective-permute-start(bf16[2048,1024]{1,0:T(8,128)(2,1)} %get-tuple-element.86.refs_4_), channel_id=1, source_target_pairs={{0,8},{1,9},{2,10},{3,11},{4,12},{5,13},{6,14},{7,15},{8,0},{9,1},... | collective-permute-start | bytes 12582920 | tf_op jit(solution)/shard_map/ppermute | solution.py:211
  49.1 95.2 %collective-permute-start.1 = (bf16[2048,1024]{1,0:T(8,128)(2,1)}, bf16[2048,1024]{1,0:T(8,128)(2,1)}, u32[]{:S(2)}, u32[]{:S(2)}) collective-permute-start(bf16[2048,1024]{1,0:T(8,128)(2,1)} %get-tuple-element.86.refs_4_), channel_id=1, source_target_pairs={{2,0},{3,1},{4,2},{5,3},{6,4},{7,5},{10,8},{11,9},{12,10},{13,11},... | collective-permute-start | bytes 12582920 | tf_op jit(solution)/shard_map/ppermute | solution.py:211
  148.9 7.5 %collective-permute-start.8 = (bf16[2048,1024]{1,0:T(8,128)(2,1)}, bf16[2048,1024]{1,0:T(8,128)(2,1)}, u32[]{:S(2)}, u32[]{:S(2)}) collective-permute-start(bf16[2048,1024]{1,0:T(8,128)(2,1)} %broadcast_select_fusion.1.refs_4_), channel_id=1, source_target_pairs={{0,8},{1,9},{2,10},{3,11},{4,12},{5,13},{6,14},{7,15},{8,0},{9,1},... | collective-permute-start | bytes 12582920 | tf_op jit(solution)/shard_map/ppermute | solution.py:211
  148.9 13.5 %collective-permute-start.7 = (bf16[1024,2048]{1,0:T(8,128)(2,1)}, bf16[1024,2048]{1,0:T(8,128)(2,1)}, u32[]{:S(2)}, u32[]{:S(2)}) collective-permute-start(bf16[1024,2048]{1,0:T(8,128)(2,1)} %collective-permute-done.2.refs_2_), channel_id=1, source_target_pairs={{0,8},{1,9},{2,10},{3,11},{4,12},{5,13},{6,14},{7,15},{8,0},{9,1},... | collective-permute-start | bytes 12582920 | tf_op jit(solution)/shard_map/ppermute | solution.py:211
  149.4 94.7 %collective-permute-start.6 = (bf16[2048,1024]{1,0:T(8,128)(2,1)}, bf16[2048,1024]{1,0:T(8,128)(2,1)}, u32[]{:S(2)}, u32[]{:S(2)}) collective-permute-start(bf16[2048,1024]{1,0:T(8,128)(2,1)} %collective-permute-done.1), channel_id=1, source_target_pairs={{2,0},{3,1},{4,2},{5,3},{10,8},{11,9},{12,10},{13,11},{18,16},{19,... | collective-permute-start | bytes 12582920 | tf_op jit(solution)/shard_map/ppermute | solution.py:211
  150.7 93.4 %collective-permute-start.9 = (bf16[2048,1024]{1,0:T(8,128)(2,1)}, bf16[2048,1024]{1,0:T(8,128)(2,1)}, u32[]{:S(2)}, u32[]{:S(2)}) collective-permute-start(bf16[2048,1024]{1,0:T(8,128)(2,1)} %collective-permute-done.5), channel_id=1, source_target_pairs={{2,4},{3,5},{4,6},{5,7},{10,12},{11,13},{12,14},{13,15},{18,20},{1... | collective-permute-start | bytes 12582920 | tf_op jit(solution)/shard_map/ppermute | solution.py:211
  177.8 2.1 copy-start
  195.2 51.5 %copy-start.3 = (f32[1024,1024]{1,0:T(8,128)}, f32[1024,1024]{1,0:T(8,128)S(1)}, u32[]{:S(2)}) copy-start(f32[1024,1024]{1,0:T(8,128)S(1)} %shard_map.39.refs_6_) | copy-start | bytes 12582916
  246.8 4.6 %copy-start.14 = (bf16[2048,1024]{1,0:T(8,128)(2,1)}, bf16[2048,1024]{1,0:T(8,128)(2,1)S(1)}, u32[]{:S(2)}) copy-start(bf16[2048,1024]{1,0:T(8,128)(2,1)S(1)} %broadcast_select_fusion.refs_4_) | copy-start | bytes 12582916
  246.8 11.1 %collective-permute-start.11 = (bf16[2048,1024]{1,0:T(8,128)(2,1)S(1)}, bf16[2048,1024]{1,0:T(8,128)(2,1)S(1)}, u32[]{:S(2)}, u32[]{:S(2)}) collective-permute-start(bf16[2048,1024]{1,0:T(8,128)(2,1)S(1)} %broadcast_select_fusion.refs_4_), channel_id=1, source_target_pairs={{0,8},{1,9},{2,10},{3,11},{4,12},{5,13},{6,14},{7,15},{8,0},{9,1},... | collective-permute-start | bytes 12582920 | tf_op jit(solution)/shard_map/ppermute | solution.py:211
  254.4 42.5 %collective-permute-start.13 = (bf16[2048,512]{1,0:T(8,128)(2,1)}, bf16[2048,512]{1,0:T(8,128)(2,1)}, u32[]{:S(2)}, u32[]{:S(2)}) collective-permute-start(bf16[2048,512]{1,0:T(8,128)(2,1)} %slice.47), channel_id=1, source_target_pairs={{4,6},{5,7},{12,14},{13,15},{20,22},{21,23},{28,30},{29,31}} | collective-permute-start | bytes 6291464 | tf_op jit(solution)/shard_map/ppermute | solution.py:211
  256.4 49.2 %collective-permute-start.10 = (bf16[2048,512]{1,0:T(8,128)(2,1)}, bf16[2048,512]{1,0:T(8,128)(2,1)}, u32[]{:S(2)}, u32[]{:S(2)}) collective-permute-start(bf16[2048,512]{1,0:T(8,128)(2,1)} %slice.44), channel_id=1, source_target_pairs={{2,0},{3,1},{10,8},{11,9},{18,16},{19,17},{26,24},{27,25}} | collective-permute-start | bytes 6291464 | tf_op jit(solution)/shard_map/ppermute | solution.py:211
  257.9 2.0 copy-start.15
  271.8 24.9 %collective-permute-start.12 = (bf16[1024,512]{1,0:T(8,128)(2,1)}, bf16[1024,512]{1,0:T(8,128)(2,1)S(1)}, u32[]{:S(2)}, u32[]{:S(2)}) collective-permute-start(bf16[1024,512]{1,0:T(8,128)(2,1)} %get-tuple-element.101), channel_id=1, source_target_pairs={{0,16},{1,17},{2,18},{3,19},{4,20},{5,21},{6,22},{7,23},{8,24},{9,... | collective-permute-start | bytes 3145736 | tf_op jit(solution)/shard_map/ppermute | solution.py:211
  308.9 4.4 %collective-permute-start.15 = (bf16[2048,512]{1,0:T(8,128)(2,1)S(1)}, bf16[2048,512]{1,0:T(8,128)(2,1)S(1)}, u32[]{:S(2)}, u32[]{:S(2)}) collective-permute-start(bf16[2048,512]{1,0:T(8,128)(2,1)S(1)} %select_select_fusion.refs_4_), channel_id=1, source_target_pairs={{0,8},{1,9},{2,10},{3,11},{4,12},{5,13},{6,14},{7,15},{8,0},{9,1},... | collective-permute-start | bytes 6291464 | tf_op jit(solution)/shard_map/ppermute | solution.py:211
  308.9 27.7 %collective-permute-start.14 = (bf16[2048,256]{1,0:T(8,128)(2,1)}, bf16[2048,256]{1,0:T(8,128)(2,1)S(1)}, u32[]{:S(2)}, u32[]{:S(2)}) collective-permute-start(bf16[2048,256]{1,0:T(8,128)(2,1)} %get-tuple-element.106), channel_id=1, source_target_pairs={{2,0},{3,1},{10,8},{11,9},{18,16},{19,17},{26,24},{27,25}} | collective-permute-start | bytes 3145736 | tf_op jit(solution)/shard_map/ppermute | solution.py:211
  310.2 26.4 %collective-permute-start.16 = (bf16[1024,512]{1,0:T(8,128)(2,1)S(1)}, bf16[1024,512]{1,0:T(8,128)(2,1)S(1)}, u32[]{:S(2)}, u32[]{:S(2)}) collective-permute-start(bf16[1024,512]{1,0:T(8,128)(2,1)S(1)} %get-tuple-element.116), channel_id=1, source_target_pairs={{0,16},{1,17},{2,18},{3,19},{4,20},{5,21},{6,22},{7,23},{8,24},{9,... | collective-permute-start | bytes 3145736 | tf_op jit(solution)/shard_map/ppermute | solution.py:211
  312.6 24.0 %collective-permute-start.17 = (bf16[2048,256]{1,0:T(8,128)(2,1)S(1)}, bf16[2048,256]{1,0:T(8,128)(2,1)S(1)}, u32[]{:S(2)}, u32[]{:S(2)}) collective-permute-start(bf16[2048,256]{1,0:T(8,128)(2,1)S(1)} %get-tuple-element.120), channel_id=1, source_target_pairs={{4,6},{5,7},{12,14},{13,15},{20,22},{21,23},{28,30},{29,31}} | collective-permute-start | bytes 3145736 | tf_op jit(solution)/shard_map/ppermute | solution.py:211
  323.7 60.0 %copy-start.4 = (f32[1024,512]{1,0:T(8,128)}, f32[1024,512]{1,0:T(8,128)S(1)}, u32[]{:S(2)}) copy-start(f32[1024,512]{1,0:T(8,128)S(1)} %get-tuple-element.155.keep) | copy-start | bytes 6291460
  337.2 31.7 %collective-permute-start.19 = (bf16[1024,1024]{1,0:T(8,128)(2,1)S(1)}, bf16[1024,1024]{1,0:T(8,128)(2,1)S(1)}, u32[]{:S(2)}, u32[]{:S(2)}) collective-permute-start(bf16[1024,1024]{1,0:T(8,128)(2,1)S(1)} %fusion), channel_id=1, source_target_pairs={{2,11},{3,10},{6,15},{7,14},{8,1},{9,0},{12,5},{13,4},{18,27},{19,... | collective-permute-start | bytes 6291464 | tf_op jit(solution)/shard_map/ppermute | solution.py:211
  340.3 8.4 %collective-permute-start.21 = (bf16[2048,256]{1,0:T(8,128)(2,1)S(1)}, bf16[2048,256]{1,0:T(8,128)(2,1)S(1)}, u32[]{:S(2)}, u32[]{:S(2)}) collective-permute-start(bf16[2048,256]{1,0:T(8,128)(2,1)S(1)} %select_select_fusion.2.refs_4_), channel_id=1, source_target_pairs={{0,8},{1,9},{2,10},{3,11},{4,12},{5,13},{6,14},{7,15},{8,0},{9,1},... | collective-permute-start | bytes 3145736 | tf_op jit(solution)/shard_map/ppermute | solution.py:211
  341.7 27.2 %collective-permute-start.18 = (bf16[2048,256]{1,0:T(8,128)(2,1)}, bf16[2048,256]{1,0:T(8,128)(2,1)S(1)}, u32[]{:S(2)}, u32[]{:S(2)}) collective-permute-start(bf16[2048,256]{1,0:T(8,128)(2,1)} %get-tuple-element.124), channel_id=1, source_target_pairs={{2,0},{3,1},{10,8},{11,9},{18,16},{19,17},{26,24},{27,25}} | collective-permute-start | bytes 3145736 | tf_op jit(solution)/shard_map/ppermute | solution.py:211
  343.0 25.9 %collective-permute-start.20 = (bf16[1024,512]{1,0:T(8,128)(2,1)S(1)}, bf16[1024,512]{1,0:T(8,128)(2,1)S(1)}, u32[]{:S(2)}, u32[]{:S(2)}) collective-permute-start(bf16[1024,512]{1,0:T(8,128)(2,1)S(1)} %get-tuple-element.130), channel_id=1, source_target_pairs={{0,16},{1,17},{2,18},{3,19},{4,20},{5,21},{6,22},{7,23},{8,24},{9,... | collective-permute-start | bytes 3145736 | tf_op jit(solution)/shard_map/ppermute | solution.py:211
  345.3 23.6 %collective-permute-start.22 = (bf16[2048,256]{1,0:T(8,128)(2,1)}, bf16[2048,256]{1,0:T(8,128)(2,1)S(1)}, u32[]{:S(2)}, u32[]{:S(2)}) collective-permute-start(bf16[2048,256]{1,0:T(8,128)(2,1)} %get-tuple-element.139), channel_id=1, source_target_pairs={{4,6},{5,7},{12,14},{13,15},{20,22},{21,23},{28,30},{29,31}} | collective-permute-start | bytes 3145736 | tf_op jit(solution)/shard_map/ppermute | solution.py:211
  368.9 14.8 %copy-start.8 = (bf16[1024,512]{1,0:T(8,128)(2,1)}, bf16[1024,512]{1,0:T(8,128)(2,1)S(1)}, u32[]{:S(2)}) copy-start(bf16[1024,512]{1,0:T(8,128)(2,1)S(1)} %collective-permute-done.20.came) | copy-start | bytes 3145732
  371.0 2.7 collective-permute-start.23
  371.1 17.8 %collective-permute-start.26 = (bf16[1024,256]{1,0:T(8,128)(2,1)S(1)}, bf16[1024,256]{1,0:T(8,128)(2,1)S(1)}, u32[]{:S(2)}, u32[]{:S(2)}) collective-permute-start(bf16[1024,256]{1,0:T(8,128)(2,1)S(1)} %get-tuple-element.154), channel_id=1, source_target_pairs={{0,16},{1,17},{2,18},{3,19},{4,20},{5,21},{6,22},{7,23},{8,24},{9,... | collective-permute-start | bytes 1572872 | tf_op jit(solution)/shard_map/ppermute | solution.py:211
  381.4 15.9 %copy-start.6 = (f32[1024,256]{1,0:T(8,128)}, f32[1024,256]{1,0:T(8,128)S(1)}, u32[]{:S(2)}) copy-start(f32[1024,256]{1,0:T(8,128)S(1)} %get-tuple-element.150.keep) | copy-start | bytes 3145732
  381.4 15.8 %collective-permute-start.24 = (bf16[1024,256]{1,0:T(8,128)(2,1)S(1)}, bf16[1024,256]{1,0:T(8,128)(2,1)S(1)}, u32[]{:S(2)}, u32[]{:S(2)}) collective-permute-start(bf16[1024,256]{1,0:T(8,128)(2,1)S(1)} %get-tuple-element.151), channel_id=1, source_target_pairs={{0,16},{1,17},{2,18},{3,19},{4,20},{5,21},{6,22},{7,23},{8,24},{9,... | collective-permute-start | bytes 1572872 | tf_op jit(solution)/shard_map/ppermute | solution.py:211
  385.0 16.9 %collective-permute-start.28 = (bf16[1024,512]{1,0:T(8,128)(2,1)}, bf16[1024,512]{1,0:T(8,128)(2,1)}, u32[]{:S(2)}, u32[]{:S(2)}) collective-permute-start(bf16[1024,512]{1,0:T(8,128)(2,1)} %add_convert_fusion), channel_id=1, source_target_pairs={{0,9},{1,8},{4,13},{5,12},{10,3},{11,2},{14,7},{15,6},{16,25},{17,... | collective-permute-start | bytes 3145736 | tf_op jit(solution)/shard_map/ppermute | solution.py:211
  388.9 9.3 %copy-start.10 = (bf16[1024,256]{1,0:T(8,128)(2,1)}, bf16[1024,256]{1,0:T(8,128)(2,1)S(1)}, u32[]{:S(2)}) copy-start(bf16[1024,256]{1,0:T(8,128)(2,1)S(1)} %collective-permute-done.26.came) | copy-start | bytes 1572868
  389.9 22.7 %collective-permute-start.27 = (bf16[1024,256]{1,0:T(8,128)(2,1)}, bf16[1024,256]{1,0:T(8,128)(2,1)}, u32[]{:S(2)}, u32[]{:S(2)}) collective-permute-start(bf16[1024,256]{1,0:T(8,128)(2,1)} %add_convert_fusion.1), channel_id=1, source_target_pairs={{0,9},{1,8},{4,13},{5,12},{10,3},{11,2},{14,7},{15,6},{16,25},{17,... | collective-permute-start | bytes 1572872 | tf_op jit(solution)/shard_map/ppermute | solution.py:211
  398.2 17.7 %collective-permute-start.25 = (bf16[1024,256]{1,0:T(8,128)(2,1)}, bf16[1024,256]{1,0:T(8,128)(2,1)}, u32[]{:S(2)}, u32[]{:S(2)}) collective-permute-start(bf16[1024,256]{1,0:T(8,128)(2,1)} %add_convert_fusion.2), channel_id=1, source_target_pairs={{0,9},{1,8},{4,13},{5,12},{10,3},{11,2},{14,7},{15,6},{16,25},{17,... | collective-permute-start | bytes 1572872 | tf_op jit(solution)/shard_map/ppermute | solution.py:211
  402.0 2.2 copy-start.1
  404.1 1.6 copy-start.5
  405.7 1.2 copy-start.9
  407.0 5.6 %copy-start.2 = (f32[1024,1024]{1,0:T(8,128)S(1)}, f32[1024,1024]{1,0:T(8,128)}, u32[]{:S(2)}) copy-start(f32[1024,1024]{1,0:T(8,128)} %pad_maximum_fusion.one) | copy-start | bytes 12582916
  407.0 5.6 %copy-start.11 = (bf16[1024,256]{1,0:T(8,128)(2,1)S(1)}, bf16[1024,256]{1,0:T(8,128)(2,1)}, u32[]{:S(2)}) copy-start(bf16[1024,256]{1,0:T(8,128)(2,1)} %copy-done.10) | copy-start | bytes 1572868
  412.5 3.3 copy-start.7
  412.5 3.3 copy-start.13
  (1 other events, 1.0 us)

commit v4 on v3

--- a/solution.py
+++ b/solution.py
@@ -46,38 +46,74 @@
     return lax.psum_scatter(term, "arc", scatter_dimension=1, tiled=True)
 
 
-def filter_kernel(weight, behind, here, straight, turned):
-    band = behind.shape[1]
-    found = jnp.dot(weight[:, :band], behind[0], preferred_element_type=jnp.float32)
-    found += jnp.dot(weight[:, band:], here[0], preferred_element_type=jnp.float32)
-    found = found.astype(jnp.bfloat16)
-    straight[...] = found
+def filter_kernel(weight, taken, *refs):
+    rows, turned = refs[-2:]
+    found = jnp.dot(weight[...], taken[0], preferred_element_type=jnp.float32).astype(jnp.bfloat16)
+    rows[...] = found
     turned[...] = found.T
 
 
-def filter_rows(weight, behind, here):
-    channels, count, width = here.shape
-    band = behind.shape[1]
+def filter_half(weight, taken, place, held=()):
+    channels, lags, width = taken.shape
+    count = weight.shape[0]
+    half = channels * count
     return pl.pallas_call(
         filter_kernel,
         out_shape=(
-            jax.ShapeDtypeStruct((channels * count, width), jnp.bfloat16),
-            jax.ShapeDtypeStruct((width, channels * count), jnp.bfloat16),
+            jax.ShapeDtypeStruct((2 * half, width), jnp.bfloat16),
+            jax.ShapeDtypeStruct((width, 2 * half), jnp.bfloat16),
         ),
         grid=(channels,),
         in_specs=[
-            pl.BlockSpec((count, band + count), lambda c: (0, 0)),
-            pl.BlockSpec((1, band, width), lambda c: (c, 0, 0)),
-            pl.BlockSpec((1, count, width), lambda c: (c, 0, 0)),
-        ],
-        out_specs=(pl.BlockSpec((count, width), lambda c: (c, 0)), pl.BlockSpec((width, count), lambda c: (0, c))),
+            pl.BlockSpec((count, lags), lambda c: (0, 0)),
+            pl.BlockSpec((1, lags, width), lambda c: (c, 0, 0)),
+        ]
+        + [pl.BlockSpec(memory_space=pl.ANY)] * len(held),
+        out_specs=(
+            pl.BlockSpec((count, width), lambda c: (place * channels + c, 0)),
+            pl.BlockSpec((width, count), lambda c: (0, place * channels + c)),
+        ),
+        input_output_aliases={2 + i: i for i in range(len(held))},
         compiler_params=pltpu.CompilerParams(vmem_limit_bytes=40 << 20),
         cost_estimate=pl.CostEstimate(
-            flops=2 * count * (band + count) * width * channels,
-            bytes_accessed=2 * channels * width * (band + 3 * count),
+            flops=2 * count * lags * width * channels,
+            bytes_accessed=2 * channels * width * (lags + 2 * count),
             transcendentals=0,
         ),
-    )(weight, behind, here)
+    )(weight, taken, *held)
+
+
+def cut_kernel(flags, up, down, over, *pieces):
+    over[...] = jnp.where(flags[0] == 1, down[...], up[...])
+    count = len(pieces) // 2
+    for source, group in ((up, pieces[:count]), (down, pieces[count:])):
+        start = 0
+        for piece in group:
+            part = piece.shape[1]
+            piece[...] = source[:, start : start + part]
+            start += part
+
+
+def cut_out(from_above, up, down, parts):
+    rows, width = up.shape
+    tall = rows // 4
+
+    def spec(part):
+        return pl.BlockSpec((tall, part), lambda i, w: (i, 0))
+
+    found = pl.pallas_call(
+        cut_kernel,
+        out_shape=[jax.ShapeDtypeStruct((rows, part), up.dtype) for part in (width, *parts, *parts)],
+        grid_spec=pltpu.PrefetchScalarGridSpec(
+            num_scalar_prefetch=1,
+            grid=(rows // tall,),
+            in_specs=[spec(width)] * 2,
+            out_specs=[spec(part) for part in (width, *parts, *parts)],
+        ),
+        compiler_params=pltpu.CompilerParams(vmem_limit_bytes=40 << 20),
+        cost_estimate=pl.CostEstimate(flops=rows, bytes_accessed=10 * rows * width, transcendentals=0),
+    )(from_above, up, down)
+    return found[0], found[1 : 1 + len(parts)], found[1 + len(parts) :]
 
 
 def product_kernel(flags, *refs):
@@ -237,8 +273,11 @@
     low, even_spot = spot < SPOTS // 2, spot % 2 == 0
 
     weight = band_weights(coef, arc_ids, epochs_here)
-    behind = lax.ppermute(jnp.swapaxes(partials[cut:], 0, 1), "arc", [(a, a + 1) for a in range(arcs - 1)])
-    v["own"], v["own_t"] = filter_rows(weight, behind, jnp.swapaxes(partials, 0, 1))
+    behind = lax.ppermute(partials[cut:], "arc", [(a, a + 1) for a in range(arcs - 1)])
+    here = jnp.swapaxes(partials, 0, 1)
+    held = filter_half(weight[band:, band:], here, 0)
+    first = jnp.concatenate([jnp.swapaxes(behind, 0, 1), here[:, :band]], 1)
+    v["own"], v["own_t"] = filter_half(weight[:band, : 2 * band], first, 1, held)
     v["up1"], v["down1"] = hop(v["own"], 1, 1), hop(v["own"], 1, -1)
     v["far_t"] = sides(v["own_t"])
     v["own_o"], v["own_to"] = cores(v["own"]), cores(v["own_t"])

time: 420 us -> 418 us (level)
    ppermute x28, starting transfers between devices: 62.8 us -> 57.3 us  [send(): return lax.ppermute(value, AXES, pairs(arcs, cols, target))]
    unnamed x39 -> x46, local copies, waits for them, and re-layouts: 13.8 us -> 17.4 us
  transfers between devices with their start and end apart: 29 -> 29, of which waited for: 12 -> 13; matrix products, arithmetic and copies ran while one was open for 6% -> 7% of each run, Pallas kernels for 21% -> 22%
where the time goes in v4:
time: 418 us; the launch traced here: 416 us
  waiting for transfers between devices  196 us (47%)
  Pallas kernels  98.1 us (23%)
  starting transfers between devices  61.1 us (15%)
  local copies, waits for them, and re-layouts  35.5 us (8%)
  other arithmetic  24.9 us (6%)
    ppermute x28, waiting for transfers between devices, send(): return lax.ppermute(value, AXES, pairs(arcs, cols, target))  196 us
    pallas_call x7, Pallas kernels, products(): pl.pallas_call(product_kernel, out_shape=whole if first is None else (who...  79.2 us
    ppermute x28, starting transfers between devices, send(): return lax.ppermute(value, AXES, pairs(arcs, cols, target))  57.3 us
    unnamed x46, local copies, waits for them, and re-layouts  17.4 us
    pallas_call x3, Pallas kernels, place(): pl.pallas_call(place_kernel, out_shape=jax.ShapeDtypeStruct((rows, 2 * wi...  12 us
  transfers between devices with their start and end apart: 29, of which 13 were waited for; matrix products, arithmetic and copies ran while one was open for 7% of the time, Pallas kernels for 22%

profile of v4, /device:TPU:0, one launch (start us, length us, event | category | flops | bytes accessed | tf_op | source)
XLA Modules:
  0.0 416.1 jit_solution(2745135364358413857)
XLA Ops:
  1.6 2.0 copy.13
  3.6 3.7 collective-permute-start
  7.3 3.4 copy.14
  16.7 3.4 shard_map.37
  20.1 2.0 pad_maximum_fusion.taken
  22.2 3.5 shard_map.38
  25.6 11.7 %collective-permute-start.4 = (bf16[1024,2048]{1,0:T(8,128)(2,1)}, bf16[1024,2048]{1,0:T(8,128)(2,1)}, u32[]{:S(2)}, u32[]{:S(2)}) collective-permute-start(bf16[1024,2048]{1,0:T(8,128)(2,1)} %get-tuple-element.145.refs_0_), channel_id=1, source_target_pairs={{0,8},{1,9},{2,10},{3,11},{4,12},{5,13},{6,14},{7,15},{8,0},{9,1},... | collective-permute-start | bytes 12582920 | tf_op jit(solution)/shard_map/ppermute | solution.py:247
  38.8 5.4 %collective-permute-start.5 = (bf16[2048,1024]{1,0:T(8,128)(2,1)}, bf16[2048,1024]{1,0:T(8,128)(2,1)}, u32[]{:S(2)}, u32[]{:S(2)}) collective-permute-start(bf16[2048,1024]{1,0:T(8,128)(2,1)} %get-tuple-element.90.refs_4_), channel_id=1, source_target_pairs={{0,2},{1,3},{2,4},{3,5},{4,6},{5,7},{8,10},{9,11},{10,12},{11,13},... | collective-permute-start | bytes 12582920 | tf_op jit(solution)/shard_map/ppermute | solution.py:247
  45.6 84.5 %collective-permute-done.2.refs_2_ = bf16[1024,2048]{1,0:T(8,128)(2,1)} collective-permute-done((bf16[1024,2048]{1,0:T(8,128)(2,1)}, bf16[1024,2048]{1,0:T(8,128)(2,1)}, u32[]{:S(2)}, u32[]{:S(2)}) %collective-permute-start.2) | collective-permute-done | bytes 4194336 | tf_op jit(solution)/shard_map/ppermute | solution.py:247
  130.1 2.2 collective-permute-done.5
  132.3 7.1 %collective-permute-done.1 = bf16[2048,1024]{1,0:T(8,128)(2,1)} collective-permute-done((bf16[2048,1024]{1,0:T(8,128)(2,1)}, bf16[2048,1024]{1,0:T(8,128)(2,1)}, u32[]{:S(2)}, u32[]{:S(2)}) %collective-permute-start.1) | collective-permute-done | bytes 4194336 | tf_op jit(solution)/shard_map/ppermute | solution.py:247
  139.4 4.6 %broadcast_select_fusion.1.refs_4_ = bf16[2048,1024]{1,0:T(8,128)(2,1)} fusion(bf16[2048,1024]{1,0:T(8,128)(2,1)} %collective-permute-done.1, bf16[2048,1024]{1,0:T(8,128)(2,1)} %collective-permute-done.5, pred[]{:T(512)S(6)} %lt.29), kind=kLoop, calls=%fused_computation.3 | loop fusion | flops 2097152 | bytes 12582913 | tf_op jit(solution)/shard_map/jit(_where)/select_n | solution.py:292
  145.9 2.6 collective-permute-start.9
  148.6 2.9 collective-permute-done.8.refs_5_
  151.6 6.0 %collective-permute-done.7.refs_3_ = bf16[1024,2048]{1,0:T(8,128)(2,1)} collective-permute-done((bf16[1024,2048]{1,0:T(8,128)(2,1)}, bf16[1024,2048]{1,0:T(8,128)(2,1)}, u32[]{:S(2)}, u32[]{:S(2)}) %collective-permute-start.7) | collective-permute-done | bytes 4194336 | tf_op jit(solution)/shard_map/ppermute | solution.py:247
  157.6 15.4 %shard_map.39.refs_6_ = f32[1024,1024]{1,0:T(8,128)S(1)} custom-call(s32[2]{0:T(128)S(1)} %pad_add_fusion.1.flags, bf16[1024,2048]{1,0:T(8,128)(2,1)} %get-tuple-element.145.refs_0_, bf16[1024,2048]{1,0:T(8,128)(2,1)} %collective-permute-done.4.refs_1_, bf16[1024,2048]{1,0:T(8,128)(2,1)} %collective-permute-done.2.refs_2_, ...), custom_call_target="tpu_custom_call" | custom-call | flops 2097152 | bytes 2097152 | tf_op jit(solution)/shard_map/pallas_call | solution.py:158
  172.9 2.0 copy-done
  174.9 15.3 %shard_map.40.refs_6_ = f32[1024,1024]{1,0:T(8,128)S(1)} custom-call(s32[2]{0:T(128)S(1)} %pad_add_fusion.2.flags, bf16[1024,2048]{1,0:T(8,128)(2,1)} %get-tuple-element.145.refs_0_, bf16[1024,2048]{1,0:T(8,128)(2,1)} %collective-permute-done.4.refs_1_, bf16[1024,2048]{1,0:T(8,128)(2,1)} %collective-permute-done.2.refs_2_, ...), custom_call_target="tpu_custom_call" | custom-call | flops 2097152 | bytes 2097152 | tf_op jit(solution)/shard_map/pallas_call | solution.py:158
  190.3 49.0 %collective-permute-done.6 = bf16[2048,1024]{1,0:T(8,128)(2,1)} collective-permute-done((bf16[2048,1024]{1,0:T(8,128)(2,1)}, bf16[2048,1024]{1,0:T(8,128)(2,1)}, u32[]{:S(2)}, u32[]{:S(2)}) %collective-permute-start.6) | collective-permute-done | bytes 4194336 | tf_op jit(solution)/shard_map/ppermute | solution.py:247
  239.2 2.6 broadcast_select_fusion.refs_4_
  242.0 4.5 %slice.56 = bf16[2048,512]{1,0:T(8,128)(2,1)} slice(bf16[2048,1024]{1,0:T(8,128)(2,1)} %collective-permute-done.6), slice={[0:2048], [0:512]} | slice | bytes 4194304 | tf_op jit(solution)/shard_map/slice | solution.py:312
  246.5 3.1 slice.59
  254.8 11.8 %shard_map.42 = (f32[1024,512]{1,0:T(8,128)S(1)}, bf16[1024,512]{1,0:T(8,128)(2,1)}) custom-call(s32[2]{0:T(128)S(1)} %pad_add_fusion.2.flags, bf16[1024,2048]{1,0:T(8,128)(2,1)} %get-tuple-element.145.refs_0_, bf16[1024,2048]{1,0:T(8,128)(2,1)} %collective-permute-done.4.refs_1_, bf16[1024,2048]{1,0:T(8,128)(2,1)} %collective-permute-done.2.refs_2_, ...), custom_call_target="tpu_custom_call" | custom-call | flops 1048576 | bytes 1048576 | tf_op jit(solution)/shard_map/pallas_call | solution.py:158
  266.6 2.4 collective-permute-start.12
  269.1 3.8 fusion.1
  272.9 11.1 %shard_map.41 = (f32[1024,512]{1,0:T(8,128)S(1)}, bf16[1024,512]{1,0:T(8,128)(2,1)S(1)}) custom-call(s32[2]{0:T(128)S(1)} %pad_add_fusion.2.flags, bf16[1024,2048]{1,0:T(8,128)(2,1)} %get-tuple-element.145.refs_0_, bf16[1024,2048]{1,0:T(8,128)(2,1)} %collective-permute-done.4.refs_1_, bf16[1024,2048]{1,0:T(8,128)(2,1)} %collective-permute-done.2.refs_2_, ...), custom_call_target="tpu_custom_call" | custom-call | flops 1048576 | bytes 1048576 | tf_op jit(solution)/shard_map/pallas_call | solution.py:158
  284.0 7.8 %collective-permute-done.12 = bf16[1024,512]{1,0:T(8,128)(2,1)} collective-permute-done((bf16[1024,512]{1,0:T(8,128)(2,1)}, bf16[1024,512]{1,0:T(8,128)(2,1)}, u32[]{:S(2)}, u32[]{:S(2)}) %collective-permute-start.12) | collective-permute-done | bytes 1048608 | tf_op jit(solution)/shard_map/ppermute | solution.py:247
  293.3 7.6 %collective-permute-done.10 = bf16[2048,512]{1,0:T(8,128)(2,1)} collective-permute-done((bf16[2048,512]{1,0:T(8,128)(2,1)}, bf16[2048,512]{1,0:T(8,128)(2,1)}, u32[]{:S(2)}, u32[]{:S(2)}) %collective-permute-start.10) | collective-permute-done | bytes 2097184 | tf_op jit(solution)/shard_map/ppermute | solution.py:247
  300.9 3.2 select_select_fusion.refs_4_
  305.5 2.4 collective-permute-start.16
  308.9 10.4 %shard_map.43 = (f32[1024,512]{1,0:T(8,128)S(1)}, bf16[1024,512]{1,0:T(8,128)(2,1)S(1)}) custom-call(s32[2]{0:T(128)S(1)} %pad_add_fusion.1.flags, bf16[1024,2048]{1,0:T(8,128)(2,1)} %get-tuple-element.145.refs_0_, bf16[1024,2048]{1,0:T(8,128)(2,1)} %collective-permute-done.4.refs_1_, bf16[1024,2048]{1,0:T(8,128)(2,1)} %collective-permute-done.2.refs_2_, ...), custom_call_target="tpu_custom_call" | custom-call | flops 1048576 | bytes 1048576 | tf_op jit(solution)/shard_map/pallas_call | solution.py:158
  319.3 12.4 %collective-permute-done.14 = bf16[2048,256]{1,0:T(8,128)(2,1)S(1)} collective-permute-done((bf16[2048,256]{1,0:T(8,128)(2,1)S(1)}, bf16[2048,256]{1,0:T(8,128)(2,1)S(1)}, u32[]{:S(2)}, u32[]{:S(2)}) %collective-permute-start.14) | collective-permute-done | bytes 1048608 | tf_op jit(solution)/shard_map/ppermute | solution.py:247
  339.3 2.3 collective-permute-start.20
  343.3 2.5 pad_maximum_fusion.1.one
  345.8 7.6 %shard_map.44 = (f32[1024,256]{1,0:T(8,128)S(1)}, bf16[1024,256]{1,0:T(8,128)(2,1)S(1)}) custom-call(s32[2]{0:T(128)S(1)} %pad_add_fusion.1.flags, bf16[1024,2048]{1,0:T(8,128)(2,1)} %get-tuple-element.145.refs_0_, bf16[1024,2048]{1,0:T(8,128)(2,1)} %collective-permute-done.4.refs_1_, bf16[1024,2048]{1,0:T(8,128)(2,1)} %collective-permute-done.2.refs_2_, ...), custom_call_target="tpu_custom_call" | custom-call | flops 524288 | bytes 524288 | tf_op jit(solution)/shard_map/pallas_call | solution.py:158
  353.4 11.8 %collective-permute-done.18 = bf16[2048,256]{1,0:T(8,128)(2,1)S(1)} collective-permute-done((bf16[2048,256]{1,0:T(8,128)(2,1)}, bf16[2048,256]{1,0:T(8,128)(2,1)S(1)}, u32[]{:S(2)}, u32[]{:S(2)}) %collective-permute-start.18) | collective-permute-done | bytes 1048608 | tf_op jit(solution)/shard_map/ppermute | solution.py:247
  365.2 2.1 select_select_fusion.1.refs_4_
  367.4 2.3 collective-permute-start.26
  370.1 7.6 %shard_map.45 = (f32[1024,256]{1,0:T(8,128)S(1)}, bf16[1024,256]{1,0:T(8,128)(2,1)S(1)}) custom-call(s32[2]{0:T(128)S(1)} %pad_add_fusion.1.flags, bf16[1024,2048]{1,0:T(8,128)(2,1)} %get-tuple-element.145.refs_0_, bf16[1024,2048]{1,0:T(8,128)(2,1)} %collective-permute-done.4.refs_1_, bf16[1024,2048]{1,0:T(8,128)(2,1)} %collective-permute-done.2.refs_2_, ...), custom_call_target="tpu_custom_call" | custom-call | flops 524288 | bytes 524288 | tf_op jit(solution)/shard_map/pallas_call | solution.py:158
  377.7 2.3 collective-permute-start.24
  381.4 3.9 collective-permute-start.28
  387.1 2.1 collective-permute-start.27
  389.2 4.3 %collective-permute-done.24.came = bf16[1024,256]{1,0:T(8,128)(2,1)S(1)} collective-permute-done((bf16[1024,256]{1,0:T(8,128)(2,1)S(1)}, bf16[1024,256]{1,0:T(8,128)(2,1)S(1)}, u32[]{:S(2)}, u32[]{:S(2)}) %collective-permute-start.24) | collective-permute-done | bytes 524320 | tf_op jit(solution)/shard_map/ppermute | solution.py:247
  395.2 3.7 collective-permute-start.25
  399.0 2.2 copy-done.1
  404.0 5.6 %shard_map.46.refs_0_ = f32[1024,2048]{1,0:T(8,128)} custom-call(s32[2]{0:T(128)S(1)} %pad_add_fusion.flags, f32[1024,1024]{1,0:T(8,128)S(1)} %copy-done.1, f32[1024,512]{1,0:T(8,128)S(1)} %copy-done.6, bf16[1024,512]{1,0:T(8,128)(2,1)S(1)} %copy-done.10, bf16[1024,1024]{1,0:T(8,128)(2,1)S(1)} %collective-permute-done.19.far_one, ...), custom_call_target="tpu_custom_call" | custom-call | flops 524288 | bytes 11534336 | tf_op jit(solution)/shard_map/pallas_call | solution.py:200
  409.6 3.2 shard_map.47.refs_0_
  412.8 3.2 shard_map.48
  (102 shorter events, 38.9 us)
Async XLA Ops:
  0.0 1.6 slice-start
  0.0 7.3 %copy-start.17 = (bf16[512,4,1024]{2,1,0:T(4,128)(2,1)S(1)}, bf16[512,4,1024]{2,1,0:T(4,128)(2,1)}, u32[]{:S(2)}) copy-start(bf16[512,4,1024]{2,1,0:T(4,128)(2,1)} %param.3) | copy-start | bytes 12582916
  3.6 16.5 %collective-permute-start = (bf16[256,4,1024]{2,0,1:T(8,128)(2,1)}, bf16[256,4,1024]{2,0,1:T(8,128)(2,1)}, u32[]{:S(2)}, u32[]{:S(2)}) collective-permute-start(bf16[256,4,1024]{2,0,1:T(8,128)(2,1)} %copy.13), channel_id=1, source_target_pairs={{0,8},{8,16},{16,24},{1,9},{9,17},{17,25},{2,10},{10,18},{18,26},{... | collective-permute-start | bytes 6291464 | tf_op jit(solution)/shard_map/ppermute | solution.py:276
  7.3 3.5 copy-start.20
  11.8 4.0 copy-start.21
  13.9 2.8 copy-start.4
  25.6 19.9 %collective-permute-start.4 = (bf16[1024,2048]{1,0:T(8,128)(2,1)}, bf16[1024,2048]{1,0:T(8,128)(2,1)}, u32[]{:S(2)}, u32[]{:S(2)}) collective-permute-start(bf16[1024,2048]{1,0:T(8,128)(2,1)} %get-tuple-element.145.refs_0_), channel_id=1, source_target_pairs={{0,8},{1,9},{2,10},{3,11},{4,12},{5,13},{6,14},{7,15},{8,0},{9,1},... | collective-permute-start | bytes 12582920 | tf_op jit(solution)/shard_map/ppermute | solution.py:247
  37.3 92.8 %collective-permute-start.2 = (bf16[1024,2048]{1,0:T(8,128)(2,1)}, bf16[1024,2048]{1,0:T(8,128)(2,1)}, u32[]{:S(2)}, u32[]{:S(2)}) collective-permute-start(bf16[1024,2048]{1,0:T(8,128)(2,1)} %get-tuple-element.145.refs_0_), channel_id=1, source_target_pairs={{0,1},{1,0},{2,3},{3,2},{4,5},{5,4},{6,7},{7,6},{8,9},{9,8},{10,11... | collective-permute-start | bytes 12582920 | tf_op jit(solution)/shard_map/ppermute | solution.py:247
  38.8 93.5 %collective-permute-start.5 = (bf16[2048,1024]{1,0:T(8,128)(2,1)}, bf16[2048,1024]{1,0:T(8,128)(2,1)}, u32[]{:S(2)}, u32[]{:S(2)}) collective-permute-start(bf16[2048,1024]{1,0:T(8,128)(2,1)} %get-tuple-element.90.refs_4_), channel_id=1, source_target_pairs={{0,2},{1,3},{2,4},{3,5},{4,6},{5,7},{8,10},{9,11},{10,12},{11,13},... | collective-permute-start | bytes 12582920 | tf_op jit(solution)/shard_map/ppermute | solution.py:247
  44.2 88.1 %collective-permute-start.3 = (bf16[2048,1024]{1,0:T(8,128)(2,1)}, bf16[2048,1024]{1,0:T(8,128)(2,1)}, u32[]{:S(2)}, u32[]{:S(2)}) collective-permute-start(bf16[2048,1024]{1,0:T(8,128)(2,1)} %get-tuple-element.90.refs_4_), channel_id=1, source_target_pairs={{0,8},{1,9},{2,10},{3,11},{4,12},{5,13},{6,14},{7,15},{8,0},{9,1},... | collective-permute-start | bytes 12582920 | tf_op jit(solution)/shard_map/ppermute | solution.py:247
  44.2 95.2 %collective-permute-start.1 = (bf16[2048,1024]{1,0:T(8,128)(2,1)}, bf16[2048,1024]{1,0:T(8,128)(2,1)}, u32[]{:S(2)}, u32[]{:S(2)}) collective-permute-start(bf16[2048,1024]{1,0:T(8,128)(2,1)} %get-tuple-element.90.refs_4_), channel_id=1, source_target_pairs={{2,0},{3,1},{4,2},{5,3},{6,4},{7,5},{10,8},{11,9},{12,10},{13,11},... | collective-permute-start | bytes 12582920 | tf_op jit(solution)/shard_map/ppermute | solution.py:247
  144.1 7.5 %collective-permute-start.8 = (bf16[2048,1024]{1,0:T(8,128)(2,1)}, bf16[2048,1024]{1,0:T(8,128)(2,1)}, u32[]{:S(2)}, u32[]{:S(2)}) collective-permute-start(bf16[2048,1024]{1,0:T(8,128)(2,1)} %broadcast_select_fusion.1.refs_4_), channel_id=1, source_target_pairs={{0,8},{1,9},{2,10},{3,11},{4,12},{5,13},{6,14},{7,15},{8,0},{9,1},... | collective-permute-start | bytes 12582920 | tf_op jit(solution)/shard_map/ppermute | solution.py:247
  144.1 13.5 %collective-permute-start.7 = (bf16[1024,2048]{1,0:T(8,128)(2,1)}, bf16[1024,2048]{1,0:T(8,128)(2,1)}, u32[]{:S(2)}, u32[]{:S(2)}) collective-permute-start(bf16[1024,2048]{1,0:T(8,128)(2,1)} %collective-permute-done.2.refs_2_), channel_id=1, source_target_pairs={{0,8},{1,9},{2,10},{3,11},{4,12},{5,13},{6,14},{7,15},{8,0},{9,1},... | collective-permute-start | bytes 12582920 | tf_op jit(solution)/shard_map/ppermute | solution.py:247
  144.6 94.7 %collective-permute-start.6 = (bf16[2048,1024]{1,0:T(8,128)(2,1)}, bf16[2048,1024]{1,0:T(8,128)(2,1)}, u32[]{:S(2)}, u32[]{:S(2)}) collective-permute-start(bf16[2048,1024]{1,0:T(8,128)(2,1)} %collective-permute-done.1), channel_id=1, source_target_pairs={{2,0},{3,1},{4,2},{5,3},{10,8},{11,9},{12,10},{13,11},{18,16},{19,... | collective-permute-start | bytes 12582920 | tf_op jit(solution)/shard_map/ppermute | solution.py:247
  145.9 93.4 %collective-permute-start.9 = (bf16[2048,1024]{1,0:T(8,128)(2,1)}, bf16[2048,1024]{1,0:T(8,128)(2,1)}, u32[]{:S(2)}, u32[]{:S(2)}) collective-permute-start(bf16[2048,1024]{1,0:T(8,128)(2,1)} %collective-permute-done.5), channel_id=1, source_target_pairs={{2,4},{3,5},{4,6},{5,7},{10,12},{11,13},{12,14},{13,15},{18,20},{1... | collective-permute-start | bytes 12582920 | tf_op jit(solution)/shard_map/ppermute | solution.py:247
  172.9 2.0 copy-start
  190.3 51.6 %copy-start.3 = (f32[1024,1024]{1,0:T(8,128)}, f32[1024,1024]{1,0:T(8,128)S(1)}, u32[]{:S(2)}) copy-start(f32[1024,1024]{1,0:T(8,128)S(1)} %shard_map.40.refs_6_) | copy-start | bytes 12582916
  241.9 7.7 %copy-start.15 = (bf16[2048,1024]{1,0:T(8,128)(2,1)}, bf16[2048,1024]{1,0:T(8,128)(2,1)S(1)}, u32[]{:S(2)}) copy-start(bf16[2048,1024]{1,0:T(8,128)(2,1)S(1)} %broadcast_select_fusion.refs_4_) | copy-start | bytes 12582916
  241.9 10.9 %collective-permute-start.11 = (bf16[2048,1024]{1,0:T(8,128)(2,1)S(1)}, bf16[2048,1024]{1,0:T(8,128)(2,1)S(1)}, u32[]{:S(2)}, u32[]{:S(2)}) collective-permute-start(bf16[2048,1024]{1,0:T(8,128)(2,1)S(1)} %broadcast_select_fusion.refs_4_), channel_id=1, source_target_pairs={{0,8},{1,9},{2,10},{3,11},{4,12},{5,13},{6,14},{7,15},{8,0},{9,1},... | collective-permute-start | bytes 12582920 | tf_op jit(solution)/shard_map/ppermute | solution.py:247
  249.6 43.8 %collective-permute-start.13 = (bf16[2048,512]{1,0:T(8,128)(2,1)}, bf16[2048,512]{1,0:T(8,128)(2,1)}, u32[]{:S(2)}, u32[]{:S(2)}) collective-permute-start(bf16[2048,512]{1,0:T(8,128)(2,1)} %slice.59), channel_id=1, source_target_pairs={{4,6},{5,7},{12,14},{13,15},{20,22},{21,23},{28,30},{29,31}} | collective-permute-start | bytes 6291464 | tf_op jit(solution)/shard_map/ppermute | solution.py:247
  251.5 49.4 %collective-permute-start.10 = (bf16[2048,512]{1,0:T(8,128)(2,1)}, bf16[2048,512]{1,0:T(8,128)(2,1)}, u32[]{:S(2)}, u32[]{:S(2)}) collective-permute-start(bf16[2048,512]{1,0:T(8,128)(2,1)} %slice.56), channel_id=1, source_target_pairs={{2,0},{3,1},{10,8},{11,9},{18,16},{19,17},{26,24},{27,25}} | collective-permute-start | bytes 6291464 | tf_op jit(solution)/shard_map/ppermute | solution.py:247
  252.8 2.0 copy-start.16
  266.6 25.1 %collective-permute-start.12 = (bf16[1024,512]{1,0:T(8,128)(2,1)}, bf16[1024,512]{1,0:T(8,128)(2,1)}, u32[]{:S(2)}, u32[]{:S(2)}) collective-permute-start(bf16[1024,512]{1,0:T(8,128)(2,1)} %get-tuple-element.105), channel_id=1, source_target_pairs={{0,16},{1,17},{2,18},{3,19},{4,20},{5,21},{6,22},{7,23},{8,24},{9,... | collective-permute-start | bytes 3145736 | tf_op jit(solution)/shard_map/ppermute | solution.py:247
  304.1 4.8 %collective-permute-start.15 = (bf16[2048,512]{1,0:T(8,128)(2,1)S(1)}, bf16[2048,512]{1,0:T(8,128)(2,1)S(1)}, u32[]{:S(2)}, u32[]{:S(2)}) collective-permute-start(bf16[2048,512]{1,0:T(8,128)(2,1)S(1)} %select_select_fusion.refs_4_), channel_id=1, source_target_pairs={{0,8},{1,9},{2,10},{3,11},{4,12},{5,13},{6,14},{7,15},{8,0},{9,1},... | collective-permute-start | bytes 6291464 | tf_op jit(solution)/shard_map/ppermute | solution.py:247
  304.2 27.4 %collective-permute-start.14 = (bf16[2048,256]{1,0:T(8,128)(2,1)S(1)}, bf16[2048,256]{1,0:T(8,128)(2,1)S(1)}, u32[]{:S(2)}, u32[]{:S(2)}) collective-permute-start(bf16[2048,256]{1,0:T(8,128)(2,1)S(1)} %get-tuple-element.110), channel_id=1, source_target_pairs={{2,0},{3,1},{10,8},{11,9},{18,16},{19,17},{26,24},{27,25}} | collective-permute-start | bytes 3145736 | tf_op jit(solution)/shard_map/ppermute | solution.py:247
  305.5 26.2 %collective-permute-start.16 = (bf16[1024,512]{1,0:T(8,128)(2,1)S(1)}, bf16[1024,512]{1,0:T(8,128)(2,1)S(1)}, u32[]{:S(2)}, u32[]{:S(2)}) collective-permute-start(bf16[1024,512]{1,0:T(8,128)(2,1)S(1)} %get-tuple-element.120), channel_id=1, source_target_pairs={{0,16},{1,17},{2,18},{3,19},{4,20},{5,21},{6,22},{7,23},{8,24},{9,... | collective-permute-start | bytes 3145736 | tf_op jit(solution)/shard_map/ppermute | solution.py:247
  307.9 23.8 %collective-permute-start.17 = (bf16[2048,256]{1,0:T(8,128)(2,1)S(1)}, bf16[2048,256]{1,0:T(8,128)(2,1)S(1)}, u32[]{:S(2)}, u32[]{:S(2)}) collective-permute-start(bf16[2048,256]{1,0:T(8,128)(2,1)S(1)} %get-tuple-element.124), channel_id=1, source_target_pairs={{4,6},{5,7},{12,14},{13,15},{20,22},{21,23},{28,30},{29,31}} | collective-permute-start | bytes 3145736 | tf_op jit(solution)/shard_map/ppermute | solution.py:247
  319.3 60.7 %copy-start.5 = (f32[1024,512]{1,0:T(8,128)}, f32[1024,512]{1,0:T(8,128)S(1)}, u32[]{:S(2)}) copy-start(f32[1024,512]{1,0:T(8,128)S(1)} %get-tuple-element.159.keep) | copy-start | bytes 6291460
  333.1 1.7 copy-start.19
  333.4 31.8 %collective-permute-start.19 = (bf16[1024,1024]{1,0:T(8,128)(2,1)S(1)}, bf16[1024,1024]{1,0:T(8,128)(2,1)S(1)}, u32[]{:S(2)}, u32[]{:S(2)}) collective-permute-start(bf16[1024,1024]{1,0:T(8,128)(2,1)S(1)} %fusion), channel_id=1, source_target_pairs={{2,11},{3,10},{6,15},{7,14},{8,1},{9,0},{12,5},{13,4},{18,27},{19,... | collective-permute-start | bytes 6291464 | tf_op jit(solution)/shard_map/ppermute | solution.py:247
  336.6 9.2 %collective-permute-start.21 = (bf16[2048,256]{1,0:T(8,128)(2,1)S(1)}, bf16[2048,256]{1,0:T(8,128)(2,1)S(1)}, u32[]{:S(2)}, u32[]{:S(2)}) collective-permute-start(bf16[2048,256]{1,0:T(8,128)(2,1)S(1)} %select_select_fusion.2.refs_4_), channel_id=1, source_target_pairs={{0,8},{1,9},{2,10},{3,11},{4,12},{5,13},{6,14},{7,15},{8,0},{9,1},... | collective-permute-start | bytes 3145736 | tf_op jit(solution)/shard_map/ppermute | solution.py:247
  338.0 27.2 %collective-permute-start.18 = (bf16[2048,256]{1,0:T(8,128)(2,1)}, bf16[2048,256]{1,0:T(8,128)(2,1)S(1)}, u32[]{:S(2)}, u32[]{:S(2)}) collective-permute-start(bf16[2048,256]{1,0:T(8,128)(2,1)} %get-tuple-element.128), channel_id=1, source_target_pairs={{2,0},{3,1},{10,8},{11,9},{18,16},{19,17},{26,24},{27,25}} | collective-permute-start | bytes 3145736 | tf_op jit(solution)/shard_map/ppermute | solution.py:247
  339.3 25.9 %collective-permute-start.20 = (bf16[1024,512]{1,0:T(8,128)(2,1)S(1)}, bf16[1024,512]{1,0:T(8,128)(2,1)S(1)}, u32[]{:S(2)}, u32[]{:S(2)}) collective-permute-start(bf16[1024,512]{1,0:T(8,128)(2,1)S(1)} %get-tuple-element.134), channel_id=1, source_target_pairs={{0,16},{1,17},{2,18},{3,19},{4,20},{5,21},{6,22},{7,23},{8,24},{9,... | collective-permute-start | bytes 3145736 | tf_op jit(solution)/shard_map/ppermute | solution.py:247
  341.6 23.6 %collective-permute-start.22 = (bf16[2048,256]{1,0:T(8,128)(2,1)}, bf16[2048,256]{1,0:T(8,128)(2,1)}, u32[]{:S(2)}, u32[]{:S(2)}) collective-permute-start(bf16[2048,256]{1,0:T(8,128)(2,1)} %get-tuple-element.143), channel_id=1, source_target_pairs={{4,6},{5,7},{12,14},{13,15},{20,22},{21,23},{28,30},{29,31}} | collective-permute-start | bytes 3145736 | tf_op jit(solution)/shard_map/ppermute | solution.py:247
  365.2 14.8 %copy-start.9 = (bf16[1024,512]{1,0:T(8,128)(2,1)}, bf16[1024,512]{1,0:T(8,128)(2,1)S(1)}, u32[]{:S(2)}) copy-start(bf16[1024,512]{1,0:T(8,128)(2,1)S(1)} %collective-permute-done.20.came) | copy-start | bytes 3145732
  367.3 2.7 collective-permute-start.23
  367.4 17.9 %collective-permute-start.26 = (bf16[1024,256]{1,0:T(8,128)(2,1)S(1)}, bf16[1024,256]{1,0:T(8,128)(2,1)S(1)}, u32[]{:S(2)}, u32[]{:S(2)}) collective-permute-start(bf16[1024,256]{1,0:T(8,128)(2,1)S(1)} %get-tuple-element.158), channel_id=1, source_target_pairs={{0,16},{1,17},{2,18},{3,19},{4,20},{5,21},{6,22},{7,23},{8,24},{9,... | collective-permute-start | bytes 1572872 | tf_op jit(solution)/shard_map/ppermute | solution.py:247
  377.7 16.8 %copy-start.7 = (f32[1024,256]{1,0:T(8,128)}, f32[1024,256]{1,0:T(8,128)S(1)}, u32[]{:S(2)}) copy-start(f32[1024,256]{1,0:T(8,128)S(1)} %get-tuple-element.154.keep) | copy-start | bytes 3145732
  377.7 15.8 %collective-permute-start.24 = (bf16[1024,256]{1,0:T(8,128)(2,1)S(1)}, bf16[1024,256]{1,0:T(8,128)(2,1)S(1)}, u32[]{:S(2)}, u32[]{:S(2)}) collective-permute-start(bf16[1024,256]{1,0:T(8,128)(2,1)S(1)} %get-tuple-element.155), channel_id=1, source_target_pairs={{0,16},{1,17},{2,18},{3,19},{4,20},{5,21},{6,22},{7,23},{8,24},{9,... | collective-permute-start | bytes 1572872 | tf_op jit(solution)/shard_map/ppermute | solution.py:247
  381.4 17.6 %collective-permute-start.28 = (bf16[1024,512]{1,0:T(8,128)(2,1)}, bf16[1024,512]{1,0:T(8,128)(2,1)}, u32[]{:S(2)}, u32[]{:S(2)}) collective-permute-start(bf16[1024,512]{1,0:T(8,128)(2,1)} %add_convert_fusion), channel_id=1, source_target_pairs={{0,9},{1,8},{4,13},{5,12},{10,3},{11,2},{14,7},{15,6},{16,25},{17,... | collective-permute-start | bytes 3145736 | tf_op jit(solution)/shard_map/ppermute | solution.py:247
  387.1 22.5 %collective-permute-start.27 = (bf16[1024,256]{1,0:T(8,128)(2,1)}, bf16[1024,256]{1,0:T(8,128)(2,1)}, u32[]{:S(2)}, u32[]{:S(2)}) collective-permute-start(bf16[1024,256]{1,0:T(8,128)(2,1)} %add_convert_fusion.1), channel_id=1, source_target_pairs={{0,9},{1,8},{4,13},{5,12},{10,3},{11,2},{14,7},{15,6},{16,25},{17,... | collective-permute-start | bytes 1572872 | tf_op jit(solution)/shard_map/ppermute | solution.py:247
  395.2 17.6 %collective-permute-start.25 = (bf16[1024,256]{1,0:T(8,128)(2,1)}, bf16[1024,256]{1,0:T(8,128)(2,1)}, u32[]{:S(2)}, u32[]{:S(2)}) collective-permute-start(bf16[1024,256]{1,0:T(8,128)(2,1)} %add_convert_fusion.2), channel_id=1, source_target_pairs={{0,9},{1,8},{4,13},{5,12},{10,3},{11,2},{14,7},{15,6},{16,25},{17,... | collective-permute-start | bytes 1572872 | tf_op jit(solution)/shard_map/ppermute | solution.py:247
  399.0 2.2 copy-start.1
  401.2 1.6 copy-start.6
  404.0 5.6 %copy-start.2 = (f32[1024,1024]{1,0:T(8,128)S(1)}, f32[1024,1024]{1,0:T(8,128)}, u32[]{:S(2)}) copy-start(f32[1024,1024]{1,0:T(8,128)} %pad_maximum_fusion.1.one) | copy-start | bytes 12582916
  404.0 5.6 %copy-start.12 = (bf16[1024,256]{1,0:T(8,128)(2,1)S(1)}, bf16[1024,256]{1,0:T(8,128)(2,1)}, u32[]{:S(2)}) copy-start(bf16[1024,256]{1,0:T(8,128)(2,1)} %copy-done.11) | copy-start | bytes 1572868
  409.6 3.3 copy-start.8
  409.6 3.3 copy-start.14
  (4 other events, 3.8 us)

commit v5 on v4

--- a/solution.py
+++ b/solution.py
@@ -74,7 +74,7 @@
             pl.BlockSpec((width, count), lambda c: (0, place * channels + c)),
         ),
         input_output_aliases={2 + i: i for i in range(len(held))},
-        compiler_params=pltpu.CompilerParams(vmem_limit_bytes=40 << 20),
+        compiler_params=pltpu.CompilerParams(vmem_limit_bytes=24 << 20),
         cost_estimate=pl.CostEstimate(
             flops=2 * count * lags * width * channels,
             bytes_accessed=2 * channels * width * (lags + 2 * count),
@@ -110,7 +110,7 @@
             in_specs=[spec(width)] * 2,
             out_specs=[spec(part) for part in (width, *parts, *parts)],
         ),
-        compiler_params=pltpu.CompilerParams(vmem_limit_bytes=40 << 20),
+        compiler_params=pltpu.CompilerParams(vmem_limit_bytes=24 << 20),
         cost_estimate=pl.CostEstimate(flops=rows, bytes_accessed=10 * rows * width, transcendentals=0),
     )(from_above, up, down)
     return found[0], found[1 : 1 + len(parts)], found[1 + len(parts) :]
@@ -167,7 +167,7 @@
             out_specs=here if first is None else (here, here),
             scratch_shapes=[pltpu.VMEM((2, rows, depth), near[0].dtype), pltpu.SemaphoreType.DMA((2,))],
         ),
-        compiler_params=pltpu.CompilerParams(vmem_limit_bytes=40 << 20),
+        compiler_params=pltpu.CompilerParams(vmem_limit_bytes=24 << 20),
         cost_estimate=pl.CostEstimate(flops=depth * part, bytes_accessed=depth * part, transcendentals=0),
     )(flags, *near, *far, *right, *([] if first is None else [first]))
 
@@ -214,7 +214,7 @@
             out_specs=pl.BlockSpec((rows, tile), lambda n, i, w: (0, (w[0] + i) % 2 * count + first + n)),
         ),
         input_output_aliases={6: 0} if held else {},
-        compiler_params=pltpu.CompilerParams(vmem_limit_bytes=40 << 20),
+        compiler_params=pltpu.CompilerParams(vmem_limit_bytes=24 << 20),
         cost_estimate=pl.CostEstimate(flops=rows * part, bytes_accessed=22 * rows * part, transcendentals=0),
     )(flags, one, keep, came, far_one, far_two, *held)
 

time: 418 us -> 417 us (level)
    unnamed x46 -> x48, local copies, waits for them, and re-layouts: 17.4 us -> 18.2 us
  transfers between devices with their start and end apart: 29 -> 29, of which waited for: 13 -> 12; matrix products, arithmetic and copies ran while one was open for 7% -> 7% of each run, Pallas kernels for 22% -> 21%
where the time goes in v5:
time: 417 us; the launch traced here: 415 us
  waiting for transfers between devices  198 us (47%)
  Pallas kernels  94.3 us (23%)
  starting transfers between devices  60.3 us (14%)
  local copies, waits for them, and re-layouts  37.1 us (9%)
  other arithmetic  25 us (6%)
    ppermute x28, waiting for transfers between devices, send(): return lax.ppermute(value, AXES, pairs(arcs, cols, target))  198 us
    pallas_call x7, Pallas kernels, products(): pl.pallas_call(product_kernel, out_shape=whole if first is None else (who...  75.4 us
    ppermute x28, starting transfers between devices, send(): return lax.ppermute(value, AXES, pairs(arcs, cols, target))  56.6 us
    unnamed x48, local copies, waits for them, and re-layouts  18.2 us
    pallas_call x3, Pallas kernels, place(): pl.pallas_call(place_kernel, out_shape=jax.ShapeDtypeStruct((rows, 2 * wi...  12 us
  transfers between devices with their start and end apart: 29, of which 12 were waited for; matrix products, arithmetic and copies ran while one was open for 7% of the time, Pallas kernels for 21%

profile of v5, /device:TPU:0, one launch (start us, length us, event | category | flops | bytes accessed | tf_op | source)
XLA Modules:
  0.0 415.4 jit_solution(8382519734208509158)
XLA Ops:
  1.6 2.0 copy.13
  3.6 3.7 collective-permute-start
  7.3 3.4 copy.14
  16.7 3.4 shard_map.37
  20.1 2.0 pad_maximum_fusion.taken
  22.2 3.5 shard_map.38
  25.6 11.7 %collective-permute-start.4 = (bf16[1024,2048]{1,0:T(8,128)(2,1)}, bf16[1024,2048]{1,0:T(8,128)(2,1)}, u32[]{:S(2)}, u32[]{:S(2)}) collective-permute-start(bf16[1024,2048]{1,0:T(8,128)(2,1)} %get-tuple-element.145.refs_0_), channel_id=1, source_target_pairs={{0,8},{1,9},{2,10},{3,11},{4,12},{5,13},{6,14},{7,15},{8,0},{9,1},... | collective-permute-start | bytes 12582920 | tf_op jit(solution)/shard_map/ppermute | solution.py:247
  38.8 5.4 %collective-permute-start.5 = (bf16[2048,1024]{1,0:T(8,128)(2,1)}, bf16[2048,1024]{1,0:T(8,128)(2,1)}, u32[]{:S(2)}, u32[]{:S(2)}) collective-permute-start(bf16[2048,1024]{1,0:T(8,128)(2,1)} %get-tuple-element.90.refs_4_), channel_id=1, source_target_pairs={{0,2},{1,3},{2,4},{3,5},{4,6},{5,7},{8,10},{9,11},{10,12},{11,13},... | collective-permute-start | bytes 12582920 | tf_op jit(solution)/shard_map/ppermute | solution.py:247
  45.6 84.5 %collective-permute-done.2.refs_2_ = bf16[1024,2048]{1,0:T(8,128)(2,1)} collective-permute-done((bf16[1024,2048]{1,0:T(8,128)(2,1)}, bf16[1024,2048]{1,0:T(8,128)(2,1)}, u32[]{:S(2)}, u32[]{:S(2)}) %collective-permute-start.2) | collective-permute-done | bytes 4194336 | tf_op jit(solution)/shard_map/ppermute | solution.py:247
  130.1 2.2 collective-permute-done.5
  132.3 7.1 %collective-permute-done.1 = bf16[2048,1024]{1,0:T(8,128)(2,1)} collective-permute-done((bf16[2048,1024]{1,0:T(8,128)(2,1)}, bf16[2048,1024]{1,0:T(8,128)(2,1)}, u32[]{:S(2)}, u32[]{:S(2)}) %collective-permute-start.1) | collective-permute-done | bytes 4194336 | tf_op jit(solution)/shard_map/ppermute | solution.py:247
  139.4 4.6 %broadcast_select_fusion.1.refs_4_ = bf16[2048,1024]{1,0:T(8,128)(2,1)} fusion(bf16[2048,1024]{1,0:T(8,128)(2,1)} %collective-permute-done.1, bf16[2048,1024]{1,0:T(8,128)(2,1)} %collective-permute-done.5, pred[]{:T(512)S(6)} %lt.29), kind=kLoop, calls=%fused_computation.3 | loop fusion | flops 2097152 | bytes 12582913 | tf_op jit(solution)/shard_map/jit(_where)/select_n | solution.py:292
  145.8 2.7 collective-permute-start.9
  148.7 2.8 collective-permute-done.8.refs_5_
  151.5 6.0 %collective-permute-done.7.refs_3_ = bf16[1024,2048]{1,0:T(8,128)(2,1)} collective-permute-done((bf16[1024,2048]{1,0:T(8,128)(2,1)}, bf16[1024,2048]{1,0:T(8,128)(2,1)}, u32[]{:S(2)}, u32[]{:S(2)}) %collective-permute-start.7) | collective-permute-done | bytes 4194336 | tf_op jit(solution)/shard_map/ppermute | solution.py:247
  157.5 15.3 %shard_map.39.refs_6_ = f32[1024,1024]{1,0:T(8,128)S(1)} custom-call(s32[2]{0:T(128)S(1)} %pad_add_fusion.1.flags, bf16[1024,2048]{1,0:T(8,128)(2,1)} %get-tuple-element.145.refs_0_, bf16[1024,2048]{1,0:T(8,128)(2,1)} %collective-permute-done.4.refs_1_, bf16[1024,2048]{1,0:T(8,128)(2,1)} %collective-permute-done.2.refs_2_, ...), custom_call_target="tpu_custom_call" | custom-call | flops 2097152 | bytes 2097152 | tf_op jit(solution)/shard_map/pallas_call | solution.py:158
  174.8 15.3 %shard_map.40.refs_6_ = f32[1024,1024]{1,0:T(8,128)S(1)} custom-call(s32[2]{0:T(128)S(1)} %pad_add_fusion.2.flags, bf16[1024,2048]{1,0:T(8,128)(2,1)} %get-tuple-element.145.refs_0_, bf16[1024,2048]{1,0:T(8,128)(2,1)} %collective-permute-done.4.refs_1_, bf16[1024,2048]{1,0:T(8,128)(2,1)} %collective-permute-done.2.refs_2_, ...), custom_call_target="tpu_custom_call" | custom-call | flops 2097152 | bytes 2097152 | tf_op jit(solution)/shard_map/pallas_call | solution.py:158
  190.2 2.1 copy-done.6
  192.3 46.9 %collective-permute-done.6 = bf16[2048,1024]{1,0:T(8,128)(2,1)} collective-permute-done((bf16[2048,1024]{1,0:T(8,128)(2,1)}, bf16[2048,1024]{1,0:T(8,128)(2,1)}, u32[]{:S(2)}, u32[]{:S(2)}) %collective-permute-start.6) | collective-permute-done | bytes 4194336 | tf_op jit(solution)/shard_map/ppermute | solution.py:247
  239.2 2.6 broadcast_select_fusion.refs_4_
  241.9 4.5 %slice.56 = bf16[2048,512]{1,0:T(8,128)(2,1)} slice(bf16[2048,1024]{1,0:T(8,128)(2,1)} %collective-permute-done.6), slice={[0:2048], [0:512]} | slice | bytes 4194304 | tf_op jit(solution)/shard_map/slice | solution.py:312
  246.4 3.1 slice.59
  252.8 11.9 %shard_map.42 = (f32[1024,512]{1,0:T(8,128)S(1)}, bf16[1024,512]{1,0:T(8,128)(2,1)}) custom-call(s32[2]{0:T(128)S(1)} %pad_add_fusion.2.flags, bf16[1024,2048]{1,0:T(8,128)(2,1)} %get-tuple-element.145.refs_0_, bf16[1024,2048]{1,0:T(8,128)(2,1)} %collective-permute-done.4.refs_1_, bf16[1024,2048]{1,0:T(8,128)(2,1)} %collective-permute-done.2.refs_2_, ...), custom_call_target="tpu_custom_call" | custom-call | flops 1048576 | bytes 1048576 | tf_op jit(solution)/shard_map/pallas_call | solution.py:158
  264.7 2.4 collective-permute-start.12
  267.1 4.6 %fusion.1 = (bf16[2048,256]{1,0:T(8,128)(2,1)}, bf16[2048,256]{1,0:T(8,128)(2,1)}, bf16[2048,256]{1,0:T(8,128)(2,1)}, bf16[2048,256]{1,0:T(8,128)(2,1)}) fusion(bf16[2048,1024]{1,0:T(8,128)(2,1)} %collective-permute-done.9, bf16[2048,1024]{1,0:T(8,128)(2,1)} %collective-permute-done.6), kind=kLoop, calls=%fused_computation.20 | loop fusion | bytes 8388608 | tf_op jit(solution)/shard_map/slice | solution.py:311
  273.4 10.5 %shard_map.41 = (f32[1024,512]{1,0:T(8,128)S(1)}, bf16[1024,512]{1,0:T(8,128)(2,1)S(1)}) custom-call(s32[2]{0:T(128)S(1)} %pad_add_fusion.2.flags, bf16[1024,2048]{1,0:T(8,128)(2,1)} %get-tuple-element.145.refs_0_, bf16[1024,2048]{1,0:T(8,128)(2,1)} %collective-permute-done.4.refs_1_, bf16[1024,2048]{1,0:T(8,128)(2,1)} %collective-permute-done.2.refs_2_, ...), custom_call_target="tpu_custom_call" | custom-call | flops 1048576 | bytes 1048576 | tf_op jit(solution)/shard_map/pallas_call | solution.py:158
  283.9 5.9 %collective-permute-done.12 = bf16[1024,512]{1,0:T(8,128)(2,1)} collective-permute-done((bf16[1024,512]{1,0:T(8,128)(2,1)}, bf16[1024,512]{1,0:T(8,128)(2,1)}, u32[]{:S(2)}, u32[]{:S(2)}) %collective-permute-start.12) | collective-permute-done | bytes 1048608 | tf_op jit(solution)/shard_map/ppermute | solution.py:247
  291.4 9.4 %collective-permute-done.10 = bf16[2048,512]{1,0:T(8,128)(2,1)} collective-permute-done((bf16[2048,512]{1,0:T(8,128)(2,1)}, bf16[2048,512]{1,0:T(8,128)(2,1)}, u32[]{:S(2)}, u32[]{:S(2)}) %collective-permute-start.10) | collective-permute-done | bytes 2097184 | tf_op jit(solution)/shard_map/ppermute | solution.py:247
  300.8 3.4 select_select_fusion.refs_4_
  305.5 2.4 collective-permute-start.16
  308.9 9.4 %shard_map.43 = (f32[1024,512]{1,0:T(8,128)S(1)}, bf16[1024,512]{1,0:T(8,128)(2,1)S(1)}) custom-call(s32[2]{0:T(128)S(1)} %pad_add_fusion.1.flags, bf16[1024,2048]{1,0:T(8,128)(2,1)} %get-tuple-element.145.refs_0_, bf16[1024,2048]{1,0:T(8,128)(2,1)} %collective-permute-done.4.refs_1_, bf16[1024,2048]{1,0:T(8,128)(2,1)} %collective-permute-done.2.refs_2_, ...), custom_call_target="tpu_custom_call" | custom-call | flops 1048576 | bytes 1048576 | tf_op jit(solution)/shard_map/pallas_call | solution.py:158
  318.4 13.5 %collective-permute-done.14 = bf16[2048,256]{1,0:T(8,128)(2,1)S(1)} collective-permute-done((bf16[2048,256]{1,0:T(8,128)(2,1)}, bf16[2048,256]{1,0:T(8,128)(2,1)S(1)}, u32[]{:S(2)}, u32[]{:S(2)}) %collective-permute-start.14) | collective-permute-done | bytes 1048608 | tf_op jit(solution)/shard_map/ppermute | solution.py:247
  338.3 2.4 collective-permute-start.20
  341.5 2.3 pad_maximum_fusion.1.one
  343.8 6.5 %shard_map.44 = (f32[1024,256]{1,0:T(8,128)S(1)}, bf16[1024,256]{1,0:T(8,128)(2,1)S(1)}) custom-call(s32[2]{0:T(128)S(1)} %pad_add_fusion.1.flags, bf16[1024,2048]{1,0:T(8,128)(2,1)} %get-tuple-element.145.refs_0_, bf16[1024,2048]{1,0:T(8,128)(2,1)} %collective-permute-done.4.refs_1_, bf16[1024,2048]{1,0:T(8,128)(2,1)} %collective-permute-done.2.refs_2_, ...), custom_call_target="tpu_custom_call" | custom-call | flops 524288 | bytes 524288 | tf_op jit(solution)/shard_map/pallas_call | solution.py:158
  350.3 13.9 %collective-permute-done.18 = bf16[2048,256]{1,0:T(8,128)(2,1)S(1)} collective-permute-done((bf16[2048,256]{1,0:T(8,128)(2,1)}, bf16[2048,256]{1,0:T(8,128)(2,1)S(1)}, u32[]{:S(2)}, u32[]{:S(2)}) %collective-permute-start.18) | collective-permute-done | bytes 1048608 | tf_op jit(solution)/shard_map/ppermute | solution.py:247
  364.2 2.3 select_select_fusion.1.refs_4_
  366.6 2.4 collective-permute-start.26
  369.3 6.5 %shard_map.45 = (f32[1024,256]{1,0:T(8,128)S(1)}, bf16[1024,256]{1,0:T(8,128)(2,1)S(1)}) custom-call(s32[2]{0:T(128)S(1)} %pad_add_fusion.1.flags, bf16[1024,2048]{1,0:T(8,128)(2,1)} %get-tuple-element.145.refs_0_, bf16[1024,2048]{1,0:T(8,128)(2,1)} %collective-permute-done.4.refs_1_, bf16[1024,2048]{1,0:T(8,128)(2,1)} %collective-permute-done.2.refs_2_, ...), custom_call_target="tpu_custom_call" | custom-call | flops 524288 | bytes 524288 | tf_op jit(solution)/shard_map/pallas_call | solution.py:158
  375.7 2.4 collective-permute-start.24
  379.5 3.8 collective-permute-start.28
  385.1 2.1 collective-permute-start.27
  387.2 5.6 %collective-permute-done.24.came = bf16[1024,256]{1,0:T(8,128)(2,1)S(1)} collective-permute-done((bf16[1024,256]{1,0:T(8,128)(2,1)S(1)}, bf16[1024,256]{1,0:T(8,128)(2,1)S(1)}, u32[]{:S(2)}, u32[]{:S(2)}) %collective-permute-start.24) | collective-permute-done | bytes 524320 | tf_op jit(solution)/shard_map/ppermute | solution.py:247
  394.6 3.7 collective-permute-start.25
  398.3 2.2 copy-done.2
  403.4 5.6 %shard_map.46.refs_0_ = f32[1024,2048]{1,0:T(8,128)} custom-call(s32[2]{0:T(128)S(1)} %pad_add_fusion.flags, f32[1024,1024]{1,0:T(8,128)S(1)} %copy-done.2, f32[1024,512]{1,0:T(8,128)S(1)} %copy-done.11, bf16[1024,512]{1,0:T(8,128)(2,1)S(1)} %copy-done.15, bf16[1024,1024]{1,0:T(8,128)(2,1)S(1)} %collective-permute-done.19.far_one, ...), custom_call_target="tpu_custom_call" | custom-call | flops 524288 | bytes 11534336 | tf_op jit(solution)/shard_map/pallas_call | solution.py:200
  409.0 3.2 shard_map.47.refs_0_
  412.2 3.2 shard_map.48
  (104 shorter events, 38.3 us)
Async XLA Ops:
  0.0 7.3 %copy-start.20 = (bf16[512,4,1024]{2,1,0:T(4,128)(2,1)S(1)}, bf16[512,4,1024]{2,1,0:T(4,128)(2,1)}, u32[]{:S(2)}) copy-start(bf16[512,4,1024]{2,1,0:T(4,128)(2,1)} %param.3) | copy-start | bytes 12582916
  3.6 16.5 %collective-permute-start = (bf16[256,4,1024]{2,0,1:T(8,128)(2,1)}, bf16[256,4,1024]{2,0,1:T(8,128)(2,1)}, u32[]{:S(2)}, u32[]{:S(2)}) collective-permute-start(bf16[256,4,1024]{2,0,1:T(8,128)(2,1)} %copy.13), channel_id=1, source_target_pairs={{0,8},{8,16},{16,24},{1,9},{9,17},{17,25},{2,10},{10,18},{18,26},{... | collective-permute-start | bytes 6291464 | tf_op jit(solution)/shard_map/ppermute | solution.py:276
  7.3 3.5 copy-start.21
  11.8 4.0 copy-start.22
  13.9 2.8 copy-start.7
  25.6 19.9 %collective-permute-start.4 = (bf16[1024,2048]{1,0:T(8,128)(2,1)}, bf16[1024,2048]{1,0:T(8,128)(2,1)}, u32[]{:S(2)}, u32[]{:S(2)}) collective-permute-start(bf16[1024,2048]{1,0:T(8,128)(2,1)} %get-tuple-element.145.refs_0_), channel_id=1, source_target_pairs={{0,8},{1,9},{2,10},{3,11},{4,12},{5,13},{6,14},{7,15},{8,0},{9,1},... | collective-permute-start | bytes 12582920 | tf_op jit(solution)/shard_map/ppermute | solution.py:247
  37.3 92.8 %collective-permute-start.2 = (bf16[1024,2048]{1,0:T(8,128)(2,1)}, bf16[1024,2048]{1,0:T(8,128)(2,1)}, u32[]{:S(2)}, u32[]{:S(2)}) collective-permute-start(bf16[1024,2048]{1,0:T(8,128)(2,1)} %get-tuple-element.145.refs_0_), channel_id=1, source_target_pairs={{0,1},{1,0},{2,3},{3,2},{4,5},{5,4},{6,7},{7,6},{8,9},{9,8},{10,11... | collective-permute-start | bytes 12582920 | tf_op jit(solution)/shard_map/ppermute | solution.py:247
  38.8 93.5 %collective-permute-start.5 = (bf16[2048,1024]{1,0:T(8,128)(2,1)}, bf16[2048,1024]{1,0:T(8,128)(2,1)}, u32[]{:S(2)}, u32[]{:S(2)}) collective-permute-start(bf16[2048,1024]{1,0:T(8,128)(2,1)} %get-tuple-element.90.refs_4_), channel_id=1, source_target_pairs={{0,2},{1,3},{2,4},{3,5},{4,6},{5,7},{8,10},{9,11},{10,12},{11,13},... | collective-permute-start | bytes 12582920 | tf_op jit(solution)/shard_map/ppermute | solution.py:247
  44.3 88.1 %collective-permute-start.3 = (bf16[2048,1024]{1,0:T(8,128)(2,1)}, bf16[2048,1024]{1,0:T(8,128)(2,1)}, u32[]{:S(2)}, u32[]{:S(2)}) collective-permute-start(bf16[2048,1024]{1,0:T(8,128)(2,1)} %get-tuple-element.90.refs_4_), channel_id=1, source_target_pairs={{0,8},{1,9},{2,10},{3,11},{4,12},{5,13},{6,14},{7,15},{8,0},{9,1},... | collective-permute-start | bytes 12582920 | tf_op jit(solution)/shard_map/ppermute | solution.py:247
  44.3 95.2 %collective-permute-start.1 = (bf16[2048,1024]{1,0:T(8,128)(2,1)}, bf16[2048,1024]{1,0:T(8,128)(2,1)}, u32[]{:S(2)}, u32[]{:S(2)}) collective-permute-start(bf16[2048,1024]{1,0:T(8,128)(2,1)} %get-tuple-element.90.refs_4_), channel_id=1, source_target_pairs={{2,0},{3,1},{4,2},{5,3},{6,4},{7,5},{10,8},{11,9},{12,10},{13,11},... | collective-permute-start | bytes 12582920 | tf_op jit(solution)/shard_map/ppermute | solution.py:247
  144.0 7.5 %collective-permute-start.8 = (bf16[2048,1024]{1,0:T(8,128)(2,1)}, bf16[2048,1024]{1,0:T(8,128)(2,1)}, u32[]{:S(2)}, u32[]{:S(2)}) collective-permute-start(bf16[2048,1024]{1,0:T(8,128)(2,1)} %broadcast_select_fusion.1.refs_4_), channel_id=1, source_target_pairs={{0,8},{1,9},{2,10},{3,11},{4,12},{5,13},{6,14},{7,15},{8,0},{9,1},... | collective-permute-start | bytes 12582920 | tf_op jit(solution)/shard_map/ppermute | solution.py:247
  144.0 13.5 %collective-permute-start.7 = (bf16[1024,2048]{1,0:T(8,128)(2,1)}, bf16[1024,2048]{1,0:T(8,128)(2,1)}, u32[]{:S(2)}, u32[]{:S(2)}) collective-permute-start(bf16[1024,2048]{1,0:T(8,128)(2,1)} %collective-permute-done.2.refs_2_), channel_id=1, source_target_pairs={{0,8},{1,9},{2,10},{3,11},{4,12},{5,13},{6,14},{7,15},{8,0},{9,1},... | collective-permute-start | bytes 12582920 | tf_op jit(solution)/shard_map/ppermute | solution.py:247
  144.5 94.7 %collective-permute-start.6 = (bf16[2048,1024]{1,0:T(8,128)(2,1)}, bf16[2048,1024]{1,0:T(8,128)(2,1)}, u32[]{:S(2)}, u32[]{:S(2)}) collective-permute-start(bf16[2048,1024]{1,0:T(8,128)(2,1)} %collective-permute-done.1), channel_id=1, source_target_pairs={{2,0},{3,1},{4,2},{5,3},{10,8},{11,9},{12,10},{13,11},{18,16},{19,... | collective-permute-start | bytes 12582920 | tf_op jit(solution)/shard_map/ppermute | solution.py:247
  145.8 93.4 %collective-permute-start.9 = (bf16[2048,1024]{1,0:T(8,128)(2,1)}, bf16[2048,1024]{1,0:T(8,128)(2,1)}, u32[]{:S(2)}, u32[]{:S(2)}) collective-permute-start(bf16[2048,1024]{1,0:T(8,128)(2,1)} %collective-permute-done.5), channel_id=1, source_target_pairs={{2,4},{3,5},{4,6},{5,7},{10,12},{11,13},{12,14},{13,15},{18,20},{1... | collective-permute-start | bytes 12582920 | tf_op jit(solution)/shard_map/ppermute | solution.py:247
  172.9 2.0 copy-start
  190.2 2.1 copy-start.6
  241.8 10.9 %copy-start.4 = (bf16[2048,1024]{1,0:T(8,128)(2,1)}, bf16[2048,1024]{1,0:T(8,128)(2,1)S(1)}, u32[]{:S(2)}) copy-start(bf16[2048,1024]{1,0:T(8,128)(2,1)S(1)} %broadcast_select_fusion.refs_4_) | copy-start | bytes 12582916
  241.9 10.9 %collective-permute-start.11 = (bf16[2048,1024]{1,0:T(8,128)(2,1)S(1)}, bf16[2048,1024]{1,0:T(8,128)(2,1)S(1)}, u32[]{:S(2)}, u32[]{:S(2)}) collective-permute-start(bf16[2048,1024]{1,0:T(8,128)(2,1)S(1)} %broadcast_select_fusion.refs_4_), channel_id=1, source_target_pairs={{0,8},{1,9},{2,10},{3,11},{4,12},{5,13},{6,14},{7,15},{8,0},{9,1},... | collective-permute-start | bytes 12582920 | tf_op jit(solution)/shard_map/ppermute | solution.py:247
  249.5 41.8 %collective-permute-start.13 = (bf16[2048,512]{1,0:T(8,128)(2,1)}, bf16[2048,512]{1,0:T(8,128)(2,1)}, u32[]{:S(2)}, u32[]{:S(2)}) collective-permute-start(bf16[2048,512]{1,0:T(8,128)(2,1)} %slice.59), channel_id=1, source_target_pairs={{4,6},{5,7},{12,14},{13,15},{20,22},{21,23},{28,30},{29,31}} | collective-permute-start | bytes 6291464 | tf_op jit(solution)/shard_map/ppermute | solution.py:247
  251.5 49.3 %collective-permute-start.10 = (bf16[2048,512]{1,0:T(8,128)(2,1)}, bf16[2048,512]{1,0:T(8,128)(2,1)}, u32[]{:S(2)}, u32[]{:S(2)}) collective-permute-start(bf16[2048,512]{1,0:T(8,128)(2,1)} %slice.56), channel_id=1, source_target_pairs={{2,0},{3,1},{10,8},{11,9},{18,16},{19,17},{26,24},{27,25}} | collective-permute-start | bytes 6291464 | tf_op jit(solution)/shard_map/ppermute | solution.py:247
  252.8 11.9 %copy-start.8 = (bf16[2048,1024]{1,0:T(8,128)(2,1)}, bf16[2048,1024]{1,0:T(8,128)(2,1)S(1)}, u32[]{:S(2)}) copy-start(bf16[2048,1024]{1,0:T(8,128)(2,1)S(1)} %collective-permute-done.11.refs_5_) | copy-start | bytes 12582916
  264.7 25.1 %collective-permute-start.12 = (bf16[1024,512]{1,0:T(8,128)(2,1)}, bf16[1024,512]{1,0:T(8,128)(2,1)}, u32[]{:S(2)}, u32[]{:S(2)}) collective-permute-start(bf16[1024,512]{1,0:T(8,128)(2,1)} %get-tuple-element.105), channel_id=1, source_target_pairs={{0,16},{1,17},{2,18},{3,19},{4,20},{5,21},{6,22},{7,23},{8,24},{9,... | collective-permute-start | bytes 3145736 | tf_op jit(solution)/shard_map/ppermute | solution.py:247
  267.1 4.6 %copy-start.5 = (bf16[2048,1024]{1,0:T(8,128)(2,1)S(1)}, bf16[2048,1024]{1,0:T(8,128)(2,1)}, u32[]{:S(2)}) copy-start(bf16[2048,1024]{1,0:T(8,128)(2,1)} %copy-done.4) | copy-start | bytes 12582916
  267.1 6.3 %copy-start.9 = (bf16[2048,1024]{1,0:T(8,128)(2,1)S(1)}, bf16[2048,1024]{1,0:T(8,128)(2,1)}, u32[]{:S(2)}) copy-start(bf16[2048,1024]{1,0:T(8,128)(2,1)} %copy-done.8) | copy-start | bytes 12582916
  300.8 8.1 %copy-start.1 = (f32[1024,1024]{1,0:T(8,128)S(1)}, f32[1024,1024]{1,0:T(8,128)}, u32[]{:S(2)}) copy-start(f32[1024,1024]{1,0:T(8,128)} %copy-done) | copy-start | bytes 12582916
  304.2 4.8 %collective-permute-start.15 = (bf16[2048,512]{1,0:T(8,128)(2,1)S(1)}, bf16[2048,512]{1,0:T(8,128)(2,1)S(1)}, u32[]{:S(2)}, u32[]{:S(2)}) collective-permute-start(bf16[2048,512]{1,0:T(8,128)(2,1)S(1)} %select_select_fusion.refs_4_), channel_id=1, source_target_pairs={{0,8},{1,9},{2,10},{3,11},{4,12},{5,13},{6,14},{7,15},{8,0},{9,1},... | collective-permute-start | bytes 6291464 | tf_op jit(solution)/shard_map/ppermute | solution.py:247
  304.2 27.7 %collective-permute-start.14 = (bf16[2048,256]{1,0:T(8,128)(2,1)}, bf16[2048,256]{1,0:T(8,128)(2,1)S(1)}, u32[]{:S(2)}, u32[]{:S(2)}) collective-permute-start(bf16[2048,256]{1,0:T(8,128)(2,1)} %get-tuple-element.110), channel_id=1, source_target_pairs={{2,0},{3,1},{10,8},{11,9},{18,16},{19,17},{26,24},{27,25}} | collective-permute-start | bytes 3145736 | tf_op jit(solution)/shard_map/ppermute | solution.py:247
  305.5 26.4 %collective-permute-start.16 = (bf16[1024,512]{1,0:T(8,128)(2,1)S(1)}, bf16[1024,512]{1,0:T(8,128)(2,1)S(1)}, u32[]{:S(2)}, u32[]{:S(2)}) collective-permute-start(bf16[1024,512]{1,0:T(8,128)(2,1)S(1)} %get-tuple-element.120), channel_id=1, source_target_pairs={{0,16},{1,17},{2,18},{3,19},{4,20},{5,21},{6,22},{7,23},{8,24},{9,... | collective-permute-start | bytes 3145736 | tf_op jit(solution)/shard_map/ppermute | solution.py:247
  308.0 23.9 %collective-permute-start.17 = (bf16[2048,256]{1,0:T(8,128)(2,1)}, bf16[2048,256]{1,0:T(8,128)(2,1)S(1)}, u32[]{:S(2)}, u32[]{:S(2)}) collective-permute-start(bf16[2048,256]{1,0:T(8,128)(2,1)} %get-tuple-element.124), channel_id=1, source_target_pairs={{4,6},{5,7},{12,14},{13,15},{20,22},{21,23},{28,30},{29,31}} | collective-permute-start | bytes 3145736 | tf_op jit(solution)/shard_map/ppermute | solution.py:247
  318.4 59.8 %copy-start.10 = (f32[1024,512]{1,0:T(8,128)}, f32[1024,512]{1,0:T(8,128)S(1)}, u32[]{:S(2)}) copy-start(f32[1024,512]{1,0:T(8,128)S(1)} %get-tuple-element.159.keep) | copy-start | bytes 6291460
  332.5 31.7 %collective-permute-start.19 = (bf16[1024,1024]{1,0:T(8,128)(2,1)S(1)}, bf16[1024,1024]{1,0:T(8,128)(2,1)S(1)}, u32[]{:S(2)}, u32[]{:S(2)}) collective-permute-start(bf16[1024,1024]{1,0:T(8,128)(2,1)S(1)} %fusion), channel_id=1, source_target_pairs={{2,11},{3,10},{6,15},{7,14},{8,1},{9,0},{12,5},{13,4},{18,27},{19,... | collective-permute-start | bytes 6291464 | tf_op jit(solution)/shard_map/ppermute | solution.py:247
  335.6 8.2 %collective-permute-start.21 = (bf16[2048,256]{1,0:T(8,128)(2,1)S(1)}, bf16[2048,256]{1,0:T(8,128)(2,1)S(1)}, u32[]{:S(2)}, u32[]{:S(2)}) collective-permute-start(bf16[2048,256]{1,0:T(8,128)(2,1)S(1)} %select_select_fusion.2.refs_4_), channel_id=1, source_target_pairs={{0,8},{1,9},{2,10},{3,11},{4,12},{5,13},{6,14},{7,15},{8,0},{9,1},... | collective-permute-start | bytes 3145736 | tf_op jit(solution)/shard_map/ppermute | solution.py:247
  337.0 27.2 %collective-permute-start.18 = (bf16[2048,256]{1,0:T(8,128)(2,1)}, bf16[2048,256]{1,0:T(8,128)(2,1)S(1)}, u32[]{:S(2)}, u32[]{:S(2)}) collective-permute-start(bf16[2048,256]{1,0:T(8,128)(2,1)} %get-tuple-element.128), channel_id=1, source_target_pairs={{2,0},{3,1},{10,8},{11,9},{18,16},{19,17},{26,24},{27,25}} | collective-permute-start | bytes 3145736 | tf_op jit(solution)/shard_map/ppermute | solution.py:247
  338.3 25.9 %collective-permute-start.20 = (bf16[1024,512]{1,0:T(8,128)(2,1)S(1)}, bf16[1024,512]{1,0:T(8,128)(2,1)S(1)}, u32[]{:S(2)}, u32[]{:S(2)}) collective-permute-start(bf16[1024,512]{1,0:T(8,128)(2,1)S(1)} %get-tuple-element.134), channel_id=1, source_target_pairs={{0,16},{1,17},{2,18},{3,19},{4,20},{5,21},{6,22},{7,23},{8,24},{9,... | collective-permute-start | bytes 3145736 | tf_op jit(solution)/shard_map/ppermute | solution.py:247
  340.8 23.5 %collective-permute-start.22 = (bf16[2048,256]{1,0:T(8,128)(2,1)}, bf16[2048,256]{1,0:T(8,128)(2,1)S(1)}, u32[]{:S(2)}, u32[]{:S(2)}) collective-permute-start(bf16[2048,256]{1,0:T(8,128)(2,1)} %get-tuple-element.143), channel_id=1, source_target_pairs={{4,6},{5,7},{12,14},{13,15},{20,22},{21,23},{28,30},{29,31}} | collective-permute-start | bytes 3145736 | tf_op jit(solution)/shard_map/ppermute | solution.py:247
  364.2 14.0 %copy-start.14 = (bf16[1024,512]{1,0:T(8,128)(2,1)}, bf16[1024,512]{1,0:T(8,128)(2,1)S(1)}, u32[]{:S(2)}) copy-start(bf16[1024,512]{1,0:T(8,128)(2,1)S(1)} %collective-permute-done.20.came) | copy-start | bytes 3145732
  366.5 2.7 collective-permute-start.23
  366.6 16.7 %collective-permute-start.26 = (bf16[1024,256]{1,0:T(8,128)(2,1)S(1)}, bf16[1024,256]{1,0:T(8,128)(2,1)S(1)}, u32[]{:S(2)}, u32[]{:S(2)}) collective-permute-start(bf16[1024,256]{1,0:T(8,128)(2,1)S(1)} %get-tuple-element.158), channel_id=1, source_target_pairs={{0,16},{1,17},{2,18},{3,19},{4,20},{5,21},{6,22},{7,23},{8,24},{9,... | collective-permute-start | bytes 1572872 | tf_op jit(solution)/shard_map/ppermute | solution.py:247
  375.7 18.0 %copy-start.12 = (f32[1024,256]{1,0:T(8,128)}, f32[1024,256]{1,0:T(8,128)S(1)}, u32[]{:S(2)}) copy-start(f32[1024,256]{1,0:T(8,128)S(1)} %get-tuple-element.154.keep) | copy-start | bytes 3145732
  375.7 17.1 %collective-permute-start.24 = (bf16[1024,256]{1,0:T(8,128)(2,1)S(1)}, bf16[1024,256]{1,0:T(8,128)(2,1)S(1)}, u32[]{:S(2)}, u32[]{:S(2)}) collective-permute-start(bf16[1024,256]{1,0:T(8,128)(2,1)S(1)} %get-tuple-element.155), channel_id=1, source_target_pairs={{0,16},{1,17},{2,18},{3,19},{4,20},{5,21},{6,22},{7,23},{8,24},{9,... | collective-permute-start | bytes 1572872 | tf_op jit(solution)/shard_map/ppermute | solution.py:247
  379.5 18.8 %collective-permute-start.28 = (bf16[1024,512]{1,0:T(8,128)(2,1)}, bf16[1024,512]{1,0:T(8,128)(2,1)}, u32[]{:S(2)}, u32[]{:S(2)}) collective-permute-start(bf16[1024,512]{1,0:T(8,128)(2,1)} %add_convert_fusion), channel_id=1, source_target_pairs={{0,9},{1,8},{4,13},{5,12},{10,3},{11,2},{14,7},{15,6},{16,25},{17,... | collective-permute-start | bytes 3145736 | tf_op jit(solution)/shard_map/ppermute | solution.py:247
  385.1 23.8 %collective-permute-start.27 = (bf16[1024,256]{1,0:T(8,128)(2,1)}, bf16[1024,256]{1,0:T(8,128)(2,1)}, u32[]{:S(2)}, u32[]{:S(2)}) collective-permute-start(bf16[1024,256]{1,0:T(8,128)(2,1)} %add_convert_fusion.1), channel_id=1, source_target_pairs={{0,9},{1,8},{4,13},{5,12},{10,3},{11,2},{14,7},{15,6},{16,25},{17,... | collective-permute-start | bytes 1572872 | tf_op jit(solution)/shard_map/ppermute | solution.py:247
  394.6 17.6 %collective-permute-start.25 = (bf16[1024,256]{1,0:T(8,128)(2,1)}, bf16[1024,256]{1,0:T(8,128)(2,1)}, u32[]{:S(2)}, u32[]{:S(2)}) collective-permute-start(bf16[1024,256]{1,0:T(8,128)(2,1)} %add_convert_fusion.2), channel_id=1, source_target_pairs={{0,9},{1,8},{4,13},{5,12},{10,3},{11,2},{14,7},{15,6},{16,25},{17,... | collective-permute-start | bytes 1572872 | tf_op jit(solution)/shard_map/ppermute | solution.py:247
  398.3 2.2 copy-start.2
  403.3 5.6 %copy-start.3 = (f32[1024,1024]{1,0:T(8,128)S(1)}, f32[1024,1024]{1,0:T(8,128)}, u32[]{:S(2)}) copy-start(f32[1024,1024]{1,0:T(8,128)} %pad_maximum_fusion.1.one) | copy-start | bytes 12582916
  403.4 5.6 %copy-start.17 = (bf16[1024,256]{1,0:T(8,128)(2,1)S(1)}, bf16[1024,256]{1,0:T(8,128)(2,1)}, u32[]{:S(2)}) copy-start(bf16[1024,256]{1,0:T(8,128)(2,1)} %copy-done.16) | copy-start | bytes 1572868
  408.9 3.3 copy-start.13
  408.9 3.3 copy-start.19
  (5 other events, 6.0 us)
